TPU v7x, 256 devices: a whole 4x4x8 slice. The times are simulated.
256 devices in a mesh: req: 32 (over y, x, core), head: 8 (over z).
Axes of the slice: x: 4, y: 4, z: 8, core: 2. Of those that a mesh axis runs over, the one named last changes fastest.
Arguments:
- tokens: bfloat16 [4096, 1536], P(('req', 'head')), may hold values from -6 to 6
- pre_gain: float32 [1536], replicated, may hold values from 0.1 to 1.9
- inner_weight: bfloat16 [1536, 2, 3072], P(None, None, 'head')
- shared_weight: bfloat16 [1536, 304], replicated, may hold values from -0.15625 to 0.15625
- conv_inner: float32 [4, 3072], P(None, 'head'), may hold values from -0.5 to 0.5
- conv_inner_bias: float32 [3072], P('head'), may hold values from -0.5 to 0.5
- conv_shared: float32 [4, 256], replicated, may hold values from -0.5 to 0.5
- conv_shared_bias: float32 [256], replicated, may hold values from -0.5 to 0.5
- step_bias: float32 [48], P('head'), may hold values from -4 to 0
- decay_log: float32 [48], P('head'), may hold values from 0 to 2.77
- skip_gain: float32 [48], P('head'), may hold values from 0.5 to 1.5
- gate_gain: float32 [3072], P('head'), may hold values from 0.1 to 1.9
- out_weight: bfloat16 [3072, 1536], P('head'), may hold values from -0.109375 to 0.109375
- states: bfloat16 [1024, 48, 64, 128], P('req', 'head'), may hold values from -1.1953125 to 1.1953125
- edge_inner: bfloat16 [1024, 3, 3072], P('req', None, 'head'), may hold values from -6 to 6
- edge_shared: bfloat16 [1024, 3, 256], P('req'), may hold values from -6 to 6
- counts: int32 [1024], P('req'), may hold values from 1 to 4, as said below
- mig_ids: int32 [32], replicated, may hold values from 0 to 1023, as said below
- mig_dest: int32 [32], replicated, may hold values from 0 to 1023, as said below
- reorder: int32 [1024], replicated, may hold values from 0 to 1023, as said below
Outputs:
- hidden_out: bfloat16 [4096, 1536], P(('req', 'head'))
- states_out: bfloat16 [1024, 48, 64, 128], P('req', 'head')
- edge_inner_out: bfloat16 [1024, 3, 3072], P('req', None, 'head')
- edge_shared_out: bfloat16 [1024, 3, 256], P('req')
Inputs may be any that keep to these rules, and one draw needn't show every extreme that they name: counts: each slot's token rows are r * 4 to r * 4 + 3 of tokens; the first counts[r] of them are real. mig_ids: distinct old slots listed by owner: entry i is one of the slots i * 32 to (i + 1) * 32 - 1, those held by index i of req. mig_dest: a reordering of the slots in mig_ids. reorder: a permutation of all slots. The 32 new slots j with j // 32 = d take at most 1 values reorder[j] of any one block of 32 slots, and exactly 1 of some block.
All inputs are finite; a program needn't handle non-finite values.
Results may differ from a plain program's by a relative error of at most 0.013.
Values may be sent and summed in bfloat16 or wider, within the bound.
A program may use at most 128 MiB of HBM per device.

v0:
```python
import jax
import jax.numpy as jnp
from jax import lax
from jax.sharding import PartitionSpec as P

EPS = 1e-05


def advance(carried, step_now, inputs_now, entry_now, readout_now, decay, skip_gain):
    factor = jnp.exp(step_now * decay)
    carried = (
        carried * factor[:, :, None, None]
        + (step_now[:, :, None] * inputs_now)[:, :, :, None] * entry_now[:, None, None, :]
    )
    produced = jnp.einsum("khpn,kn->khp", carried, readout_now, precision=lax.Precision.HIGHEST)
    return (carried, produced + skip_gain[None, :, None] * inputs_now)


def depthwise(edge, fresh, weight, offset_bias):
    sequence = jnp.concatenate([edge, fresh], axis=1).astype(jnp.float32)
    window = fresh.shape[1]
    summed = sequence[:, 0:window] * weight[0]
    for offset in range(1, weight.shape[0]):
        summed = summed + sequence[:, offset : offset + window] * weight[offset]
    return jax.nn.silu(summed + offset_bias)


def new_edge(edge, fresh, counts):
    sequence = jnp.concatenate([edge, fresh], axis=1)
    keep_rows = edge.shape[1]
    result = edge
    for length in range(1, fresh.shape[1] + 1):
        result = jnp.where(
            (counts == length)[:, None, None], sequence[:, length : length + keep_rows], result
        )
    return result


def rank_rows(partner, position, capacity):
    matching = partner[:, None] == partner[None, :]
    earlier = position[None, :] < position[:, None]
    ranking = jnp.sum(jnp.logical_and(matching, earlier), axis=1)
    return partner * capacity + ranking


def pack_pages(member, send_rows, buffer_rows):
    empty = jnp.zeros((buffer_rows,) + member.shape[1:], member.dtype)
    return empty.at[send_rows].set(member)


def route_rows(anchor, first_slot, slot_count, all_slots, capacity):
    inverse = jnp.zeros(all_slots.shape, jnp.int32).at[anchor].set(all_slots)
    targets = lax.dynamic_slice_in_dim(inverse, first_slot, slot_count)
    send_rows = rank_rows(targets // slot_count, targets % slot_count, capacity)
    sources = lax.dynamic_slice_in_dim(anchor, first_slot, slot_count)
    recv_rows = rank_rows(sources // slot_count, jnp.arange(slot_count, dtype=jnp.int32), capacity)
    return (send_rows, recv_rows)


def local(
    tokens,
    pre_gain,
    inner_weight,
    shared_weight,
    conv_inner,
    conv_inner_bias,
    conv_shared,
    conv_shared_bias,
    step_bias,
    decay_log,
    skip_gain,
    gate_gain,
    out_weight,
    states,
    edge_inner,
    edge_shared,
    counts,
    mig_ids,
    mig_dest,
    reorder,
):
    slot_count = states.shape[0]
    heads_here = states.shape[1]
    head_dim = states.shape[2]
    state_dim = states.shape[3]
    inner_here = heads_here * head_dim
    groups = lax.axis_size("req")
    device = lax.axis_index("req")
    first_slot = device * slot_count
    moving = mig_ids.shape[0] // groups
    stride = (slot_count + groups - 1) // groups
    all_slots = jnp.arange(slot_count * groups, dtype=jnp.int32)
    rows_in = tokens.astype(jnp.float32)
    normed = (
        rows_in * lax.rsqrt(jnp.mean(rows_in * rows_in, axis=-1, keepdims=True) + EPS) * pre_gain
    ).astype(jnp.bfloat16)
    inner_flat = inner_weight.reshape(inner_weight.shape[0], 2 * inner_here)
    piece_rows = lax.all_gather(normed, "head", axis=0, tiled=True)
    inner_rows = jnp.dot(piece_rows, inner_flat, preferred_element_type=jnp.float32).astype(
        jnp.bfloat16
    )
    shared_rows = jnp.dot(piece_rows, shared_weight, preferred_element_type=jnp.float32).astype(
        jnp.bfloat16
    )
    projected = jnp.concatenate([inner_rows, shared_rows], axis=1)
    own_ids = lax.dynamic_slice_in_dim(mig_ids, device * moving, moving)
    local_ids = own_ids - first_slot
    arrived = (
        lax.all_gather(states[local_ids], "req", axis=0, tiled=True),
        lax.all_gather(edge_inner[local_ids], "req", axis=0, tiled=True),
        lax.all_gather(edge_shared[local_ids], "req", axis=0, tiled=True),
    )
    picked = jnp.argmax(mig_dest[None, :] == own_ids[:, None], axis=1)
    sectioned_states = states.at[local_ids].set(arrived[0][picked])
    sectioned_inner = edge_inner.at[local_ids].set(arrived[1][picked])
    sectioned_shared = edge_shared.at[local_ids].set(arrived[2][picked])
    send_rows, recv_rows = route_rows(reorder, first_slot, slot_count, all_slots, stride)
    buffer_rows = groups * stride
    received = (
        lax.all_to_all(
            pack_pages(sectioned_states, send_rows, buffer_rows),
            "req",
            split_axis=0,
            concat_axis=0,
            tiled=True,
        ),
        lax.all_to_all(
            pack_pages(sectioned_inner, send_rows, buffer_rows),
            "req",
            split_axis=0,
            concat_axis=0,
            tiled=True,
        ),
        lax.all_to_all(
            pack_pages(sectioned_shared, send_rows, buffer_rows),
            "req",
            split_axis=0,
            concat_axis=0,
            tiled=True,
        ),
    )
    moved_states = received[0][recv_rows]
    moved_inner = received[1][recv_rows]
    moved_shared = received[2][recv_rows]
    window = projected.shape[0] // slot_count
    projected = projected.reshape(slot_count, window, projected.shape[1])
    gate_part = projected[:, :, :inner_here]
    value_part = projected[:, :, inner_here : 2 * inner_here]
    fresh_shared = projected[:, :, 2 * inner_here : 2 * inner_here + 2 * state_dim]
    head_index = lax.axis_index("head")
    step_raw = lax.dynamic_slice_in_dim(
        projected[:, :, 2 * inner_here + 2 * state_dim :],
        head_index * heads_here,
        heads_here,
        axis=2,
    )
    edge_inner_out = new_edge(moved_inner, value_part, counts)
    edge_shared_out = new_edge(moved_shared, fresh_shared, counts)
    mixed_inner = depthwise(moved_inner, value_part, conv_inner, conv_inner_bias)
    mixed_shared = depthwise(moved_shared, fresh_shared, conv_shared, conv_shared_bias)
    valid = jnp.arange(window)[None, :] < counts[:, None]
    step_size = jax.nn.softplus(step_raw.astype(jnp.float32) + step_bias)
    step_size = jnp.where(valid[:, :, None], step_size, 0.0)
    decay = -jnp.exp(decay_log)
    inputs = mixed_inner.reshape(slot_count, window, heads_here, head_dim)
    entries = mixed_shared[:, :, :state_dim]
    readouts = mixed_shared[:, :, state_dim:]
    carried = moved_states.astype(jnp.float32)
    collected = []
    for position in range(window):
        carried, produced = advance(
            carried,
            step_size[:, position],
            inputs[:, position],
            entries[:, position],
            readouts[:, position],
            decay,
            skip_gain,
        )
        collected.append(produced)
    outputs = jnp.stack(collected, axis=1)
    outputs = outputs.reshape(slot_count, window, inner_here)
    gated = outputs * jax.nn.silu(gate_part.astype(jnp.float32))
    square_part = jnp.sum(gated * gated, axis=-1, keepdims=True)
    square_sum = lax.psum(square_part, "head")
    full_inner = inner_here * lax.axis_size("head")
    scaled = gated * lax.rsqrt(square_sum / full_inner + EPS) * gate_gain
    scaled = (
        jnp.where(valid[:, :, None], scaled, 0.0)
        .astype(jnp.bfloat16)
        .reshape(slot_count * window, inner_here)
    )
    mixer = lax.psum_scatter(
        jnp.dot(scaled, out_weight, preferred_element_type=jnp.float32).astype(jnp.bfloat16),
        "head",
        scatter_dimension=0,
        tiled=True,
    ).astype(jnp.float32)
    hidden_out = (rows_in + mixer).astype(jnp.bfloat16)
    return (hidden_out, carried.astype(jnp.bfloat16), edge_inner_out, edge_shared_out)


def solution(mesh):
    placed = (
        P(("req", "head"), None),
        P(),
        P(None, None, "head"),
        P(),
        P(None, "head"),
        P("head"),
        P(),
        P(),
        P("head"),
        P("head"),
        P("head"),
        P("head"),
        P("head", None),
        P("req", "head", None, None),
        P("req", None, "head"),
        P("req", None, None),
        P("req"),
        P(),
        P(),
        P(),
    )
    return jax.shard_map(
        local,
        mesh=mesh,
        in_specs=placed,
        out_specs=(
            P(("req", "head"), None),
            P("req", "head", None, None),
            P("req", None, "head"),
            P("req", None, None),
        ),
        check_vma=False,
    )
```

profile of v0, /device:TPU:2, one launch (start us, length us, event | category | flops | bytes accessed | tf_op | source)
XLA Modules:
  0.0 327.2 jit_solution(12424475779777113080)
XLA Ops:
  7.3 4.9 %copy.182 = bf16[32,6,64,128]{3,2,1,0:T(8,128)(2,1)} copy(bf16[32,6,64,128]{3,2,1,0:T(8,128)(2,1)} %param.39) | data formatting | bytes 6291456
  12.2 0.6 dynamic_slice.13
  13.5 1.5 constant_dynamic-slice_fusion.1
  15.0 1.3 bitcast_reduce_fusion
  18.1 24.2 %all_gather.15 = bf16[32,3,256]{2,1,0:T(4,128)(2,1)S(1)} all-gather(bf16[1,3,256]{2,1,0:T(4,128)(2,1)S(1)} %copy.132), channel_id=1, replica_groups=mesh['req'=32,'head'=8] {'req'}, dimensions={0}, use_global_device_ids=true | all-gather | bytes 50688 | tf_op jit(solution)/shard_map/all_gather | solution.py:111
  42.3 0.7 and_reduce_fusion
  43.0 0.6 dynamic-slice_select_fusion.2
  43.8 4.3 %scatter_custom_fusion = s32[1024]{0:T(1024)S(1)} fusion(s32[1024]{0:T(1024)S(1)} %compare_select_fusion.1, s32[1024]{0:T(1024)S(1)} %iota.23, s32[]{:T(128)} %constant.131.clone.1), kind=kCustom, calls=%fused_computation.125 | custom fusion | bytes 4100 | tf_op jit(solution)/shard_map/scatter | solution.py:52
  48.1 0.1 and_select_fusion.1
  48.3 0.2 convert_reduce_fusion.1
  48.5 0.7 broadcast_in_dim.159
  49.1 4.2 %scatter_fusion.2 = bf16[32,3,256]{2,1,0:T(4,128)(2,1)} fusion(bf16[32,3,256]{2,1,0:T(4,128)(2,1)} %broadcast_in_dim.159, s32[32]{0:T(128)S(1)} %compare_select_fusion.3, bf16[32,3,256]{2,1,0:T(4,128)(2,1)S(1)} %copy.100), kind=kCustom, calls=%fused_computation.6 | custom fusion | bytes 147584 | tf_op jit(solution)/shard_map/scatter | solution.py:48
  53.3 5.8 %all-to-all-start.2 = ((bf16[32,3,256]{2,1,0:T(4,128)(2,1)}), bf16[32,3,256]{2,1,0:T(4,128)(2,1)S(1)}, u32[]{:S(2)}, u32[]{:S(2)}) async-start(bf16[32,3,256]{2,1,0:T(4,128)(2,1)} %scatter_fusion.2), calls=%async_computation.2 | async-start | bytes 131072 | tf_op jit(solution)/shard_map/all_to_all | solution.py:134
  59.2 0.1 fusion.34
  59.4 28.8 %all_gather.13 = bf16[128,1536]{1,0:T(8,128)(2,1)S(1)} all-gather(bf16[16,1536]{1,0:T(8,128)(2,1)S(1)} %fusion.36), channel_id=1, replica_groups=mesh['req'=32,'head'=8] {'head'}, dimensions={0}, use_global_device_ids=true | all-gather | bytes 442368 | tf_op jit(solution)/shard_map/all_gather | solution.py:98
  88.2 0.4 convolution_convert_fusion.2
  88.6 0.1 copy.88
  88.8 2.1 copy.142
  91.0 0.5 convolution_convert_fusion.1
  91.6 0.1 constant_dynamic-slice_fusion.3
  91.7 0.1 copy.128
  91.8 24.0 %all_gather.14 = bf16[32,3,384]{2,1,0:T(4,128)(2,1)S(1)} all-gather(bf16[1,3,384]{2,1,0:T(4,128)(2,1)S(1)} %copy.130), channel_id=1, replica_groups=mesh['req'=32,'head'=8] {'req'}, dimensions={0}, use_global_device_ids=true | all-gather | bytes 76032 | tf_op jit(solution)/shard_map/all_gather | solution.py:110
  115.8 0.2 convert_reduce_fusion
  116.0 0.6 dynamic-slice_select_fusion.1
  116.6 0.1 fusion.49
  116.8 0.7 and_reduce_fusion.1
  117.6 0.7 broadcast_in_dim.158
  118.3 4.0 %scatter_fusion.1 = bf16[32,3,384]{2,1,0:T(4,128)(2,1)} fusion(bf16[32,3,384]{2,1,0:T(4,128)(2,1)} %broadcast_in_dim.158, s32[32]{0:T(128)S(1)} %compare_select_fusion.3, bf16[32,3,384]{2,1,0:T(4,128)(2,1)S(1)} %copy.95), kind=kCustom, calls=%fused_computation.5 | custom fusion | bytes 221312 | tf_op jit(solution)/shard_map/scatter | solution.py:48
  122.3 5.5 %all-to-all-start.1 = ((bf16[32,3,384]{2,1,0:T(4,128)(2,1)}), bf16[32,3,384]{2,1,0:T(4,128)(2,1)S(1)}, u32[]{:S(2)}, u32[]{:S(2)}) async-start(bf16[32,3,384]{2,1,0:T(4,128)(2,1)} %scatter_fusion.1), calls=%async_computation.1 | async-start | bytes 196608 | tf_op jit(solution)/shard_map/all_to_all | solution.py:127
  127.8 2.3 fusion.38
  130.0 2.5 broadcast_in_dim.83
  132.5 10.2 %scatter_fusion = bf16[32,6,64,128]{3,2,1,0:T(8,128)(2,1)} fusion(bf16[32,6,64,128]{3,2,1,0:T(8,128)(2,1)} %broadcast_in_dim.83, s32[32]{0:T(128)S(1)} %compare_select_fusion.3, bf16[32,6,64,128]{3,2,1,0:T(8,128)(2,1)} %fusion.38), kind=kCustom, calls=%fused_computation.4 | custom fusion | bytes 9437312 | tf_op jit(solution)/shard_map/scatter | solution.py:48
  142.7 7.6 %all-to-all-start = ((bf16[32,6,64,128]{3,2,1,0:T(8,128)(2,1)}), bf16[32,6,64,128]{3,2,1,0:T(8,128)(2,1)}, u32[]{:S(2)}, u32[]{:S(2)}) async-start(bf16[32,6,64,128]{3,2,1,0:T(8,128)(2,1)} %scatter_fusion), calls=%async_computation | async-start | bytes 6291456 | tf_op jit(solution)/shard_map/all_to_all | solution.py:120
  150.3 0.2 reduce-scatter.2.cloned.1.call-start
  150.6 0.1 copy.141
  150.7 0.1 copy.140
  150.8 0.1 copy.139
  150.8 0.1 copy.138
  151.0 0.1 copy.91
  151.0 0.1 copy.102
  151.1 0.1 copy.105
  151.5 0.6 gather_fusion.2
  152.2 0.3 fusion.45
  152.4 0.6 copy.116
  153.1 0.2 divide_multiply_fusion.1
  153.4 0.7 gather_fusion.1
  154.1 0.1 divide_multiply_fusion
  154.2 0.1 reshape.267
  154.4 0.7 fusion.41
  155.1 0.2 fusion.30
  155.3 34.7 %all-to-all-done = bf16[32,6,64,128]{3,2,1,0:T(8,128)(2,1)} async-done(((bf16[32,6,64,128]{3,2,1,0:T(8,128)(2,1)}), bf16[32,6,64,128]{3,2,1,0:T(8,128)(2,1)}, u32[]{:S(2)}, u32[]{:S(2)}) %all-to-all-start) | async-done | bytes 3145760 | tf_op jit(solution)/shard_map/all_to_all | solution.py:120
  190.0 4.5 %gather_fusion = bf16[32,6,64,128]{3,2,1,0:T(8,128)(2,1)} fusion(bf16[32,6,64,128]{3,2,1,0:T(8,128)(2,1)} %all-to-all-done, s32[1024]{0:T(1024)S(1)} %pad_clamp_fusion), kind=kCustom, calls=%fused_computation | custom fusion | bytes 6291584 | tf_op jit(solution)/shard_map/gather | solution.py:142
  194.6 16.5 %fusion = f32[32,1,6,64]{3,1,2,0:T(1,128)S(1)} fusion(bf16[32,6,64,128]{3,2,1,0:T(8,128)(2,1)} %gather_fusion, f32[32,128]{1,0:T(8,128)S(1)} %bitcast.123, f32[32,6,64]{2,1,0:T(8,128)S(1)} %get-tuple-element.136, f32[32,6]{1,0:T(8,128)S(1)} %copy.91, f32[32,4,256]{2,1,0:T(4,128)S(1)} %divide_multiply_fusion.1), kind=kOutput, calls=%fused_computation.11 | convolution fusion | flops 25165824 | bytes 3375104 | tf_op jit(solution)/shard_map/khpn,kn->khp/dot_general | solution.py:15
  211.1 16.0 %fusion.1 = f32[32,1,6,64]{3,1,2,0:T(1,128)S(1)} fusion(bf16[32,6,64,128]{3,2,1,0:T(8,128)(2,1)S(1)} %copy-done.1, f32[32,128]{1,0:T(8,128)S(1)} %bitcast.133, f32[32,6,64]{2,1,0:T(8,128)S(1)} %get-tuple-element.139, f32[32,6]{1,0:T(8,128)S(1)} %copy.102, f32[32,128]{1,0:T(8,128)S(1)} %bitcast.124, f32[32,6,64]{2,1,0:T(8,128)S(1)} %get-tuple-element.136, ...), kind=kOutput, calls=%fused_computation.12 | convolution fusion | flops 29884416 | bytes 3538944 | tf_op jit(solution)/shard_map/khpn,kn->khp/dot_general | solution.py:15
  227.2 19.6 %fusion.16 = f32[32,1,6,64]{3,1,2,0:T(1,128)S(1)} fusion(bf16[32,6,64,128]{3,2,1,0:T(8,128)(2,1)S(1)} %copy-done.1, f32[32,128]{1,0:T(8,128)S(1)} %bitcast.130, f32[32,6,64]{2,1,0:T(8,128)S(1)} %get-tuple-element.138, f32[32,6]{1,0:T(8,128)S(1)} %copy.105, f32[32,128]{1,0:T(8,128)S(1)} %bitcast.134, f32[32,6,64]{2,1,0:T(8,128)S(1)} %get-tuple-element.139, ...), kind=kOutput, calls=%fused_computation.28 | convolution fusion | flops 34603008 | bytes 3702784 | tf_op jit(solution)/shard_map/khpn,kn->khp/dot_general | solution.py:15
  246.8 21.4 %fusion.3 = f32[32,1,6,64]{3,1,2,0:T(1,128)S(1)} fusion(f32[32,128]{1,0:T(8,128)S(1)} %bitcast.128, f32[32,6,64]{2,1,0:T(8,128)S(1)} %get-tuple-element.137, f32[32,6]{1,0:T(8,128)S(1)} %copy.107, bf16[32,6,64,128]{3,2,1,0:T(8,128)(2,1)S(1)} %copy-done.1, f32[32,128]{1,0:T(8,128)S(1)} %bitcast.131, f32[32,6,64]{2,1,0:T(8,128)S(1)} %get-tuple-element.138, ...), kind=kOutput, calls=%fused_computation.14 | convolution fusion | flops 39321600 | bytes 3866624 | tf_op jit(solution)/shard_map/khpn,kn->khp/dot_general | solution.py:15
  268.2 0.1 bitcast_add_fusion.3
  268.6 0.1 multiply_reduce_fusion
  268.8 16.8 %psum.7 = f32[32,4,1]{0,1,2:T(4,128)S(1)} all-reduce(f32[32,4,1]{0,1,2:T(4,128)S(1)} %bitcast.137), channel_id=1, replica_groups=mesh['req'=32,'head'=8] {'head'}, use_global_device_ids=true, to_apply=%region_11.12 | all-reduce | flops 128 | bytes 1024 | tf_op jit(solution)/shard_map/psum | solution.py:185
  285.5 0.1 select_convert_fusion
  285.7 1.1 convolution_convert_fusion
  286.9 10.6 %fusion.2 = bf16[32,6,64,128]{3,2,1,0:T(8,128)(2,1)} fusion(f32[32,128]{1,0:T(8,128)S(1)} %bitcast.129, f32[32,6,64]{2,1,0:T(8,128)S(1)} %get-tuple-element.137, f32[32,6]{1,0:T(8,128)S(1)} %copy.107, f32[32,128]{1,0:T(8,128)S(1)} %bitcast.132, f32[32,6,64]{2,1,0:T(8,128)S(1)} %get-tuple-element.138, f32[32,6]{1,0:T(8,128)S(1)} %copy.105, ...), kind=kLoop, calls=%fused_computation.13 | loop fusion | flops 22020096 | bytes 6556672 | tf_op jit(solution)/shard_map/convert_element_type | solution.py:200
  297.5 21.4 %reduce-scatter.2.cloned.1.call-done = bf16[16,1536]{1,0:T(8,128)(2,1)} async-done(((bf16[128,1536]{1,0:T(8,128)(2,1)}), bf16[16,1536]{1,0:T(8,128)(2,1)}) %reduce-scatter.2.cloned.1.call-update) | async-done | bytes 49168 | tf_op jit(solution)/shard_map/reduce_scatter | solution.py:193
  319.0 1.4 fusion.37
  (94 shorter events, 1.8 us)
Async XLA Ops:
  7.2 278.6 %copy-start = (bf16[384,1536]{1,0:T(8,128)(2,1)S(1)}, bf16[384,1536]{1,0:T(8,128)(2,1)}, u32[]{:S(2)}) copy-start(bf16[384,1536]{1,0:T(8,128)(2,1)} %param.38) | copy-start | bytes 3538948
  7.2 35.1 %copy-start.18 = (s32[3]{0:T(128)S(1)}, s32[3]{0:T(128)}, u32[]{:S(2)}) copy-start(s32[3]{0:T(128)} %constant.151.clone.1) | copy-start | bytes 40
  7.2 52.0 %copy-start.3 = (bf16[16,1536]{1,0:T(8,128)(2,1)S(1)}, bf16[16,1536]{1,0:T(8,128)(2,1)}, u32[]{:S(2)}) copy-start(bf16[16,1536]{1,0:T(8,128)(2,1)} %param.26) | copy-start | bytes 147460
  7.2 52.1 %copy-start.6 = (f32[1536]{0:T(1024)S(1)}, f32[1536]{0:T(1024)}, u32[]{:S(2)}) copy-start(f32[1536]{0:T(1024)} %param.27) | copy-start | bytes 18436
  7.2 81.0 %copy-start.2 = (bf16[1536,304]{0,1:T(8,128)(2,1)S(1)}, bf16[1536,304]{0,1:T(8,128)(2,1)}, u32[]{:S(2)}) copy-start(bf16[1536,304]{0,1:T(8,128)(2,1)} %param.29) | copy-start | bytes 2801668
  7.2 5.0 %copy-start.4 = (bf16[32,3,384]{2,0,1:T(8,128)(2,1)S(1)}, bf16[32,3,384]{2,0,1:T(8,128)(2,1)}, u32[]{:S(2)}) copy-start(bf16[32,3,384]{2,0,1:T(8,128)(2,1)} %param.40) | copy-start | bytes 221188
  7.2 4.9 %copy-start.5 = (bf16[32,3,256]{2,0,1:T(8,128)(2,1)S(1)}, bf16[32,3,256]{2,0,1:T(8,128)(2,1)}, u32[]{:S(2)}) copy-start(bf16[32,3,256]{2,0,1:T(8,128)(2,1)} %param.41) | copy-start | bytes 147460
  7.2 5.0 %copy-start.19 = (s32[32]{0:T(128)S(1)}, s32[32]{0:T(128)}, u32[]{:S(2)}) copy-start(s32[32]{0:T(128)} %param.43) | copy-start | bytes 388
  7.3 7.8 %copy-start.16 = (s32[32]{0:T(128)S(1)}, s32[32]{0:T(128)}, u32[]{:S(2)}) copy-start(s32[32]{0:T(128)} %param.44) | copy-start | bytes 388
  7.3 36.5 %copy-start.8 = (s32[1024]{0:T(1024)S(1)}, s32[1024]{0:T(1024)}, u32[]{:S(2)}) copy-start(s32[1024]{0:T(1024)} %param.45) | copy-start | bytes 12292
  7.3 120.5 %all-gather.2.cloned.1.call-start = ((), (), s32[]{:S(2)}) async-start(), calls=%async_computation.4 | async-start | bytes 3244032 | tf_op jit(solution)/shard_map/all_gather | solution.py:109
  53.3 69.0 %all-to-all-start.2 = ((bf16[32,3,256]{2,1,0:T(4,128)(2,1)}), bf16[32,3,256]{2,1,0:T(4,128)(2,1)S(1)}, u32[]{:S(2)}, u32[]{:S(2)}) async-start(bf16[32,3,256]{2,1,0:T(4,128)(2,1)} %scatter_fusion.2), calls=%async_computation.2 | async-start | bytes 131072 | tf_op jit(solution)/shard_map/all_to_all | solution.py:134
  90.9 25.0 %copy-start.15 = (s32[32]{0:T(128)S(1)}, s32[32]{0:T(128)}, u32[]{:S(2)}) copy-start(s32[32]{0:T(128)} %param.42) | copy-start | bytes 388
  90.9 25.0 %copy-start.20 = (f32[6]{0:T(128)S(1)}, f32[6]{0:T(128)}, u32[]{:S(2)}) copy-start(f32[6]{0:T(128)} %param.35) | copy-start | bytes 76
  90.9 25.6 %copy-start.14 = (f32[6]{0:T(128)S(1)}, f32[6]{0:T(128)}, u32[]{:S(2)}) copy-start(f32[6]{0:T(128)} %param.34) | copy-start | bytes 76
  91.0 25.8 %copy-start.17 = (s32[4]{0:T(128)S(1)}, s32[4]{0:T(128)}, u32[]{:S(2)}) copy-start(s32[4]{0:T(128)} %constant.142.clone.1) | copy-start | bytes 52
  122.3 20.4 %all-to-all-start.1 = ((bf16[32,3,384]{2,1,0:T(4,128)(2,1)}), bf16[32,3,384]{2,1,0:T(4,128)(2,1)S(1)}, u32[]{:S(2)}, u32[]{:S(2)}) async-start(bf16[32,3,384]{2,1,0:T(4,128)(2,1)} %scatter_fusion.1), calls=%async_computation.1 | async-start | bytes 196608 | tf_op jit(solution)/shard_map/all_to_all | solution.py:127
  142.7 8.6 %copy-start.7 = (f32[4,384]{1,0:T(4,128)S(1)}, f32[4,384]{1,0:T(4,128)}, u32[]{:S(2)}) copy-start(f32[4,384]{1,0:T(4,128)} %param.30) | copy-start | bytes 18436
  142.7 8.6 %copy-start.9 = (f32[4,256]{1,0:T(4,128)S(1)}, f32[4,256]{1,0:T(4,128)}, u32[]{:S(2)}) copy-start(f32[4,256]{1,0:T(4,128)} %param.32) | copy-start | bytes 12292
  142.7 10.4 %copy-start.12 = (f32[256]{0:T(256)S(1)}, f32[256]{0:T(256)}, u32[]{:S(2)}) copy-start(f32[256]{0:T(256)} %param.33) | copy-start | bytes 3076
  142.7 47.3 %all-to-all-start = ((bf16[32,6,64,128]{3,2,1,0:T(8,128)(2,1)}), bf16[32,6,64,128]{3,2,1,0:T(8,128)(2,1)}, u32[]{:S(2)}, u32[]{:S(2)}) async-start(bf16[32,6,64,128]{3,2,1,0:T(8,128)(2,1)} %scatter_fusion), calls=%async_computation | async-start | bytes 6291456 | tf_op jit(solution)/shard_map/all_to_all | solution.py:120
  150.3 3.8 %copy-start.10 = (f32[384]{0:T(512)S(1)}, f32[384]{0:T(512)}, u32[]{:S(2)}) copy-start(f32[384]{0:T(512)} %param.31) | copy-start | bytes 4612
  150.3 168.6 %reduce-scatter.2.cloned.1.call-start = ((), (), s32[]{:S(2)}) async-start(), calls=%async_computation.5 | async-start | bytes 442368 | tf_op jit(solution)/shard_map/reduce_scatter | solution.py:193
  194.6 16.6 %copy-start.1 = (bf16[32,6,64,128]{3,2,1,0:T(8,128)(2,1)S(1)}, bf16[32,6,64,128]{3,2,1,0:T(8,128)(2,1)}, u32[]{:S(2)}) copy-start(bf16[32,6,64,128]{3,2,1,0:T(8,128)(2,1)} %gather_fusion) | copy-start | bytes 9437188
  246.7 21.4 %copy-start.13 = (f32[6]{0:T(128)S(1)}, f32[6]{0:T(128)}, u32[]{:S(2)}) copy-start(f32[6]{0:T(128)} %param.36) | copy-start | bytes 76
  246.8 38.8 %copy-start.11 = (f32[384]{0:T(512)S(1)}, f32[384]{0:T(512)}, u32[]{:S(2)}) copy-start(f32[384]{0:T(512)} %param.37) | copy-start | bytes 4612
Sparse Core Ops, SparseCore 0:
  15.2 53.5 all-gather.1
  287.0 31.9 reduce-scatter.1
where the time goes:
time: 328 us; the launch traced here: 327 us
  blocking collectives  93.7 us (29%)
  matrix products  75.5 us (23%)
  waiting for transfers between devices  56.2 us (17%)
  local copies, waits for them, and re-layouts  44.4 us (14%)
  other arithmetic  21.2 us (6%)
  starting transfers between devices  19.1 us (6%)
  between operations  17.1 us (5%)
    dot_general x4, matrix products, advance(): jnp.einsum('khpn,kn->khp', carried, readout_now, precision=lax.Precision....  73.5 us
    all_to_all x1, waiting for transfers between devices, local(): lax.all_to_all(pack_pages(sectioned_states, send_rows, buffer_rows), 'req...  34.7 us
    all_gather x1, blocking collectives, local(): piece_rows = lax.all_gather(normed, 'head', axis=0, tiled=True)  28.8 us
    all_gather x1, blocking collectives, local(): lax.all_gather(edge_shared[local_ids], 'req', axis=0, tiled=True)  24.2 us
    all_gather x1, blocking collectives, local(): lax.all_gather(edge_inner[local_ids], 'req', axis=0, tiled=True)  24 us
    reduce_scatter x1, waiting for transfers between devices, local(): lax.psum_scatter(jnp.dot(scaled, out_weight, preferred_element_type=jnp.f...  21.4 us
    scatter x3, local copies, waits for them, and re-layouts, pack_pages(): return empty.at[send_rows].set(member)  18.4 us
    psum x1, blocking collectives, local(): square_sum = lax.psum(square_part, 'head')  16.8 us
  transfers between devices with their start and end apart: 5, of which 2 were waited for; matrix products, arithmetic and copies ran while one was open for 16% of the time, Pallas kernels for 0%

commit v1 on v0

v1 whole, which is shorter than its diff:
```python
import jax
import jax.numpy as jnp
from jax import lax
from jax.sharding import PartitionSpec as P

EPS = 1e-05
HIGH = lax.Precision.HIGHEST


def depthwise(edge, fresh, weight, offset_bias):
    sequence = jnp.concatenate([edge, fresh], axis=1).astype(jnp.float32)
    window = fresh.shape[1]
    summed = sequence[:, 0:window] * weight[0]
    for offset in range(1, weight.shape[0]):
        summed = summed + sequence[:, offset : offset + window] * weight[offset]
    return jax.nn.silu(summed + offset_bias)


def new_edge(edge, fresh, counts):
    sequence = jnp.concatenate([edge, fresh], axis=1)
    keep_rows = edge.shape[1]
    result = edge
    for length in range(1, fresh.shape[1] + 1):
        result = jnp.where(
            (counts == length)[:, None, None], sequence[:, length : length + keep_rows], result
        )
    return result


def rank_rows(partner, position, capacity):
    matching = partner[:, None] == partner[None, :]
    earlier = position[None, :] < position[:, None]
    ranking = jnp.sum(jnp.logical_and(matching, earlier), axis=1)
    return partner * capacity + ranking


def route_rows(anchor, first_slot, slot_count, all_slots, capacity):
    inverse = jnp.zeros(all_slots.shape, jnp.int32).at[anchor].set(all_slots)
    targets = lax.dynamic_slice_in_dim(inverse, first_slot, slot_count)
    send_rows = rank_rows(targets // slot_count, targets % slot_count, capacity)
    sources = lax.dynamic_slice_in_dim(anchor, first_slot, slot_count)
    recv_rows = rank_rows(sources // slot_count, jnp.arange(slot_count, dtype=jnp.int32), capacity)
    return (send_rows, recv_rows)


def migrate(item, mig_dest, slot_count, groups, device):
    length = item.shape[0]
    piece = -(-length // groups)
    padded = jnp.pad(item, (0, piece * groups - length)).reshape(groups, piece)
    first = lax.all_to_all(padded, "req", 0, 0, tiled=True)
    dest_dev = mig_dest // slot_count
    order = jnp.zeros((groups,), jnp.int32).at[dest_dev].set(jnp.arange(groups, dtype=jnp.int32))
    second = lax.all_to_all(first[order], "req", 0, 0, tiled=True)
    arrived = second.reshape(-1)[:length]
    target_local = mig_dest[order[device]] - device * slot_count
    return arrived, target_local


def local(
    tokens,
    pre_gain,
    inner_weight,
    shared_weight,
    conv_inner,
    conv_inner_bias,
    conv_shared,
    conv_shared_bias,
    step_bias,
    decay_log,
    skip_gain,
    gate_gain,
    out_weight,
    states,
    edge_inner,
    edge_shared,
    counts,
    mig_ids,
    mig_dest,
    reorder,
):
    slot_count, heads_here, head_dim, state_dim = states.shape
    inner_here = heads_here * head_dim
    lanes = state_dim
    groups = lax.axis_size("req")
    device = lax.axis_index("req")
    first_slot = device * slot_count
    stride = (slot_count + groups - 1) // groups
    all_slots = jnp.arange(slot_count * groups, dtype=jnp.int32)

    rows_in = tokens.astype(jnp.float32)
    normed = (
        rows_in * lax.rsqrt(jnp.mean(rows_in * rows_in, axis=-1, keepdims=True) + EPS) * pre_gain
    ).astype(jnp.bfloat16)
    inner_flat = inner_weight.reshape(inner_weight.shape[0], 2 * inner_here)
    piece_rows = lax.all_gather(normed, "head", axis=0, tiled=True)
    inner_rows = jnp.dot(piece_rows, inner_flat, preferred_element_type=jnp.float32).astype(
        jnp.bfloat16
    )
    shared_rows = jnp.dot(piece_rows, shared_weight, preferred_element_type=jnp.float32).astype(
        jnp.bfloat16
    )

    state_rows = heads_here * head_dim * state_dim // lanes
    inner_edge_rows = edge_inner.shape[1] * edge_inner.shape[2] // lanes
    shared_edge_rows = edge_shared.shape[1] * edge_shared.shape[2] // lanes
    packed = jnp.concatenate(
        [
            states.reshape(slot_count, state_rows, lanes),
            edge_inner.reshape(slot_count, inner_edge_rows, lanes),
            edge_shared.reshape(slot_count, shared_edge_rows, lanes),
        ],
        axis=1,
    )
    row_total = packed.shape[1]

    moving = mig_ids.shape[0] // groups
    own_id = mig_ids[device * moving]
    mig_local = own_id - first_slot
    item = lax.dynamic_index_in_dim(packed, mig_local, 0, keepdims=False).reshape(-1)
    arrived, target_local = migrate(item, mig_dest, slot_count, groups, device)
    arrived = arrived.reshape(row_total, lanes)

    send_rows, recv_rows = route_rows(reorder, first_slot, slot_count, all_slots, stride)
    buffer_rows = groups * stride
    send_idx = (
        jnp.zeros((buffer_rows,), jnp.int32).at[send_rows].set(jnp.arange(slot_count, dtype=jnp.int32))
    )
    send_buf = jnp.where(
        (send_idx == target_local)[:, None, None], arrived[None], packed[send_idx]
    )
    received = lax.all_to_all(send_buf, "req", 0, 0, tiled=True)
    moved = received[recv_rows]
    moved_states = moved[:, :state_rows].reshape(slot_count, heads_here, head_dim, state_dim)
    moved_inner = moved[:, state_rows : state_rows + inner_edge_rows].reshape(edge_inner.shape)
    moved_shared = moved[:, state_rows + inner_edge_rows :].reshape(edge_shared.shape)

    window = inner_rows.shape[0] // slot_count
    inner_rows = inner_rows.reshape(slot_count, window, 2 * inner_here)
    shared_rows = shared_rows.reshape(slot_count, window, shared_rows.shape[1])
    gate_part = inner_rows[:, :, :inner_here]
    value_part = inner_rows[:, :, inner_here:]
    fresh_shared = shared_rows[:, :, : 2 * state_dim]
    head_index = lax.axis_index("head")
    step_raw = lax.dynamic_slice_in_dim(
        shared_rows[:, :, 2 * state_dim :], head_index * heads_here, heads_here, axis=2
    )
    edge_inner_out = new_edge(moved_inner, value_part, counts)
    edge_shared_out = new_edge(moved_shared, fresh_shared, counts)
    mixed_inner = depthwise(moved_inner, value_part, conv_inner, conv_inner_bias)
    mixed_shared = depthwise(moved_shared, fresh_shared, conv_shared, conv_shared_bias)
    valid = jnp.arange(window)[None, :] < counts[:, None]
    step_size = jax.nn.softplus(step_raw.astype(jnp.float32) + step_bias)
    step_size = jnp.where(valid[:, :, None], step_size, 0.0)
    decay = -jnp.exp(decay_log)
    inputs = mixed_inner.reshape(slot_count, window, heads_here, head_dim)
    entries = mixed_shared[:, :, :state_dim]
    readouts = mixed_shared[:, :, state_dim:]

    factor = jnp.exp(step_size * decay)
    cum = [factor[:, 0]]
    for t in range(1, window):
        cum.append(cum[-1] * factor[:, t])
    cumulative = jnp.stack(cum, axis=1)
    span = {}
    for t in range(window):
        span[(t, t)] = jnp.ones_like(factor[:, 0])
        for s in range(t - 1, -1, -1):
            span[(t, s)] = span[(t, s + 1)] * factor[:, s + 1]
    held = moved_states.astype(jnp.float32)
    from_state = jnp.einsum("rhpn,rtn->rthp", held, readouts, precision=HIGH)
    overlap = jnp.einsum("rtn,rsn->rts", readouts, entries, precision=HIGH)
    weighted = step_size[:, :, :, None] * inputs
    produced = []
    for t in range(window):
        acc = cumulative[:, t, :, None] * from_state[:, t]
        for s in range(t + 1):
            coef = span[(t, s)] * overlap[:, t, s, None]
            acc = acc + coef[:, :, None] * weighted[:, s]
        produced.append(acc + skip_gain[None, :, None] * inputs[:, t])
    outputs = jnp.stack(produced, axis=1)
    last = window - 1
    pushed = jnp.stack([span[(last, s)] for s in range(window)], axis=1)[:, :, :, None] * weighted
    update = jnp.einsum("rshp,rsn->rhpn", pushed, entries, precision=HIGH)
    final = cumulative[:, last, :, None, None] * held + update
    states_out = final.astype(jnp.bfloat16)

    outputs = outputs.reshape(slot_count, window, inner_here)
    gated = outputs * jax.nn.silu(gate_part.astype(jnp.float32))
    square_part = jnp.sum(gated * gated, axis=-1).reshape(slot_count * window, 1)
    pre_scaled = (
        jnp.where(valid[:, :, None], gated * gate_gain, 0.0)
        .astype(jnp.bfloat16)
        .reshape(slot_count * window, inner_here)
    )
    partial = jnp.dot(pre_scaled, out_weight, preferred_element_type=jnp.float32)
    extra = jnp.broadcast_to(square_part, (partial.shape[0], 128))
    combined = jnp.concatenate([partial, extra], axis=1)
    reduced = lax.psum_scatter(combined, "head", scatter_dimension=0, tiled=True)
    full_inner = inner_here * lax.axis_size("head")
    scale = lax.rsqrt(reduced[:, -1:] / full_inner + EPS)
    hidden_out = (rows_in + reduced[:, : partial.shape[1]] * scale).astype(jnp.bfloat16)
    return (hidden_out, states_out, edge_inner_out, edge_shared_out)


def solution(mesh):
    placed = (
        P(("req", "head"), None),
        P(),
        P(None, None, "head"),
        P(),
        P(None, "head"),
        P("head"),
        P(),
        P(),
        P("head"),
        P("head"),
        P("head"),
        P("head"),
        P("head", None),
        P("req", "head", None, None),
        P("req", None, "head"),
        P("req", None, None),
        P("req"),
        P(),
        P(),
        P(),
    )
    return jax.shard_map(
        local,
        mesh=mesh,
        in_specs=placed,
        out_specs=(
            P(("req", "head"), None),
            P("req", "head", None, None),
            P("req", None, "head"),
            P("req", None, None),
        ),
        check_vma=False,
    )
```

time: 328 us -> 190 us (0.58)
  blocking collectives: 93.7 us -> 28.9 us
  matrix products: 75.5 us -> 24.2 us
  waiting for transfers between devices: 56.2 us -> 30 us
    dot_general x5 -> x4, matrix products: 74.7 us -> 23.3 us  [the longest x1 13.4 us: local(): update = jnp.einsum('rshp,rsn->rhpn', pushed, entries, precision=HIGH)]
    all_gather x2 -> x0, blocking collectives: 48.1 us -> none  [the longest x1 24.2 us: local(): lax.all_gather(edge_shared[local_ids], 'req', axis=0, tiled=True)]
    all_to_all x3, waiting for transfers between devices: 34.7 us -> 7.15 us  [the longest x1 5.27 us: local(): received = lax.all_to_all(send_buf, 'req', 0, 0, tiled=True)]
    scatter x7 -> x2, local copies, waits for them, and re-layouts: 18.6 us -> 1.35 us  [the longest x1 0.67 us: local(): jnp.zeros((buffer_rows,), jnp.int32).at[send_rows]]
    psum x1 -> x0, blocking collectives: 16.8 us -> none  [local(): square_sum = lax.psum(square_part, 'head')]
    convert_element_type x3 -> x2, other arithmetic: 12.2 us -> 2.63 us  [the longest x1 1.59 us: local(): (rows_in + reduced[:, :partial.shape[1]] * scale).astype(jnp.bfloat16)]
    mul x0 -> x10, local copies, waits for them, and re-layouts: none -> 6.54 us  [the longest x6 4.33 us: local(): coef = span[t, s] * overlap[:, t, s, None]]
    slice x5 -> x8, local copies, waits for them, and re-layouts: 0.17 us -> 6.43 us  [the longest x1 4.05 us: local(): moved[:, :state_rows].reshape(slot_count, heads_here, head_dim, state_dim)]
  transfers between devices with their start and end apart: 5 -> 4, of which waited for: 2 -> 3; matrix products, arithmetic and copies ran while one was open for 16% -> 18% of each run, Pallas kernels for 0% -> 0%
where the time goes in v1:
time: 190 us; the launch traced here: 189 us
  local copies, waits for them, and re-layouts  42.9 us (23%)
  waiting for transfers between devices  30 us (16%)
  blocking collectives  28.9 us (15%)
  matrix products  24.2 us (13%)
  other arithmetic  23.6 us (12%)
  starting transfers between devices  21 us (11%)
  between operations  18 us (9%)
    all_gather x1, blocking collectives, local(): piece_rows = lax.all_gather(normed, 'head', axis=0, tiled=True)  28.9 us
    reduce_scatter x1, waiting for transfers between devices, local(): lax.psum_scatter(combined, 'head', scatter_dimension=0, tiled=True)  22.8 us
    dot_general x1, matrix products, local(): update = jnp.einsum('rshp,rsn->rhpn', pushed, entries, precision=HIGH)  13.4 us
    dot_general x1, matrix products, local(): from_state = jnp.einsum('rhpn,rtn->rthp', held, readouts, precision=HIGH)  9.26 us
    unnamed x61, local copies, waits for them, and re-layouts  8.57 us
    all_to_all x1, starting transfers between devices, migrate(): first = lax.all_to_all(padded, 'req', 0, 0, tiled=True)  7.62 us
    all_to_all x1, starting transfers between devices, migrate(): second = lax.all_to_all(first[order], 'req', 0, 0, tiled=True)  7.38 us
    all_to_all x1, starting transfers between devices, local(): received = lax.all_to_all(send_buf, 'req', 0, 0, tiled=True)  5.93 us
  transfers between devices with their start and end apart: 4, of which 3 were waited for; matrix products, arithmetic and copies ran while one was open for 18% of the time, Pallas kernels for 0%

profile of v1, /device:TPU:2, one launch (start us, length us, event | category | flops | bytes accessed | tf_op | source)
XLA Modules:
  0.0 188.6 jit_solution(13441082247929192009)
XLA Ops:
  7.2 1.3 dynamic_slice.26
  9.2 0.8 copy.235
  10.1 0.9 copy.234
  11.1 2.3 %pad_maximum_fusion = bf16[32,399,128]{2,1,0:T(8,128)(2,1)S(1)} fusion(bf16[32,6,128]{2,1,0:T(8,128)(2,1)S(1)} %reshape.332, bf16[32,9,128]{2,1,0:T(8,128)(2,1)S(1)} %reshape.331, bf16[32,384,128]{2,1,0:T(8,128)(2,1)} %bitcast.73), kind=kLoop, calls=%fused_computation.7 | loop fusion | flops 9805824 | bytes 6537216 | tf_op jit(solution)/shard_map/concatenate | solution.py:106
  13.4 1.7 copy-done.1
  15.1 0.2 all_to_all.23
  15.3 0.5 broadcast.276
  15.8 1.3 reduce.39
  17.1 0.8 reshape.423
  17.9 7.6 %all-to-all-start = ((bf16[32,2,798]{2,1,0:T(2,128)(2,1)}), bf16[32,2,798]{2,1,0:T(2,128)(2,1)S(1)}, u32[]{:S(2)}, u32[]{:S(2)}) async-start(bf16[32,2,798]{2,1,0:T(2,128)(2,1)} %reshape.423), calls=%async_computation | async-start | bytes 229376 | tf_op jit(solution)/shard_map/all_to_all | solution.py:50
  25.6 4.3 %scatter_custom_fusion = s32[1024]{0:T(1024)S(1)} fusion(s32[1024]{0:T(1024)S(1)} %compare_select_fusion.1, s32[1024]{0:T(1024)S(1)} %iota.23, s32[]{:T(128)} %constant.75.clone.1), kind=kCustom, calls=%fused_computation.145 | custom fusion | bytes 4100 | tf_op jit(solution)/shard_map/scatter | solution.py:38
  30.1 0.2 convert_reduce_fusion.1
  30.3 0.7 scatter_custom_fusion.1
  31.0 0.7 scatter_custom_fusion.2
  31.7 0.6 dynamic_slice.24
  34.4 0.6 dynamic_slice.25
  35.8 0.7 gather_fusion
  36.5 0.7 reduce.40
  37.2 0.8 reshape.425
  38.0 7.4 %all-to-all-start.1 = ((bf16[32,2,798]{2,1,0:T(2,128)(2,1)}), bf16[32,2,798]{2,1,0:T(2,128)(2,1)S(1)}, u32[]{:S(2)}, u32[]{:S(2)}) async-start(bf16[32,2,798]{2,1,0:T(2,128)(2,1)} %reshape.425), calls=%async_computation.1 | async-start | bytes 229376 | tf_op jit(solution)/shard_map/all_to_all | solution.py:53
  45.4 4.6 %gather_fusion.1 = bf16[32,399,128]{2,1,0:T(8,128)(2,1)} fusion(bf16[32,399,128]{2,1,0:T(8,128)(2,1)} %copy-done.1, s32[1024]{0:T(1024)S(1)} %pad_clamp_fusion.1), kind=kCustom, calls=%fused_computation.1 | custom fusion | bytes 6537344 | tf_op jit(solution)/shard_map/gather | solution.py:129
  50.0 1.9 all-to-all-done.1
  52.1 0.6 reduce
  52.7 0.2 broadcast_in_dim.162
  52.9 3.9 %broadcast_select_fusion = bf16[32,399,128]{2,1,0:T(8,128)(2,1)} fusion(bf16[32,399,128]{2,1,0:T(8,128)(2,1)} %gather_fusion.1, pred[32]{0:T(512)(128)(4,1)S(1)} %broadcast_compare_fusion.3, bf16[399,128]{1,0:T(8,128)(2,1)S(1)} %broadcast_in_dim.162), kind=kLoop, calls=%fused_computation.8 | loop fusion | flops 1634304 | bytes 6639392 | tf_op jit(solution)/shard_map/jit(_where)/select_n | solution.py:128
  56.8 5.9 %all-to-all-start.2 = ((bf16[32,399,128]{2,1,0:T(8,128)(2,1)}), bf16[32,399,128]{2,1,0:T(8,128)(2,1)}, u32[]{:S(2)}, u32[]{:S(2)}) async-start(bf16[32,399,128]{2,1,0:T(8,128)(2,1)} %broadcast_select_fusion), calls=%async_computation.2 | async-start | bytes 6553600 | tf_op jit(solution)/shard_map/all_to_all | solution.py:131
  62.9 28.9 %all_gather.3 = bf16[128,1536]{1,0:T(8,128)(2,1)S(1)} all-gather(bf16[16,1536]{1,0:T(8,128)(2,1)S(1)} %fusion.17), channel_id=1, replica_groups=mesh['req'=32,'head'=8] {'head'}, dimensions={0}, use_global_device_ids=true | all-gather | bytes 442368 | tf_op jit(solution)/shard_map/all_gather | solution.py:95
  91.8 0.4 convolution_convert_fusion.1
  92.5 2.2 %copy.278 = bf16[192,8,2,384]{3,1,2,0:T(8,128)(2,1)S(1)} copy(bf16[192,8,2,384]{3,2,1,0:T(2,128)(2,1)} %bitcast.74) | data formatting | bytes 4718592
  94.7 0.5 convolution_convert_fusion
  95.6 0.8 copy.238
  96.4 0.6 slice_multiply_fusion.20
  97.0 0.7 copy.277
  97.7 0.2 convert_reduce_fusion
  98.1 0.7 fusion.71
  98.8 5.3 %all-to-all-done.2 = bf16[32,399,128]{2,1,0:T(8,128)(2,1)} async-done(((bf16[32,399,128]{2,1,0:T(8,128)(2,1)}), bf16[32,399,128]{2,1,0:T(8,128)(2,1)}, u32[]{:S(2)}, u32[]{:S(2)}) %all-to-all-start.2) | async-done | bytes 3268640 | tf_op jit(solution)/shard_map/all_to_all | solution.py:131
  104.1 4.6 %gather_fusion.2 = bf16[32,399,128]{2,1,0:T(8,128)(2,1)} fusion(bf16[32,399,128]{2,1,0:T(8,128)(2,1)} %all-to-all-done.2, s32[1024]{0:T(1024)S(1)} %pad_clamp_fusion), kind=kCustom, calls=%fused_computation.2 | custom fusion | bytes 6537344 | tf_op jit(solution)/shard_map/gather | solution.py:132
  108.7 4.0 %slice.275 = bf16[32,384,128]{2,1,0:T(8,128)(2,1)} slice(bf16[32,399,128]{2,1,0:T(8,128)(2,1)} %gather_fusion.2), slice={[0:32], [0:384], [0:128]} | slice | bytes 6291456 | tf_op jit(solution)/shard_map/slice | solution.py:133
  113.4 0.2 divide_multiply_fusion.1
  113.6 0.3 fusion.48
  113.9 9.3 %fusion.45 = f32[32,4,6,64]{3,1,2,0:T(4,128)S(1)} fusion(bf16[32,6,64,128]{3,2,1,0:T(8,128)(2,1)} %bitcast.69, f32[32,4,256]{2,1,0:T(4,128)S(1)} %divide_multiply_fusion.1), kind=kOutput, calls=%fused_computation.93 | convolution fusion | flops 75497472 | bytes 3407872 | tf_op jit(solution)/shard_map/rhpn,rtn->rthp/dot_general | solution.py:170
  123.2 1.6 slice_reduce_fusion.9
  124.8 0.6 bitcast_multiply_fusion.2
  125.4 0.7 copy.253
  126.1 0.7 copy.252
  126.8 0.7 copy.251
  127.5 0.7 copy.250
  128.2 1.3 broadcast_multiply_fusion
  129.4 2.9 %fusion.32 = (f32[32,6,64]{2,1,0:T(8,128)S(1)}, f32[32,6,64]{2,1,0:T(8,128)S(1)}) fusion(f32[32,4,6,64]{3,1,2,0:T(4,128)S(1)} %get-tuple-element.62, f32[32,4,6,64]{3,1,2,0:T(4,128)S(1)} %fusion.45, f32[32]{0:T(128)} %get-tuple-element.40, f32[32,6]{1,0:T(8,128)} %bitcast.76, f32[6]{0:T(128)} %param.30, f32[32,4,6,64]{3,1,2,0:T(4,128)S(1)} %get-tuple-element.61, ...), kind=kLoop, calls=%fused_computation.79 | loop fusion | flops 196608 | bytes 495640 | tf_op jit(solution)/shard_map/add | solution.py:179
  132.4 0.8 copy.244
  133.2 0.8 copy.243
  133.9 0.8 copy.248
  134.7 0.8 copy.247
  135.5 2.4 %fusion.31 = (f32[32,6,64]{2,1,0:T(8,128)S(1)}, f32[32,6,64]{2,1,0:T(8,128)S(1)}) fusion(f32[32,4,6,64]{3,1,2,0:T(4,128)S(1)} %get-tuple-element.62, f32[32,4,6,64]{3,1,2,0:T(4,128)S(1)} %fusion.45, f32[32]{0:T(128)} %get-tuple-element.48, f32[32,6]{1,0:T(8,128)S(1)} %copy.244, f32[32,6]{1,0:T(8,128)S(1)} %copy.243, f32[6]{0:T(128)} %param.30, ...), kind=kLoop, calls=%fused_computation.78 | loop fusion | flops 196608 | bytes 446488 | tf_op jit(solution)/shard_map/add | solution.py:179
  138.2 1.0 select_convert_fusion
  139.6 0.4 fusion.73
  140.1 1.0 pad_maximum_fusion.1
  141.5 0.3 fusion.41
  141.8 0.6 copy.263
  142.4 0.7 fusion.37
  143.1 13.4 %add_convert_fusion = bf16[32,6,64,128]{3,2,1,0:T(8,128)(2,1)} fusion(bf16[32,6,64,128]{3,2,1,0:T(8,128)(2,1)} %bitcast.70, f32[32,6]{1,0:T(8,128)S(1)} %copy-done.10, f32[32,4,6,64]{3,1,2,0:T(4,128)S(1)} %get-tuple-element.61, f32[32,4,6]{1,2,0:T(8,128)S(1)} %copy.259, f32[32,4,256]{2,1,0:T(4,128)S(1)} %divide_multiply_fusion.1), kind=kOutput, calls=%fused_computation.6 | convolution fusion | flops 81838080 | bytes 6897664 | tf_op jit(solution)/shard_map/rshp,rsn->rhpn/dot_general | solution.py:183
  156.5 22.8 %reduce-scatter.2.cloned.1.call-done = f32[16,1664]{1,0:T(8,128)} async-done(((f32[128,1664]{1,0:T(8,128)}), f32[16,1664]{1,0:T(8,128)}) %reduce-scatter.2.cloned.1.call-update) | async-done | bytes 106512 | tf_op jit(solution)/shard_map/reduce_scatter | solution.py:198
  179.3 0.9 fusion.56
  180.2 1.6 fusion.18
  (115 shorter events, 3.7 us)
Async XLA Ops:
  7.2 132.4 %copy-start = (bf16[384,1536]{1,0:T(8,128)(2,1)S(1)}, bf16[384,1536]{1,0:T(8,128)(2,1)}, u32[]{:S(2)}) copy-start(bf16[384,1536]{1,0:T(8,128)(2,1)} %param.32) | copy-start | bytes 3538948
  11.1 14.4 %copy-start.15 = (s32[1024]{0:T(1024)S(1)}, s32[1024]{0:T(1024)}, u32[]{:S(2)}) copy-start(s32[1024]{0:T(1024)} %param.39) | copy-start | bytes 12292
  11.1 19.8 %copy-start.23 = (s32[32]{0:T(128)S(1)}, s32[32]{0:T(128)}, u32[]{:S(2)}) copy-start(s32[32]{0:T(128)} %param.38) | copy-start | bytes 388
  11.1 22.4 %copy-start.8 = (bf16[16,1536]{1,0:T(8,128)(2,1)S(1)}, bf16[16,1536]{1,0:T(8,128)(2,1)}, u32[]{:S(2)}) copy-start(bf16[16,1536]{1,0:T(8,128)(2,1)} %param.20) | copy-start | bytes 147460
  13.4 1.7 copy-start.1
  17.9 17.7 %all-to-all-start = ((bf16[32,2,798]{2,1,0:T(2,128)(2,1)}), bf16[32,2,798]{2,1,0:T(2,128)(2,1)S(1)}, u32[]{:S(2)}, u32[]{:S(2)}) async-start(bf16[32,2,798]{2,1,0:T(2,128)(2,1)} %reshape.423), calls=%async_computation | async-start | bytes 229376 | tf_op jit(solution)/shard_map/all_to_all | solution.py:50
  38.0 13.9 %all-to-all-start.1 = ((bf16[32,2,798]{2,1,0:T(2,128)(2,1)}), bf16[32,2,798]{2,1,0:T(2,128)(2,1)S(1)}, u32[]{:S(2)}, u32[]{:S(2)}) async-start(bf16[32,2,798]{2,1,0:T(2,128)(2,1)} %reshape.425), calls=%async_computation.1 | async-start | bytes 229376 | tf_op jit(solution)/shard_map/all_to_all | solution.py:53
  56.8 6.0 %copy-start.13 = (f32[1536]{0:T(1024)S(1)}, f32[1536]{0:T(1024)}, u32[]{:S(2)}) copy-start(f32[1536]{0:T(1024)} %param.21) | copy-start | bytes 18436
  56.8 35.0 %copy-start.3 = (bf16[1536,304]{0,1:T(8,128)(2,1)S(1)}, bf16[1536,304]{0,1:T(8,128)(2,1)}, u32[]{:S(2)}) copy-start(bf16[1536,304]{0,1:T(8,128)(2,1)} %param.23) | copy-start | bytes 2801668
  56.8 47.2 %all-to-all-start.2 = ((bf16[32,399,128]{2,1,0:T(8,128)(2,1)}), bf16[32,399,128]{2,1,0:T(8,128)(2,1)}, u32[]{:S(2)}, u32[]{:S(2)}) async-start(bf16[32,399,128]{2,1,0:T(8,128)(2,1)} %broadcast_select_fusion), calls=%async_computation.2 | async-start | bytes 6553600 | tf_op jit(solution)/shard_map/all_to_all | solution.py:131
  62.8 116.5 %reduce-scatter.2.cloned.1.call-start = ((), (), s32[]{:S(2)}) async-start(), calls=%async_computation.4 | async-start | bytes 958464 | tf_op jit(solution)/shard_map/reduce_scatter | solution.py:198
  92.4 3.0 %copy-start.21 = (s32[32]{0:T(128)S(1)}, s32[32]{0:T(128)}, u32[]{:S(2)}) copy-start(s32[32]{0:T(128)} %param.36) | copy-start | bytes 388
  92.5 3.0 %copy-start.24 = (f32[6]{0:T(128)S(1)}, f32[6]{0:T(128)}, u32[]{:S(2)}) copy-start(f32[6]{0:T(128)} %param.29) | copy-start | bytes 76
  92.5 3.0 %copy-start.20 = (f32[6]{0:T(128)S(1)}, f32[6]{0:T(128)}, u32[]{:S(2)}) copy-start(f32[6]{0:T(128)} %param.28) | copy-start | bytes 76
  92.5 5.5 %copy-start.14 = (f32[4,384]{1,0:T(4,128)S(1)}, f32[4,384]{1,0:T(4,128)}, u32[]{:S(2)}) copy-start(f32[4,384]{1,0:T(4,128)} %param.24) | copy-start | bytes 18436
  92.5 5.6 %copy-start.16 = (f32[4,256]{1,0:T(4,128)S(1)}, f32[4,256]{1,0:T(4,128)}, u32[]{:S(2)}) copy-start(f32[4,256]{1,0:T(4,128)} %param.26) | copy-start | bytes 12292
  95.4 13.2 %copy-start.18 = (pred[32,4]{0,1:T(4,128)(4,1)}, pred[32,4]{0,1:T(4,128)(4,1)S(1)}, u32[]{:S(2)}) copy-start(pred[32,4]{0,1:T(4,128)(4,1)S(1)} %iota_compare_fusion.1) | copy-start | bytes 388
  108.7 4.1 %copy-start.2 = (bf16[32,399,128]{2,1,0:T(8,128)(2,1)S(1)}, bf16[32,399,128]{2,1,0:T(8,128)(2,1)}, u32[]{:S(2)}) copy-start(bf16[32,399,128]{2,1,0:T(8,128)(2,1)} %gather_fusion.2) | copy-start | bytes 9805828
  108.7 4.1 %slice-start = ((bf16[32,399,128]{2,1,0:T(8,128)(2,1)}), bf16[32,9,128]{2,1,0:T(8,128)(2,1)S(1)}, s32[]{:S(2)}) async-start(bf16[32,399,128]{2,1,0:T(8,128)(2,1)} %gather_fusion.2), calls=%async_computation.5 | async-start | bytes 262144 | tf_op jit(solution)/shard_map/slice | solution.py:134
  108.7 4.3 %copy-start.17 = (f32[384]{0:T(512)S(1)}, f32[384]{0:T(512)}, u32[]{:S(2)}) copy-start(f32[384]{0:T(512)} %param.25) | copy-start | bytes 4612
  112.7 0.7 copy-start.19
  112.8 10.4 %copy-start.4 = (bf16[32,3,384]{2,1,0:T(4,128)(2,1)}, bf16[32,3,384]{2,1,0:T(4,128)(2,1)S(1)}, u32[]{:S(2)}) copy-start(bf16[32,3,384]{2,1,0:T(4,128)(2,1)S(1)} %reshape.335) | copy-start | bytes 221188
  113.2 14.3 %copy-start.6 = (bf16[32,3,256]{2,1,0:T(4,128)(2,1)}, bf16[32,3,256]{2,1,0:T(4,128)(2,1)S(1)}, u32[]{:S(2)}) copy-start(bf16[32,3,256]{2,1,0:T(4,128)(2,1)S(1)} %reshape.333) | copy-start | bytes 147460
  137.9 3.3 %copy-start.11 = (f32[32,1,6]{0,1,2:T(1,128)S(1)}, f32[32,1,6]{0,1,2:T(1,128)}, u32[]{:S(2)}) copy-start(f32[32,1,6]{0,1,2:T(1,128)} %get-tuple-element.54) | copy-start | bytes 2308
  137.9 3.3 %copy-start.12 = (f32[32,1,6]{0,1,2:T(1,128)S(1)}, f32[32,1,6]{0,1,2:T(1,128)}, u32[]{:S(2)}) copy-start(f32[32,1,6]{0,1,2:T(1,128)} %get-tuple-element.55) | copy-start | bytes 2308
  137.9 3.5 %copy-start.22 = (s32[32]{0:T(128)S(1)}, s32[32]{0:T(128)}, u32[]{:S(2)}) copy-start(s32[32]{0:T(128)} %param.36) | copy-start | bytes 388
  138.2 3.3 %copy-start.7 = (bf16[32,3,256]{2,1,0:T(4,128)(2,1)S(1)}, bf16[32,3,256]{2,1,0:T(4,128)(2,1)}, u32[]{:S(2)}) copy-start(bf16[32,3,256]{2,1,0:T(4,128)(2,1)} %copy-done.6) | copy-start | bytes 147460
  139.2 3.2 %copy-start.5 = (bf16[32,3,384]{2,1,0:T(4,128)(2,1)S(1)}, bf16[32,3,384]{2,1,0:T(4,128)(2,1)}, u32[]{:S(2)}) copy-start(bf16[32,3,384]{2,1,0:T(4,128)(2,1)} %copy-done.4) | copy-start | bytes 221188
  139.5 3.6 %copy-start.10 = (f32[32,6]{1,0:T(8,128)S(1)}, f32[32,6]{1,0:T(8,128)}, u32[]{:S(2)}) copy-start(f32[32,6]{1,0:T(8,128)} %copy.250) | copy-start | bytes 2308
  143.1 37.1 %copy-start.9 = (bf16[16,1536]{1,0:T(8,128)(2,1)S(1)}, bf16[16,1536]{1,0:T(8,128)(2,1)}, u32[]{:S(2)}) copy-start(bf16[16,1536]{1,0:T(8,128)(2,1)} %param.20) | copy-start | bytes 147460
Sparse Core Ops, SparseCore 0:
  141.2 38.0 reduce-scatter.1

commit v2 on v1

--- a/solution.py
+++ b/solution.py
@@ -1,7 +1,11 @@
+import functools
+
 import jax
 import jax.numpy as jnp
 from jax import lax
 from jax.sharding import PartitionSpec as P
+from jax.experimental import pallas as pl
+from jax.experimental.pallas import tpu as pltpu
 
 EPS = 1e-05
 HIGH = lax.Precision.HIGHEST
@@ -34,13 +38,66 @@
     return partner * capacity + ranking
 
 
+def invert(values, size):
+    hits = values[None, :] == jnp.arange(size, dtype=jnp.int32)[:, None]
+    return jnp.sum(jnp.where(hits, jnp.arange(values.shape[0], dtype=jnp.int32)[None, :], 0), axis=1)
+
+
 def route_rows(anchor, first_slot, slot_count, all_slots, capacity):
-    inverse = jnp.zeros(all_slots.shape, jnp.int32).at[anchor].set(all_slots)
-    targets = lax.dynamic_slice_in_dim(inverse, first_slot, slot_count)
+    mine = first_slot + jnp.arange(slot_count, dtype=jnp.int32)
+    hits = anchor[None, :] == mine[:, None]
+    targets = jnp.sum(jnp.where(hits, all_slots[None, :], 0), axis=1)
     send_rows = rank_rows(targets // slot_count, targets % slot_count, capacity)
     sources = lax.dynamic_slice_in_dim(anchor, first_slot, slot_count)
     recv_rows = rank_rows(sources // slot_count, jnp.arange(slot_count, dtype=jnp.int32), capacity)
     return (send_rows, recv_rows)
+
+
+def recurrence_kernel(rows_ref, *refs, group, window):
+    held_refs = refs[:group]
+    mix_ref, weight_ref, read_ref, out_ref = refs[group:]
+    for q in range(group):
+        held = held_refs[q][0].astype(jnp.float32)
+        mix = mix_ref[q]
+        read_ref[q] = lax.dot_general(
+            mix, held, (((1,), (1,)), ((), ())), precision=HIGH,
+            preferred_element_type=jnp.float32,
+        )
+        weight = weight_ref[q]
+        acc = weight[:, window : window + 1] * held
+        for s in range(window):
+            acc = acc + weight[:, s : s + 1] * mix[window + s : window + s + 1, :]
+        out_ref[q] = acc.astype(out_ref.dtype)
+
+
+def recurrence(received, rows, mix, weight, state_rows, group=4):
+    slot_count, _, lanes = received.shape
+    window = mix.shape[1] // 2
+    held_specs = [
+        pl.BlockSpec((1, state_rows, lanes), lambda i, r, q=q: (r[i * group + q], 0, 0))
+        for q in range(group)
+    ]
+    grid_spec = pltpu.PrefetchScalarGridSpec(
+        num_scalar_prefetch=1,
+        grid=(slot_count // group,),
+        in_specs=held_specs
+        + [
+            pl.BlockSpec((group, 2 * window, lanes), lambda i, r: (i, 0, 0)),
+            pl.BlockSpec((group, state_rows, 2 * window), lambda i, r: (i, 0, 0)),
+        ],
+        out_specs=[
+            pl.BlockSpec((group, 2 * window, state_rows), lambda i, r: (i, 0, 0)),
+            pl.BlockSpec((group, state_rows, lanes), lambda i, r: (i, 0, 0)),
+        ],
+    )
+    return pl.pallas_call(
+        functools.partial(recurrence_kernel, group=group, window=window),
+        grid_spec=grid_spec,
+        out_shape=[
+            jax.ShapeDtypeStruct((slot_count, 2 * window, state_rows), jnp.float32),
+            jax.ShapeDtypeStruct((slot_count, state_rows, lanes), jnp.bfloat16),
+        ],
+    )(rows, *([received] * group), mix, weight)
 
 
 def migrate(item, mig_dest, slot_count, groups, device):
@@ -49,7 +106,7 @@
     padded = jnp.pad(item, (0, piece * groups - length)).reshape(groups, piece)
     first = lax.all_to_all(padded, "req", 0, 0, tiled=True)
     dest_dev = mig_dest // slot_count
-    order = jnp.zeros((groups,), jnp.int32).at[dest_dev].set(jnp.arange(groups, dtype=jnp.int32))
+    order = invert(dest_dev, groups)
     second = lax.all_to_all(first[order], "req", 0, 0, tiled=True)
     arrived = second.reshape(-1)[:length]
     target_local = mig_dest[order[device]] - device * slot_count
@@ -122,17 +179,14 @@
 
     send_rows, recv_rows = route_rows(reorder, first_slot, slot_count, all_slots, stride)
     buffer_rows = groups * stride
-    send_idx = (
-        jnp.zeros((buffer_rows,), jnp.int32).at[send_rows].set(jnp.arange(slot_count, dtype=jnp.int32))
-    )
+    send_idx = invert(send_rows, buffer_rows)
     send_buf = jnp.where(
         (send_idx == target_local)[:, None, None], arrived[None], packed[send_idx]
     )
     received = lax.all_to_all(send_buf, "req", 0, 0, tiled=True)
-    moved = received[recv_rows]
-    moved_states = moved[:, :state_rows].reshape(slot_count, heads_here, head_dim, state_dim)
-    moved_inner = moved[:, state_rows : state_rows + inner_edge_rows].reshape(edge_inner.shape)
-    moved_shared = moved[:, state_rows + inner_edge_rows :].reshape(edge_shared.shape)
+    moved = received[:, state_rows:][recv_rows]
+    moved_inner = moved[:, :inner_edge_rows].reshape(edge_inner.shape)
+    moved_shared = moved[:, inner_edge_rows:].reshape(edge_shared.shape)
 
     window = inner_rows.shape[0] // slot_count
     inner_rows = inner_rows.reshape(slot_count, window, 2 * inner_here)
@@ -166,10 +220,25 @@
         span[(t, t)] = jnp.ones_like(factor[:, 0])
         for s in range(t - 1, -1, -1):
             span[(t, s)] = span[(t, s + 1)] * factor[:, s + 1]
-    held = moved_states.astype(jnp.float32)
-    from_state = jnp.einsum("rhpn,rtn->rthp", held, readouts, precision=HIGH)
+    weighted = step_size[:, :, :, None] * inputs
+    last = window - 1
+    pushed = jnp.stack([span[(last, s)] for s in range(window)], axis=1)[:, :, :, None] * weighted
+    carry = jnp.broadcast_to(
+        cumulative[:, last, :, None], (slot_count, heads_here, head_dim)
+    ).reshape(slot_count, 1, inner_here)
+    weight = jnp.concatenate(
+        [
+            pushed.reshape(slot_count, window, inner_here),
+            carry,
+            jnp.zeros((slot_count, window - 1, inner_here), jnp.float32),
+        ],
+        axis=1,
+    ).transpose(0, 2, 1)
+    mix = jnp.concatenate([readouts, entries], axis=1)
+    read, states_out = recurrence(received, recv_rows, mix, weight, state_rows)
+    states_out = states_out.reshape(states.shape)
+    from_state = read[:, :window].reshape(slot_count, window, heads_here, head_dim)
     overlap = jnp.einsum("rtn,rsn->rts", readouts, entries, precision=HIGH)
-    weighted = step_size[:, :, :, None] * inputs
     produced = []
     for t in range(window):
         acc = cumulative[:, t, :, None] * from_state[:, t]
@@ -178,11 +247,6 @@
             acc = acc + coef[:, :, None] * weighted[:, s]
         produced.append(acc + skip_gain[None, :, None] * inputs[:, t])
     outputs = jnp.stack(produced, axis=1)
-    last = window - 1
-    pushed = jnp.stack([span[(last, s)] for s in range(window)], axis=1)[:, :, :, None] * weighted
-    update = jnp.einsum("rshp,rsn->rhpn", pushed, entries, precision=HIGH)
-    final = cumulative[:, last, :, None, None] * held + update
-    states_out = final.astype(jnp.bfloat16)
 
     outputs = outputs.reshape(slot_count, window, inner_here)
     gated = outputs * jax.nn.silu(gate_part.astype(jnp.float32))

time: 190 us -> 255 us (1.34)
  other arithmetic: 23.6 us -> 66.9 us
  local copies, waits for them, and re-layouts: 42.9 us -> 76.8 us
  matrix products: 24.2 us -> 1.58 us
  Pallas kernels: 0 us -> 13 us
    dot_general x2 -> x0, matrix products: 22.6 us -> none  [the longest x1 13.4 us: local(): update = jnp.einsum('rshp,rsn->rhpn', pushed, entries, precision=HIGH)]
    select_n x2, other arithmetic: 1 us -> 17.1 us  [new_edge(): jnp.where((counts == length)[:, None, None], sequence[:, length:length +...]
    reduce_scatter x1, waiting for transfers between devices: 22.8 us -> 7.59 us  [local(): lax.psum_scatter(combined, 'head', scatter_dimension=0, tiled=True)]
    pallas_call x0 -> x1, Pallas kernels: none -> 13 us  [recurrence(): pl.pallas_call(functools.partial(recurrence_kernel, group=group, window=w...]
    all_to_all x1, waiting for transfers between devices: 5.27 us -> 18 us  [local(): received = lax.all_to_all(send_buf, 'req', 0, 0, tiled=True)]
    unnamed x61 -> x49, local copies, waits for them, and re-layouts: 8.57 us -> 21.1 us
    reshape x2 -> x5, local copies, waits for them, and re-layouts: 0.12 us -> 11.2 us  [the longest x1 8.04 us: local(): carry = jnp.broadcast_to(cumulative[:, last, :, None], (slot_count, heads...]
    transpose x0 -> x1, other arithmetic: none -> 8.95 us  [local(): weight = jnp.concatenate([pushed.reshape(slot_count, window, inner_here),...]
  transfers between devices with their start and end apart: 4 -> 4, of which waited for: 3 -> 3; matrix products, arithmetic and copies ran while one was open for 18% -> 23% of each run, Pallas kernels for 0% -> 0%
where the time goes in v2:
time: 255 us; the launch traced here: 253 us
  local copies, waits for them, and re-layouts  76.8 us (30%)
  other arithmetic  66.9 us (26%)
  blocking collectives  28.6 us (11%)
  waiting for transfers between devices  27.5 us (11%)
  starting transfers between devices  21 us (8%)
  between operations  17.9 us (7%)
  Pallas kernels  13 us (5%)
    all_gather x1, blocking collectives, local(): piece_rows = lax.all_gather(normed, 'head', axis=0, tiled=True)  28.6 us
    unnamed x49, local copies, waits for them, and re-layouts  21.1 us
    all_to_all x1, waiting for transfers between devices, local(): received = lax.all_to_all(send_buf, 'req', 0, 0, tiled=True)  18 us
    select_n x2, other arithmetic, new_edge(): jnp.where((counts == length)[:, None, None], sequence[:, length:length +...  17.1 us
    pallas_call x1, Pallas kernels, recurrence(): pl.pallas_call(functools.partial(recurrence_kernel, group=group, window=w...  13 us
    transpose x1, other arithmetic, local(): weight = jnp.concatenate([pushed.reshape(slot_count, window, inner_here),...  8.95 us
    reshape x1, local copies, waits for them, and re-layouts, local(): carry = jnp.broadcast_to(cumulative[:, last, :, None], (slot_count, heads...  8.04 us
    mul x1, other arithmetic, local(): jnp.stack([span[last, s] for s in range(window)], axis=1)[:, :, :, None]  7.71 us
  transfers between devices with their start and end apart: 4, of which 3 were waited for; matrix products, arithmetic and copies ran while one was open for 23% of the time, Pallas kernels for 0%

profile of v2, /device:TPU:2, one launch (start us, length us, event | category | flops | bytes accessed | tf_op | source)
XLA Modules:
  0.0 253.4 jit_solution(12835606000955185665)
XLA Ops:
  7.3 1.4 dynamic_slice.23
  9.3 0.8 copy.215
  10.2 0.9 copy.214
  11.2 2.2 pad_maximum_fusion
  13.5 1.7 copy-done.1
  15.9 1.3 reduce.31
  17.2 0.8 reshape.470
  18.0 7.6 %all-to-all-start = ((bf16[32,2,798]{2,1,0:T(2,128)(2,1)}), bf16[32,2,798]{2,1,0:T(2,128)(2,1)S(1)}, u32[]{:S(2)}, u32[]{:S(2)}) async-start(bf16[32,2,798]{2,1,0:T(2,128)(2,1)} %reshape.470), calls=%async_computation | async-start | bytes 229376 | tf_op jit(solution)/shard_map/all_to_all | solution.py:107
  28.1 28.6 %all_gather.3 = bf16[128,1536]{1,0:T(8,128)(2,1)S(1)} all-gather(bf16[16,1536]{1,0:T(8,128)(2,1)S(1)} %fusion.30), channel_id=1, replica_groups=mesh['req'=32,'head'=8] {'head'}, dimensions={0}, use_global_device_ids=true | all-gather | bytes 442368 | tf_op jit(solution)/shard_map/all_gather | solution.py:152
  57.9 0.7 copy.222
  61.4 0.7 gather_fusion
  62.1 0.7 reduce.32
  62.7 0.8 reshape.472
  63.6 7.4 %all-to-all-start.1 = ((bf16[32,2,798]{2,1,0:T(2,128)(2,1)}), bf16[32,2,798]{2,1,0:T(2,128)(2,1)S(1)}, u32[]{:S(2)}, u32[]{:S(2)}) async-start(bf16[32,2,798]{2,1,0:T(2,128)(2,1)} %reshape.472), calls=%async_computation.1 | async-start | bytes 229376 | tf_op jit(solution)/shard_map/all_to_all | solution.py:110
  71.0 4.6 %gather_fusion.1 = bf16[32,399,128]{2,1,0:T(8,128)(2,1)} fusion(bf16[32,399,128]{2,1,0:T(8,128)(2,1)} %copy-done.1, s32[1024]{0:T(1024)S(1)} %pad_clamp_fusion.1), kind=kCustom, calls=%fused_computation.1 | custom fusion | bytes 6537344 | tf_op jit(solution)/shard_map/gather | solution.py:184
  75.6 1.9 all-to-all-done.1
  77.6 0.7 reduce
  78.5 4.0 %broadcast_select_fusion = bf16[32,399,128]{2,1,0:T(8,128)(2,1)} fusion(bf16[32,399,128]{2,1,0:T(8,128)(2,1)} %gather_fusion.1, pred[32]{0:T(512)(128)(4,1)S(1)} %broadcast_compare_fusion.3, bf16[399,128]{1,0:T(8,128)(2,1)S(1)} %broadcast_in_dim.193), kind=kLoop, calls=%fused_computation.17 | loop fusion | flops 1634304 | bytes 6639392 | tf_op jit(solution)/shard_map/jit(_where)/select_n | solution.py:183
  82.5 5.8 %all-to-all-start.2 = ((bf16[32,399,128]{2,1,0:T(8,128)(2,1)}), bf16[32,399,128]{2,1,0:T(8,128)(2,1)}, u32[]{:S(2)}, u32[]{:S(2)}) async-start(bf16[32,399,128]{2,1,0:T(8,128)(2,1)} %broadcast_select_fusion), calls=%async_computation.2 | async-start | bytes 6553600 | tf_op jit(solution)/shard_map/all_to_all | solution.py:186
  88.6 0.7 copy.270
  89.5 2.1 copy.273
  92.2 2.8 %copy.263 = bf16[32,4,384]{1,2,0:T(8,128)(2,1)} copy(bf16[32,4,384]{2,1,0:T(4,128)(2,1)S(1)} %get-tuple-element.71) | data formatting | bytes 196608
  95.1 4.0 %copy.242 = f32[32,4,384]{1,2,0:T(8,128)} copy(f32[32,4,384]{2,0,1:T(8,128)S(1)} %copy_convert_fusion) | data formatting | bytes 393216 | tf_op jit(solution)/shard_map/convert_element_type | solution.py:252
  99.0 7.1 %add_divide_fusion = f32[32,4,384]{1,2,0:T(8,128)} fusion(f32[32,4,384]{1,2,0:T(8,128)} %copy.242), kind=kLoop, calls=%fused_computation.14 | loop fusion | flops 147456 | bytes 393216 | tf_op jit(solution)/shard_map/jit(silu)/div | solution.py:252
  106.1 4.5 %copy.243 = f32[32,4,384]{2,0,1:T(8,128)S(1)} copy(f32[32,4,384]{1,2,0:T(8,128)} %add_divide_fusion) | data formatting | bytes 393216 | tf_op jit(solution)/shard_map/jit(silu)/div | solution.py:252
  110.9 0.6 compare_select_fusion.1
  111.6 18.0 %all-to-all-done.2.refs_0_.refs_1_.refs_2_.refs_3_ = bf16[32,399,128]{2,1,0:T(8,128)(2,1)} async-done(((bf16[32,399,128]{2,1,0:T(8,128)(2,1)}), bf16[32,399,128]{2,1,0:T(8,128)(2,1)}, u32[]{:S(2)}, u32[]{:S(2)}) %all-to-all-start.2) | async-done | bytes 3268640 | tf_op jit(solution)/shard_map/all_to_all | solution.py:186
  129.6 0.9 slice.272
  131.9 1.5 slice_reduce_fusion.9
  133.6 0.7 copy.232
  134.3 0.7 copy.238
  135.0 0.7 copy.235
  135.7 0.7 copy.239
  136.4 0.7 copy.236
  137.0 0.7 copy.240
  137.7 0.7 copy.233
  138.4 2.9 %copy.224 = bf16[32,3,384]{1,2,0:T(8,128)(2,1)} copy(bf16[32,3,384]{2,1,0:T(4,128)(2,1)S(1)} %reshape.419) | data formatting | bytes 147456 | tf_op jit(solution)/shard_map/reshape | solution.py:188
  141.3 4.4 %fusion.8 = f32[32,7,384]{1,2,0:T(8,128)S(1)} fusion(bf16[32,3,384]{1,2,0:T(8,128)(2,1)} %copy.224, bf16[32,4,384]{1,2,0:T(8,128)(2,1)} %copy.263), kind=kLoop, calls=%fused_computation.23 | loop fusion | flops 344064 | bytes 516096 | tf_op jit(solution)/shard_map/convert_element_type | solution.py:15
  145.7 7.7 %fusion.4 = (f32[32,4,384]{1,2,0:T(8,128)}, f32[32,4,384]{1,2,0:T(8,128)}) fusion(f32[32,4,6]{1,2,0:T(8,128)S(1)} %copy.269, f32[32,4,6]{1,2,0:T(8,128)S(1)} %copy.268, f32[384]{0:T(512)S(1)} %copy-done.9, f32[384]{0:T(512)S(1)} %get-tuple-element.52, f32[32,7,384]{1,2,0:T(8,128)S(1)} %fusion.8, f32[384]{0:T(512)S(1)} %get-tuple-element.53, ...), kind=kLoop, calls=%fused_computation.13 | loop fusion | flops 688128 | bytes 1193472 | tf_op jit(solution)/shard_map/mul | solution.py:225
  153.4 5.1 %copy.255 = f32[32,4,6,64]{3,2,0,1:T(8,128)S(1)} copy(f32[32,4,6,64]{1,3,2,0:T(8,128)} %bitcast.96) | data formatting | bytes 393216 | tf_op jit(solution)/shard_map/reshape | solution.py:209
  158.6 8.0 %reshape.452 = f32[32,1,384]{1,2,0:T(8,128)} reshape(f32[32,6,64]{2,1,0:T(8,128)S(1)} %broadcast_in_dim.196) | data formatting | bytes 98304 | tf_op jit(solution)/shard_map/reshape | solution.py:228
  166.7 0.7 pad_maximum_fusion.4.refs_4_
  167.3 9.0 %maximum_bitcast_fusion.refs_5_ = f32[32,384,8]{2,1,0:T(8,128)} fusion(f32[32,1,384]{1,2,0:T(8,128)} %reshape.452, f32[32,4,384]{1,2,0:T(8,128)} %get-tuple-element.54, f32[8]{0:T(128)S(1)} %pad.8.clone), kind=kLoop, calls=%fused_computation.11 | loop fusion | flops 196608 | bytes 639008 | tf_op jit(solution)/shard_map/transpose | solution.py:236
  176.3 13.0 %shard_map.219 = (f32[32,8,384]{2,1,0:T(8,128)}, bf16[32,384,128]{2,1,0:T(8,128)(2,1)}) custom-call(s32[32]{0:T(128)} %get-tuple-element.64.rows_ref, bf16[32,399,128]{2,1,0:T(8,128)(2,1)} %all-to-all-done.2.refs_0_.refs_1_.refs_2_.refs_3_, bf16[32,399,128]{2,1,0:T(8,128)(2,1)} %all-to-all-done.2.refs_0_.refs_1_.refs_2_.refs_3_, ...), custom_call_target="tpu_custom_call" | custom-call | tf_op jit(solution)/shard_map/pallas_call | solution.py:93
  189.3 1.0 slice.230
  190.5 1.0 broadcast_multiply_fusion
  191.5 1.8 fusion.22
  193.3 1.6 stack.21
  194.9 1.8 fusion.19
  196.7 1.0 stack.22
  197.7 1.0 stack.23
  198.7 1.0 stack.24
  199.7 0.9 multiply_reduce_fusion
  200.6 0.9 multiply_select_fusion
  201.7 2.8 %copy.245 = bf16[32,4,384]{1,2,0:T(8,128)(2,1)} copy(bf16[32,4,384]{2,0,1:T(8,128)(2,1)S(1)} %multiply_select_fusion) | data formatting | bytes 196608 | tf_op jit(solution)/shard_map/jit(_where)/select_n | solution.py:255
  204.5 3.3 %copy.246 = bf16[32,4,384]{2,1,0:T(4,128)(2,1)S(1)} copy(bf16[32,4,384]{1,2,0:T(8,128)(2,1)} %copy.245) | data formatting | bytes 196608 | tf_op jit(solution)/shard_map/convert_element_type | solution.py:256
  208.3 1.0 pad_maximum_fusion.2
  209.3 2.8 %copy.266 = bf16[32,3,384]{1,2,0:T(8,128)(2,1)} copy(bf16[32,3,384]{2,1,0:T(4,128)(2,1)S(1)} %get-tuple-element.69) | data formatting | bytes 147456
  212.1 2.8 %copy.265 = bf16[32,3,384]{1,2,0:T(8,128)(2,1)} copy(bf16[32,3,384]{2,1,0:T(4,128)(2,1)S(1)} %get-tuple-element.70) | data formatting | bytes 147456
  215.9 16.8 %fusion.7 = bf16[32,3,384]{1,2,0:T(8,128)(2,1)} fusion(bf16[32,3,384]{1,2,0:T(8,128)(2,1)} %copy.265, bf16[32,3,384]{1,2,0:T(8,128)(2,1)} %copy.266, bf16[32,3,384]{1,2,0:T(8,128)(2,1)} %copy.224, pred[32]{0:T(512)(128)(4,1)S(1)} %get-tuple-element.92, pred[32]{0:T(512)(128)(4,1)S(1)} %get-tuple-element.93, pred[32]{0:T(512)(128)(4,1)S(1)} %get-tuple-element.91, ...), kind=kLoop, calls=%fused_computation.21 | loop fusion | flops 442368 | bytes 393344 | tf_op jit(solution)/shard_map/jit(_where)/select_n | solution.py:28
  232.7 3.9 %copy.251 = bf16[32,3,384]{2,0,1:T(8,128)(2,1)} copy(bf16[32,3,384]{1,2,0:T(8,128)(2,1)} %fusion.7) | data formatting | bytes 147456
  236.5 7.6 %reduce-scatter.2.cloned.1.call-done = f32[16,1664]{1,0:T(8,128)} async-done(((f32[128,1664]{1,0:T(8,128)}), f32[16,1664]{1,0:T(8,128)}) %reduce-scatter.2.cloned.1.call-update) | async-done | bytes 106512 | tf_op jit(solution)/shard_map/reduce_scatter | solution.py:262
  244.1 0.9 fusion.42
  245.0 1.6 fusion.31
  (111 shorter events, 9.6 us)
Async XLA Ops:
  7.2 200.6 %copy-start = (bf16[384,1536]{1,0:T(8,128)(2,1)S(1)}, bf16[384,1536]{1,0:T(8,128)(2,1)}, u32[]{:S(2)}) copy-start(bf16[384,1536]{1,0:T(8,128)(2,1)} %param.32) | copy-start | bytes 3538948
  7.2 18.4 %copy-start.6 = (s32[1024]{0:T(1024)S(1)}, s32[1024]{0:T(1024)}, u32[]{:S(2)}) copy-start(s32[1024]{0:T(1024)} %param.39) | copy-start | bytes 12292
  7.2 18.6 %copy-start.14 = (s32[32]{0:T(128)S(1)}, s32[32]{0:T(128)}, u32[]{:S(2)}) copy-start(s32[32]{0:T(128)} %param.38) | copy-start | bytes 388
  7.2 20.7 %copy-start.3 = (bf16[16,1536]{1,0:T(8,128)(2,1)S(1)}, bf16[16,1536]{1,0:T(8,128)(2,1)}, u32[]{:S(2)}) copy-start(bf16[16,1536]{1,0:T(8,128)(2,1)} %param.20) | copy-start | bytes 147460
  7.2 20.8 %copy-start.4 = (f32[1536]{0:T(1024)S(1)}, f32[1536]{0:T(1024)}, u32[]{:S(2)}) copy-start(f32[1536]{0:T(1024)} %param.21) | copy-start | bytes 18436
  7.2 49.5 %copy-start.2 = (bf16[1536,304]{0,1:T(8,128)(2,1)S(1)}, bf16[1536,304]{0,1:T(8,128)(2,1)}, u32[]{:S(2)}) copy-start(bf16[1536,304]{0,1:T(8,128)(2,1)} %param.23) | copy-start | bytes 2801668
  7.2 50.1 %copy-start.15 = (f32[6]{0:T(128)S(1)}, f32[6]{0:T(128)}, u32[]{:S(2)}) copy-start(f32[6]{0:T(128)} %param.29) | copy-start | bytes 76
  7.2 50.2 %copy-start.10 = (s32[32]{0:T(128)S(1)}, s32[32]{0:T(128)}, u32[]{:S(2)}) copy-start(s32[32]{0:T(128)} %param.36) | copy-start | bytes 388
  7.3 50.5 %copy-start.13 = (f32[6]{0:T(128)S(1)}, f32[6]{0:T(128)}, u32[]{:S(2)}) copy-start(f32[6]{0:T(128)} %param.28) | copy-start | bytes 76
  13.5 1.7 copy-start.1
  18.0 43.2 %all-to-all-start = ((bf16[32,2,798]{2,1,0:T(2,128)(2,1)}), bf16[32,2,798]{2,1,0:T(2,128)(2,1)S(1)}, u32[]{:S(2)}, u32[]{:S(2)}) async-start(bf16[32,2,798]{2,1,0:T(2,128)(2,1)} %reshape.470), calls=%async_computation | async-start | bytes 229376 | tf_op jit(solution)/shard_map/all_to_all | solution.py:107
  57.6 3.6 %copy-start.7 = (pred[32,4]{0,1:T(4,128)(4,1)}, pred[32,4]{0,1:T(4,128)(4,1)S(1)}, u32[]{:S(2)}) copy-start(pred[32,4]{0,1:T(4,128)(4,1)S(1)} %copy.267) | copy-start | bytes 388
  63.6 13.9 %all-to-all-start.1 = ((bf16[32,2,798]{2,1,0:T(2,128)(2,1)}), bf16[32,2,798]{2,1,0:T(2,128)(2,1)S(1)}, u32[]{:S(2)}, u32[]{:S(2)}) async-start(bf16[32,2,798]{2,1,0:T(2,128)(2,1)} %reshape.472), calls=%async_computation.1 | async-start | bytes 229376 | tf_op jit(solution)/shard_map/all_to_all | solution.py:110
  82.5 47.1 %all-to-all-start.2 = ((bf16[32,399,128]{2,1,0:T(8,128)(2,1)}), bf16[32,399,128]{2,1,0:T(8,128)(2,1)}, u32[]{:S(2)}, u32[]{:S(2)}) async-start(bf16[32,399,128]{2,1,0:T(8,128)(2,1)} %broadcast_select_fusion), calls=%async_computation.2 | async-start | bytes 6553600 | tf_op jit(solution)/shard_map/all_to_all | solution.py:186
  88.3 155.8 %reduce-scatter.2.cloned.1.call-start = ((), (), s32[]{:S(2)}) async-start(), calls=%async_computation.4 | async-start | bytes 958464 | tf_op jit(solution)/shard_map/reduce_scatter | solution.py:262
  106.1 5.4 %copy-start.5 = (f32[4,384]{1,0:T(4,128)S(1)}, f32[4,384]{1,0:T(4,128)}, u32[]{:S(2)}) copy-start(f32[4,384]{1,0:T(4,128)} %param.24) | copy-start | bytes 18436
  106.1 5.4 %copy-start.8 = (f32[4,256]{1,0:T(4,128)S(1)}, f32[4,256]{1,0:T(4,128)}, u32[]{:S(2)}) copy-start(f32[4,256]{1,0:T(4,128)} %param.26) | copy-start | bytes 12292
  106.1 25.1 %copy-start.12 = (f32[256]{0:T(256)S(1)}, f32[256]{0:T(256)}, u32[]{:S(2)}) copy-start(f32[256]{0:T(256)} %param.27) | copy-start | bytes 3076
  141.3 4.4 %copy-start.9 = (f32[384]{0:T(512)S(1)}, f32[384]{0:T(512)}, u32[]{:S(2)}) copy-start(f32[384]{0:T(512)} %param.25) | copy-start | bytes 4612
  207.8 7.2 %copy-start.11 = (s32[32]{0:T(128)S(1)}, s32[32]{0:T(128)}, u32[]{:S(2)}) copy-start(s32[32]{0:T(128)} %param.36) | copy-start | bytes 388
Sparse Core Ops, SparseCore 0:
  209.4 34.6 reduce-scatter.1

commit v3 on v2

--- a/solution.py
+++ b/solution.py
@@ -53,26 +53,32 @@
     return (send_rows, recv_rows)
 
 
-def recurrence_kernel(rows_ref, *refs, group, window):
+def recurrence_kernel(rows_ref, *refs, group, window, heads):
     held_refs = refs[:group]
     mix_ref, weight_ref, read_ref, out_ref = refs[group:]
     for q in range(group):
         held = held_refs[q][0].astype(jnp.float32)
         mix = mix_ref[q]
         read_ref[q] = lax.dot_general(
-            mix, held, (((1,), (1,)), ((), ())), precision=HIGH,
+            mix[: 2 * window], held, (((1,), (1,)), ((), ())), precision=HIGH,
             preferred_element_type=jnp.float32,
         )
-        weight = weight_ref[q]
-        acc = weight[:, window : window + 1] * held
-        for s in range(window):
-            acc = acc + weight[:, s : s + 1] * mix[window + s : window + s + 1, :]
-        out_ref[q] = acc.astype(out_ref.dtype)
-
-
-def recurrence(received, rows, mix, weight, state_rows, group=4):
+        pushed = lax.dot_general(
+            weight_ref[q], mix[window : 3 * window], (((0,), (0,)), ((), ())),
+            precision=HIGH, preferred_element_type=jnp.float32,
+        )
+        rows = held.shape[0] // heads
+        carry = mix[2 * window : 2 * window + 1]
+        for h in range(heads):
+            part = slice(h * rows, (h + 1) * rows)
+            out_ref[q, part] = (carry[:, h : h + 1] * held[part] + pushed[part]).astype(
+                out_ref.dtype
+            )
+
+
+def recurrence(received, rows, mix, weight, state_rows, heads, group=4):
     slot_count, _, lanes = received.shape
-    window = mix.shape[1] // 2
+    window = mix.shape[1] // 4
     held_specs = [
         pl.BlockSpec((1, state_rows, lanes), lambda i, r, q=q: (r[i * group + q], 0, 0))
         for q in range(group)
@@ -82,8 +88,8 @@
         grid=(slot_count // group,),
         in_specs=held_specs
         + [
-            pl.BlockSpec((group, 2 * window, lanes), lambda i, r: (i, 0, 0)),
-            pl.BlockSpec((group, state_rows, 2 * window), lambda i, r: (i, 0, 0)),
+            pl.BlockSpec((group, 4 * window, lanes), lambda i, r: (i, 0, 0)),
+            pl.BlockSpec((group, 2 * window, state_rows), lambda i, r: (i, 0, 0)),
         ],
         out_specs=[
             pl.BlockSpec((group, 2 * window, state_rows), lambda i, r: (i, 0, 0)),
@@ -91,7 +97,7 @@
         ],
     )
     return pl.pallas_call(
-        functools.partial(recurrence_kernel, group=group, window=window),
+        functools.partial(recurrence_kernel, group=group, window=window, heads=heads),
         grid_spec=grid_spec,
         out_shape=[
             jax.ShapeDtypeStruct((slot_count, 2 * window, state_rows), jnp.float32),
@@ -206,7 +212,6 @@
     step_size = jax.nn.softplus(step_raw.astype(jnp.float32) + step_bias)
     step_size = jnp.where(valid[:, :, None], step_size, 0.0)
     decay = -jnp.exp(decay_log)
-    inputs = mixed_inner.reshape(slot_count, window, heads_here, head_dim)
     entries = mixed_shared[:, :, :state_dim]
     readouts = mixed_shared[:, :, state_dim:]
 
@@ -214,41 +219,37 @@
     cum = [factor[:, 0]]
     for t in range(1, window):
         cum.append(cum[-1] * factor[:, t])
-    cumulative = jnp.stack(cum, axis=1)
     span = {}
     for t in range(window):
         span[(t, t)] = jnp.ones_like(factor[:, 0])
         for s in range(t - 1, -1, -1):
             span[(t, s)] = span[(t, s + 1)] * factor[:, s + 1]
-    weighted = step_size[:, :, :, None] * inputs
+
+    def per_head(v):
+        return jnp.repeat(v, head_dim, axis=-1)
+
+    flat_inputs = mixed_inner.reshape(slot_count, window, inner_here)
+    weighted = per_head(step_size) * flat_inputs
     last = window - 1
-    pushed = jnp.stack([span[(last, s)] for s in range(window)], axis=1)[:, :, :, None] * weighted
-    carry = jnp.broadcast_to(
-        cumulative[:, last, :, None], (slot_count, heads_here, head_dim)
-    ).reshape(slot_count, 1, inner_here)
-    weight = jnp.concatenate(
-        [
-            pushed.reshape(slot_count, window, inner_here),
-            carry,
-            jnp.zeros((slot_count, window - 1, inner_here), jnp.float32),
-        ],
+    pushed = jnp.stack([per_head(span[(last, s)]) * weighted[:, s] for s in range(window)], axis=1)
+    weight = jnp.concatenate([pushed, jnp.zeros_like(pushed)], axis=1)
+    carry = jnp.pad(cum[last], ((0, 0), (0, state_dim - heads_here)))[:, None, :]
+    mix = jnp.concatenate(
+        [readouts, entries, carry, jnp.zeros((slot_count, 2 * window - 1, state_dim), jnp.float32)],
         axis=1,
-    ).transpose(0, 2, 1)
-    mix = jnp.concatenate([readouts, entries], axis=1)
-    read, states_out = recurrence(received, recv_rows, mix, weight, state_rows)
+    )
+    read, states_out = recurrence(received, recv_rows, mix, weight, state_rows, heads_here)
     states_out = states_out.reshape(states.shape)
-    from_state = read[:, :window].reshape(slot_count, window, heads_here, head_dim)
     overlap = jnp.einsum("rtn,rsn->rts", readouts, entries, precision=HIGH)
+    skip_wide = jnp.repeat(skip_gain, head_dim)
     produced = []
     for t in range(window):
-        acc = cumulative[:, t, :, None] * from_state[:, t]
+        acc = per_head(cum[t]) * read[:, t]
         for s in range(t + 1):
-            coef = span[(t, s)] * overlap[:, t, s, None]
-            acc = acc + coef[:, :, None] * weighted[:, s]
-        produced.append(acc + skip_gain[None, :, None] * inputs[:, t])
+            acc = acc + per_head(span[(t, s)] * overlap[:, t, s, None]) * weighted[:, s]
+        produced.append(acc + skip_wide * flat_inputs[:, t])
     outputs = jnp.stack(produced, axis=1)
 
-    outputs = outputs.reshape(slot_count, window, inner_here)
     gated = outputs * jax.nn.silu(gate_part.astype(jnp.float32))
     square_part = jnp.sum(gated * gated, axis=-1).reshape(slot_count * window, 1)
     pre_scaled = (

time: 255 us -> 181 us (0.71)
  local copies, waits for them, and re-layouts: 76.8 us -> 25.5 us
  other arithmetic: 66.9 us -> 19.9 us
  waiting for transfers between devices: 27.5 us -> 49.2 us
  Pallas kernels: 13 us -> 15.7 us
    reduce_scatter x1, waiting for transfers between devices: 7.59 us -> 36.4 us  [local(): lax.psum_scatter(combined, 'head', scatter_dimension=0, tiled=True)]
    select_n x2, other arithmetic: 17.1 us -> 0.63 us  [new_edge(): jnp.where((counts == length)[:, None, None], sequence[:, length:length +...]
    unnamed x49 -> x42, local copies, waits for them, and re-layouts: 21.1 us -> 8.97 us
    reshape x3 -> x14, local copies, waits for them, and re-layouts: 13.3 us -> 1.62 us  [per_head(): return jnp.repeat(v, head_dim, axis=-1)]
    all_to_all x1, waiting for transfers between devices: 18 us -> 6.44 us  [local(): received = lax.all_to_all(send_buf, 'req', 0, 0, tiled=True)]
    transpose x1 -> x0, other arithmetic: 8.95 us -> none  [local(): weight = jnp.concatenate([pushed.reshape(slot_count, window, inner_here),...]
    mul x4 -> x3, other arithmetic: 8.76 us -> 0.47 us  [the longest x1 0.31 us: local(): weighted = per_head(step_size) * flat_inputs]
    convert_element_type x2 -> x0, local copies, waits for them, and re-layouts: 7.21 us -> none  [the longest x1 3.96 us: local(): gated = outputs * jax.nn.silu(gate_part.astype(jnp.float32))]
  transfers between devices with their start and end apart: 4 -> 4, of which waited for: 3 -> 3; matrix products, arithmetic and copies ran while one was open for 23% -> 8% of each run, Pallas kernels for 0% -> 0%
where the time goes in v3:
time: 181 us; the launch traced here: 180 us
  waiting for transfers between devices  49.2 us (27%)
  blocking collectives  28.9 us (16%)
  local copies, waits for them, and re-layouts  25.5 us (14%)
  starting transfers between devices  21 us (12%)
  other arithmetic  19.9 us (11%)
  between operations  18.1 us (10%)
  Pallas kernels  15.7 us (9%)
    reduce_scatter x1, waiting for transfers between devices, local(): lax.psum_scatter(combined, 'head', scatter_dimension=0, tiled=True)  36.4 us
    all_gather x1, blocking collectives, local(): piece_rows = lax.all_gather(normed, 'head', axis=0, tiled=True)  28.9 us
    pallas_call x1, Pallas kernels, recurrence(): pl.pallas_call(functools.partial(recurrence_kernel, group=group, window=w...  15.7 us
    unnamed x42, local copies, waits for them, and re-layouts  8.97 us
    all_to_all x1, starting transfers between devices, migrate(): first = lax.all_to_all(padded, 'req', 0, 0, tiled=True)  7.62 us
    all_to_all x1, starting transfers between devices, migrate(): second = lax.all_to_all(first[order], 'req', 0, 0, tiled=True)  7.38 us
    all_to_all x1, waiting for transfers between devices, local(): received = lax.all_to_all(send_buf, 'req', 0, 0, tiled=True)  6.44 us
    all_to_all x1, waiting for transfers between devices, migrate(): second = lax.all_to_all(first[order], 'req', 0, 0, tiled=True)  6.37 us
  transfers between devices with their start and end apart: 4, of which 3 were waited for; matrix products, arithmetic and copies ran while one was open for 8% of the time, Pallas kernels for 0%

profile of v3, /device:TPU:2, one launch (start us, length us, event | category | flops | bytes accessed | tf_op | source)
XLA Modules:
  0.0 179.9 jit_solution(16221802186281993597)
XLA Ops:
  7.2 1.3 dynamic_slice.23
  9.2 0.9 copy.123
  10.2 0.8 copy.124
  11.1 2.2 %pad_maximum_fusion = bf16[32,399,128]{2,1,0:T(8,128)(2,1)S(1)} fusion(bf16[32,6,128]{2,1,0:T(8,128)(2,1)S(1)} %reshape.350, bf16[32,9,128]{2,1,0:T(8,128)(2,1)S(1)} %reshape.349, bf16[32,384,128]{2,1,0:T(8,128)(2,1)} %bitcast.73), kind=kLoop, calls=%fused_computation.3 | loop fusion | flops 9805824 | bytes 6537216 | tf_op jit(solution)/shard_map/concatenate | solution.py:169
  13.4 1.7 copy-done.1
  15.1 0.2 all_to_all.23
  15.3 0.5 broadcast.351
  15.8 1.3 reduce.31
  17.1 0.8 reshape.436
  17.9 7.6 %all-to-all-start = ((bf16[32,2,798]{2,1,0:T(2,128)(2,1)}), bf16[32,2,798]{2,1,0:T(2,128)(2,1)S(1)}, u32[]{:S(2)}, u32[]{:S(2)}) async-start(bf16[32,2,798]{2,1,0:T(2,128)(2,1)} %reshape.436), calls=%async_computation | async-start | bytes 229376 | tf_op jit(solution)/shard_map/all_to_all | solution.py:113
  25.5 0.2 select_reduce_fusion
  25.9 0.6 dynamic_slice.21
  28.4 0.6 dynamic_slice.22
  29.6 0.2 convert_reduce_fusion
  30.0 4.6 %gather_fusion.1 = bf16[32,399,128]{2,1,0:T(8,128)(2,1)} fusion(bf16[32,399,128]{2,1,0:T(8,128)(2,1)} %copy-done.1, s32[1024]{0:T(1024)S(1)} %pad_clamp_fusion.1), kind=kCustom, calls=%fused_computation.1 | custom fusion | bytes 6537344 | tf_op jit(solution)/shard_map/gather | solution.py:190
  34.6 0.2 reshape.437
  34.8 0.7 gather_fusion
  35.5 0.7 reduce.32
  36.2 0.8 reshape.438
  37.0 7.4 %all-to-all-start.1 = ((bf16[32,2,798]{2,1,0:T(2,128)(2,1)}), bf16[32,2,798]{2,1,0:T(2,128)(2,1)S(1)}, u32[]{:S(2)}, u32[]{:S(2)}) async-start(bf16[32,2,798]{2,1,0:T(2,128)(2,1)} %reshape.438), calls=%async_computation.1 | async-start | bytes 229376 | tf_op jit(solution)/shard_map/all_to_all | solution.py:116
  44.4 0.1 fusion.13
  44.5 6.4 %all-to-all-done.1 = bf16[32,2,798]{2,1,0:T(2,128)(2,1)S(1)} async-done(((bf16[32,2,798]{2,1,0:T(2,128)(2,1)}), bf16[32,2,798]{2,1,0:T(2,128)(2,1)S(1)}, u32[]{:S(2)}, u32[]{:S(2)}) %all-to-all-start.1) | async-done | bytes 102176 | tf_op jit(solution)/shard_map/all_to_all | solution.py:116
  50.9 0.2 reshape.439
  51.1 0.6 reduce
  51.7 0.2 broadcast_in_dim.220
  51.9 3.9 %broadcast_select_fusion = bf16[32,399,128]{2,1,0:T(8,128)(2,1)} fusion(bf16[32,399,128]{2,1,0:T(8,128)(2,1)} %gather_fusion.1, pred[32]{0:T(512)(128)(4,1)S(1)} %broadcast_compare_fusion.3, bf16[399,128]{1,0:T(8,128)(2,1)S(1)} %broadcast_in_dim.220), kind=kLoop, calls=%fused_computation.4 | loop fusion | flops 1634304 | bytes 6639392 | tf_op jit(solution)/shard_map/jit(_where)/select_n | solution.py:189
  55.8 5.9 %all-to-all-start.2 = ((bf16[32,399,128]{2,1,0:T(8,128)(2,1)}), bf16[32,399,128]{2,1,0:T(8,128)(2,1)}, u32[]{:S(2)}, u32[]{:S(2)}) async-start(bf16[32,399,128]{2,1,0:T(8,128)(2,1)} %broadcast_select_fusion), calls=%async_computation.2 | async-start | bytes 6553600 | tf_op jit(solution)/shard_map/all_to_all | solution.py:192
  61.9 28.9 %all_gather.3 = bf16[128,1536]{1,0:T(8,128)(2,1)S(1)} all-gather(bf16[16,1536]{1,0:T(8,128)(2,1)S(1)} %fusion.15), channel_id=1, replica_groups=mesh['req'=32,'head'=8] {'head'}, dimensions={0}, use_global_device_ids=true | all-gather | bytes 442368 | tf_op jit(solution)/shard_map/all_gather | solution.py:158
  90.8 0.4 convolution_convert_fusion.1
  91.2 0.1 copy.121
  91.6 2.2 %copy.146 = bf16[192,8,2,384]{3,1,2,0:T(8,128)(2,1)S(1)} copy(bf16[192,8,2,384]{3,2,1,0:T(2,128)(2,1)} %bitcast.74) | data formatting | bytes 4718592
  93.9 0.5 convolution_convert_fusion
  94.7 0.2 broadcast_in_dim.226
  94.9 0.1 reshape.353
  95.8 0.2 convert_reduce_fusion.1
  96.0 0.6 compare_select_fusion.1
  96.6 6.4 %all-to-all-done.2.refs_0_.refs_1_.refs_2_.refs_3_ = bf16[32,399,128]{2,1,0:T(8,128)(2,1)} async-done(((bf16[32,399,128]{2,1,0:T(8,128)(2,1)}), bf16[32,399,128]{2,1,0:T(8,128)(2,1)}, u32[]{:S(2)}, u32[]{:S(2)}) %all-to-all-start.2) | async-done | bytes 3268640 | tf_op jit(solution)/shard_map/all_to_all | solution.py:192
  103.1 0.9 slice.272
  104.0 0.6 gather_fusion.2
  104.8 0.2 divide_multiply_fusion.1
  104.9 0.4 fusion.47
  105.3 1.0 slice_reduce_fusion.9
  106.5 0.1 reshape.404
  106.7 0.1 reshape.405
  107.3 0.1 reshape.410
  107.5 0.1 reshape.411
  108.2 0.1 reshape.408
  109.1 0.3 copy_multiply_fusion
  109.4 0.2 fusion.55
  109.6 0.8 maximum_maximum_fusion.refs_4_
  110.4 1.1 concatenate.24.refs_5_
  111.5 15.7 %shard_map.219 = (f32[32,8,384]{2,1,0:T(8,128)}, bf16[32,384,128]{2,1,0:T(8,128)(2,1)}) custom-call(s32[32]{0:T(128)} %get-tuple-element.57.rows_ref, bf16[32,399,128]{2,1,0:T(8,128)(2,1)} %all-to-all-done.2.refs_0_.refs_1_.refs_2_.refs_3_, bf16[32,399,128]{2,1,0:T(8,128)(2,1)} %all-to-all-done.2.refs_0_.refs_1_.refs_2_.refs_3_, ...), custom_call_target="tpu_custom_call" | custom-call | tf_op jit(solution)/shard_map/pallas_call | solution.py:99
  127.2 1.4 fusion.33
  128.7 1.5 fusion.32
  130.2 0.3 select_convert_fusion
  130.8 0.4 fusion.58
  131.3 1.0 pad_maximum_fusion.1
  132.3 0.4 fusion.20
  132.6 0.6 copy.141
  133.3 0.3 fusion.26
  133.5 0.6 copy.142
  134.2 36.4 %reduce-scatter.2.cloned.1.call-done = f32[16,1664]{1,0:T(8,128)} async-done(((f32[128,1664]{1,0:T(8,128)}), f32[16,1664]{1,0:T(8,128)}) %reduce-scatter.2.cloned.1.call-update) | async-done | bytes 106512 | tf_op jit(solution)/shard_map/reduce_scatter | solution.py:263
  170.6 0.9 fusion.43
  171.4 1.6 fusion.16
  (105 shorter events, 4.4 us)
Async XLA Ops:
  7.2 123.6 %copy-start = (bf16[384,1536]{1,0:T(8,128)(2,1)S(1)}, bf16[384,1536]{1,0:T(8,128)(2,1)}, u32[]{:S(2)}) copy-start(bf16[384,1536]{1,0:T(8,128)(2,1)} %param.32) | copy-start | bytes 3538948
  11.1 14.4 %copy-start.6 = (s32[1024]{0:T(1024)S(1)}, s32[1024]{0:T(1024)}, u32[]{:S(2)}) copy-start(s32[1024]{0:T(1024)} %param.39) | copy-start | bytes 12292
  11.1 14.6 %copy-start.13 = (s32[32]{0:T(128)S(1)}, s32[32]{0:T(128)}, u32[]{:S(2)}) copy-start(s32[32]{0:T(128)} %param.38) | copy-start | bytes 388
  13.4 1.7 copy-start.1
  17.9 16.8 %all-to-all-start = ((bf16[32,2,798]{2,1,0:T(2,128)(2,1)}), bf16[32,2,798]{2,1,0:T(2,128)(2,1)S(1)}, u32[]{:S(2)}, u32[]{:S(2)}) async-start(bf16[32,2,798]{2,1,0:T(2,128)(2,1)} %reshape.436), calls=%async_computation | async-start | bytes 229376 | tf_op jit(solution)/shard_map/all_to_all | solution.py:113
  30.0 14.4 %copy-start.3 = (bf16[16,1536]{1,0:T(8,128)(2,1)S(1)}, bf16[16,1536]{1,0:T(8,128)(2,1)}, u32[]{:S(2)}) copy-start(bf16[16,1536]{1,0:T(8,128)(2,1)} %param.20) | copy-start | bytes 147460
  37.0 13.9 %all-to-all-start.1 = ((bf16[32,2,798]{2,1,0:T(2,128)(2,1)}), bf16[32,2,798]{2,1,0:T(2,128)(2,1)S(1)}, u32[]{:S(2)}, u32[]{:S(2)}) async-start(bf16[32,2,798]{2,1,0:T(2,128)(2,1)} %reshape.438), calls=%async_computation.1 | async-start | bytes 229376 | tf_op jit(solution)/shard_map/all_to_all | solution.py:116
  55.8 6.0 %copy-start.4 = (f32[1536]{0:T(1024)S(1)}, f32[1536]{0:T(1024)}, u32[]{:S(2)}) copy-start(f32[1536]{0:T(1024)} %param.21) | copy-start | bytes 18436
  55.8 35.0 %copy-start.2 = (bf16[1536,304]{0,1:T(8,128)(2,1)S(1)}, bf16[1536,304]{0,1:T(8,128)(2,1)}, u32[]{:S(2)}) copy-start(bf16[1536,304]{0,1:T(8,128)(2,1)} %param.23) | copy-start | bytes 2801668
  55.8 35.6 %copy-start.10 = (s32[32]{0:T(128)S(1)}, s32[32]{0:T(128)}, u32[]{:S(2)}) copy-start(s32[32]{0:T(128)} %param.36) | copy-start | bytes 388
  55.8 47.2 %all-to-all-start.2 = ((bf16[32,399,128]{2,1,0:T(8,128)(2,1)}), bf16[32,399,128]{2,1,0:T(8,128)(2,1)}, u32[]{:S(2)}, u32[]{:S(2)}) async-start(bf16[32,399,128]{2,1,0:T(8,128)(2,1)} %broadcast_select_fusion), calls=%async_computation.2 | async-start | bytes 6553600 | tf_op jit(solution)/shard_map/all_to_all | solution.py:192
  61.8 108.8 %reduce-scatter.2.cloned.1.call-start = ((), (), s32[]{:S(2)}) async-start(), calls=%async_computation.4 | async-start | bytes 958464 | tf_op jit(solution)/shard_map/reduce_scatter | solution.py:263
  91.6 2.9 %copy-start.15 = (f32[6]{0:T(128)S(1)}, f32[6]{0:T(128)}, u32[]{:S(2)}) copy-start(f32[6]{0:T(128)} %param.29) | copy-start | bytes 76
  91.6 2.9 %copy-start.12 = (f32[6]{0:T(128)S(1)}, f32[6]{0:T(128)}, u32[]{:S(2)}) copy-start(f32[6]{0:T(128)} %param.28) | copy-start | bytes 76
  93.8 1.6 copy-start.14
  93.8 2.7 %copy-start.5 = (f32[4,384]{1,0:T(4,128)S(1)}, f32[4,384]{1,0:T(4,128)}, u32[]{:S(2)}) copy-start(f32[4,384]{1,0:T(4,128)} %param.24) | copy-start | bytes 18436
  93.8 2.8 %copy-start.7 = (f32[4,256]{1,0:T(4,128)S(1)}, f32[4,256]{1,0:T(4,128)}, u32[]{:S(2)}) copy-start(f32[4,256]{1,0:T(4,128)} %param.26) | copy-start | bytes 12292
  93.9 10.9 %copy-start.11 = (f32[256]{0:T(256)S(1)}, f32[256]{0:T(256)}, u32[]{:S(2)}) copy-start(f32[256]{0:T(256)} %param.27) | copy-start | bytes 3076
  104.6 4.5 %copy-start.8 = (f32[384]{0:T(512)S(1)}, f32[384]{0:T(512)}, u32[]{:S(2)}) copy-start(f32[384]{0:T(512)} %param.25) | copy-start | bytes 4612
  111.5 18.7 %copy-start.9 = (f32[384]{0:T(512)S(1)}, f32[384]{0:T(512)}, u32[]{:S(2)}) copy-start(f32[384]{0:T(512)} %param.31) | copy-start | bytes 4612
Sparse Core Ops, SparseCore 0:
  132.4 38.1 reduce-scatter.1

commit v4 on v3

--- a/solution.py
+++ b/solution.py
@@ -56,17 +56,31 @@
 def recurrence_kernel(rows_ref, *refs, group, window, heads):
     held_refs = refs[:group]
     mix_ref, weight_ref, read_ref, out_ref = refs[group:]
+    nt = (((1,), (1,)), ((), ()))
+    tn = (((0,), (0,)), ((), ()))
     for q in range(group):
-        held = held_refs[q][0].astype(jnp.float32)
+        held_low = held_refs[q][0]
         mix = mix_ref[q]
-        read_ref[q] = lax.dot_general(
-            mix[: 2 * window], held, (((1,), (1,)), ((), ())), precision=HIGH,
-            preferred_element_type=jnp.float32,
+        read = None
+        rest = mix[: 2 * window]
+        for _ in range(3):
+            part = rest.astype(jnp.bfloat16)
+            rest = rest - part.astype(jnp.float32)
+            term = lax.dot_general(part, held_low, nt, preferred_element_type=jnp.float32)
+            read = term if read is None else read + term
+        read_ref[q] = read
+        weight = weight_ref[q]
+        entry = mix[window : 3 * window]
+        w_hi = weight.astype(jnp.bfloat16)
+        w_lo = (weight - w_hi.astype(jnp.float32)).astype(jnp.bfloat16)
+        e_hi = entry.astype(jnp.bfloat16)
+        e_lo = (entry - e_hi.astype(jnp.float32)).astype(jnp.bfloat16)
+        pushed = (
+            lax.dot_general(w_hi, e_hi, tn, preferred_element_type=jnp.float32)
+            + lax.dot_general(w_hi, e_lo, tn, preferred_element_type=jnp.float32)
+            + lax.dot_general(w_lo, e_hi, tn, preferred_element_type=jnp.float32)
         )
-        pushed = lax.dot_general(
-            weight_ref[q], mix[window : 3 * window], (((0,), (0,)), ((), ())),
-            precision=HIGH, preferred_element_type=jnp.float32,
-        )
+        held = held_low.astype(jnp.float32)
         rows = held.shape[0] // heads
         carry = mix[2 * window : 2 * window + 1]
         for h in range(heads):
@@ -113,7 +127,9 @@
     first = lax.all_to_all(padded, "req", 0, 0, tiled=True)
     dest_dev = mig_dest // slot_count
     order = invert(dest_dev, groups)
-    second = lax.all_to_all(first[order], "req", 0, 0, tiled=True)
+    pick = (order[:, None] == jnp.arange(groups, dtype=jnp.int32)[None, :]).astype(first.dtype)
+    routed = jnp.dot(pick, first, preferred_element_type=jnp.float32).astype(first.dtype)
+    second = lax.all_to_all(routed, "req", 0, 0, tiled=True)
     arrived = second.reshape(-1)[:length]
     target_local = mig_dest[order[device]] - device * slot_count
     return arrived, target_local
@@ -179,7 +195,12 @@
     moving = mig_ids.shape[0] // groups
     own_id = mig_ids[device * moving]
     mig_local = own_id - first_slot
-    item = lax.dynamic_index_in_dim(packed, mig_local, 0, keepdims=False).reshape(-1)
+    item = jnp.concatenate(
+        [
+            lax.dynamic_index_in_dim(part, mig_local, 0, keepdims=False).reshape(-1)
+            for part in (states, edge_inner, edge_shared)
+        ]
+    )
     arrived, target_local = migrate(item, mig_dest, slot_count, groups, device)
     arrived = arrived.reshape(row_total, lanes)
 

time: 181 us -> 179 us (0.989)
  Pallas kernels: 15.7 us -> 10.5 us
  other arithmetic: 19.9 us -> 23.9 us
    pallas_call x1, Pallas kernels: 15.7 us -> 10.5 us  [recurrence(): pl.pallas_call(functools.partial(recurrence_kernel, group=group, window=w...]
    dynamic_slice x1 -> x3, local copies, waits for them, and re-layouts: 0.01 us -> 2.38 us  [local(): lax.dynamic_index_in_dim(part, mig_local, 0, keepdims=False).reshape(-1)]
    unnamed x42 -> x35, local copies, waits for them, and re-layouts: 8.97 us -> 7.26 us
  transfers between devices with their start and end apart: 4 -> 4, of which waited for: 3 -> 3; matrix products, arithmetic and copies ran while one was open for 8% -> 13% of each run, Pallas kernels for 0% -> 0%
where the time goes in v4:
time: 179 us; the launch traced here: 178 us
  waiting for transfers between devices  47.8 us (27%)
  blocking collectives  28.9 us (16%)
  local copies, waits for them, and re-layouts  26.2 us (15%)
  other arithmetic  23.9 us (13%)
  starting transfers between devices  21 us (12%)
  between operations  18 us (10%)
  Pallas kernels  10.5 us (6%)
  matrix products  1.81 us (1%)
    reduce_scatter x1, waiting for transfers between devices, local(): lax.psum_scatter(combined, 'head', scatter_dimension=0, tiled=True)  36.4 us
    all_gather x1, blocking collectives, local(): piece_rows = lax.all_gather(normed, 'head', axis=0, tiled=True)  28.9 us
    pallas_call x1, Pallas kernels, recurrence(): pl.pallas_call(functools.partial(recurrence_kernel, group=group, window=w...  10.5 us
    all_to_all x1, starting transfers between devices, migrate(): first = lax.all_to_all(padded, 'req', 0, 0, tiled=True)  7.62 us
    all_to_all x1, starting transfers between devices, migrate(): second = lax.all_to_all(routed, 'req', 0, 0, tiled=True)  7.38 us
    unnamed x35, local copies, waits for them, and re-layouts  7.26 us
    all_to_all x1, waiting for transfers between devices, migrate(): second = lax.all_to_all(routed, 'req', 0, 0, tiled=True)  6.37 us
    all_to_all x1, starting transfers between devices, local(): received = lax.all_to_all(send_buf, 'req', 0, 0, tiled=True)  5.93 us
  transfers between devices with their start and end apart: 4, of which 3 were waited for; matrix products, arithmetic and copies ran while one was open for 13% of the time, Pallas kernels for 0%

profile of v4, /device:TPU:2, one launch (start us, length us, event | category | flops | bytes accessed | tf_op | source)
XLA Modules:
  0.0 178.1 jit_solution(657091600804491792)
XLA Ops:
  7.2 1.3 dynamic_slice.31
  9.2 0.9 constant_dynamic-slice_fusion
  10.1 0.8 dynamic-slice_reduce_fusion
  10.9 0.7 dynamic-slice_reduce_fusion.1
  11.6 0.2 all_to_all.23
  11.8 0.5 broadcast.335
  12.3 1.3 reduce.35
  13.6 0.8 reshape.430
  14.4 7.6 %all-to-all-start = ((bf16[32,2,798]{2,1,0:T(2,128)(2,1)}), bf16[32,2,798]{2,1,0:T(2,128)(2,1)S(1)}, u32[]{:S(2)}, u32[]{:S(2)}) async-start(bf16[32,2,798]{2,1,0:T(2,128)(2,1)} %reshape.430), calls=%async_computation | async-start | bytes 229376 | tf_op jit(solution)/shard_map/all_to_all | solution.py:127
  22.1 0.7 and_select_fusion
  22.8 0.6 dynamic_slice.29
  24.7 0.9 copy.126
  25.7 0.8 copy.127
  27.2 1.2 dynamic_slice.30
  29.1 0.9 select_reduce_fusion
  30.0 0.2 convert_reduce_fusion
  30.4 3.4 %pad_maximum_fusion = bf16[32,399,128]{2,1,0:T(8,128)(2,1)} fusion(bf16[32,6,128]{2,1,0:T(8,128)(2,1)S(1)} %reshape.350, bf16[32,9,128]{2,1,0:T(8,128)(2,1)S(1)} %reshape.349, bf16[32,384,128]{2,1,0:T(8,128)(2,1)} %bitcast.70), kind=kLoop, calls=%fused_computation.2 | loop fusion | flops 9805824 | bytes 6537216 | tf_op jit(solution)/shard_map/concatenate | solution.py:185
  33.9 4.6 %gather_fusion = bf16[32,399,128]{2,1,0:T(8,128)(2,1)} fusion(bf16[32,399,128]{2,1,0:T(8,128)(2,1)} %pad_maximum_fusion, s32[1024]{0:T(1024)S(1)} %pad_clamp_fusion.1), kind=kCustom, calls=%fused_computation | custom fusion | bytes 6537344 | tf_op jit(solution)/shard_map/gather | solution.py:211
  38.5 0.2 reshape.431
  38.7 0.2 fusion
  38.9 0.7 reduce.36
  39.6 0.8 reshape.432
  40.4 7.4 %all-to-all-start.1 = ((bf16[32,2,798]{2,1,0:T(2,128)(2,1)}), bf16[32,2,798]{2,1,0:T(2,128)(2,1)S(1)}, u32[]{:S(2)}, u32[]{:S(2)}) async-start(bf16[32,2,798]{2,1,0:T(2,128)(2,1)} %reshape.432), calls=%async_computation.1 | async-start | bytes 229376 | tf_op jit(solution)/shard_map/all_to_all | solution.py:132
  47.8 0.1 fusion.16
  47.9 6.4 %all-to-all-done.1 = bf16[32,2,798]{2,1,0:T(2,128)(2,1)S(1)} async-done(((bf16[32,2,798]{2,1,0:T(2,128)(2,1)}), bf16[32,2,798]{2,1,0:T(2,128)(2,1)S(1)}, u32[]{:S(2)}, u32[]{:S(2)}) %all-to-all-start.1) | async-done | bytes 102176 | tf_op jit(solution)/shard_map/all_to_all | solution.py:132
  54.3 0.2 reshape.433
  54.5 0.6 reduce.2
  55.1 0.2 broadcast_in_dim.221
  55.3 3.9 %broadcast_select_fusion = bf16[32,399,128]{2,1,0:T(8,128)(2,1)} fusion(bf16[32,399,128]{2,1,0:T(8,128)(2,1)} %gather_fusion, pred[32]{0:T(512)(128)(4,1)S(1)} %broadcast_compare_fusion.3, bf16[399,128]{1,0:T(8,128)(2,1)S(1)} %broadcast_in_dim.221), kind=kLoop, calls=%fused_computation.3 | loop fusion | flops 1634304 | bytes 6639392 | tf_op jit(solution)/shard_map/jit(_where)/select_n | solution.py:210
  59.3 5.9 %all-to-all-start.2 = ((bf16[32,399,128]{2,1,0:T(8,128)(2,1)}), bf16[32,399,128]{2,1,0:T(8,128)(2,1)}, u32[]{:S(2)}, u32[]{:S(2)}) async-start(bf16[32,399,128]{2,1,0:T(8,128)(2,1)} %broadcast_select_fusion), calls=%async_computation.2 | async-start | bytes 6553600 | tf_op jit(solution)/shard_map/all_to_all | solution.py:213
  65.3 28.9 %all_gather.3 = bf16[128,1536]{1,0:T(8,128)(2,1)S(1)} all-gather(bf16[16,1536]{1,0:T(8,128)(2,1)S(1)} %fusion.18), channel_id=1, replica_groups=mesh['req'=32,'head'=8] {'head'}, dimensions={0}, use_global_device_ids=true | all-gather | bytes 442368 | tf_op jit(solution)/shard_map/all_gather | solution.py:174
  94.2 0.4 convolution_convert_fusion.2
  94.6 0.1 copy.122
  95.1 2.2 %copy.147 = bf16[192,8,2,384]{3,1,2,0:T(8,128)(2,1)S(1)} copy(bf16[192,8,2,384]{3,2,1,0:T(2,128)(2,1)} %bitcast.71) | data formatting | bytes 4718592
  97.3 0.5 convolution_convert_fusion.1
  98.1 0.2 broadcast_in_dim.227
  98.3 0.1 reshape.353
  98.5 0.1 reshape.398
  99.1 0.8 and_select_fusion.3
  99.9 0.2 convert_reduce_fusion.1
  100.1 1.3 compare_select_fusion.1
  101.4 5.1 %all-to-all-done.2.refs_0_.refs_1_.refs_2_.refs_3_ = bf16[32,399,128]{2,1,0:T(8,128)(2,1)} async-done(((bf16[32,399,128]{2,1,0:T(8,128)(2,1)}), bf16[32,399,128]{2,1,0:T(8,128)(2,1)}, u32[]{:S(2)}, u32[]{:S(2)}) %all-to-all-start.2) | async-done | bytes 3268640 | tf_op jit(solution)/shard_map/all_to_all | solution.py:213
  106.5 0.9 slice.270
  107.4 0.6 gather_fusion.1
  108.2 0.2 divide_multiply_fusion.1
  108.3 0.4 fusion.50
  108.7 1.0 slice_reduce_fusion.9
  112.5 0.3 copy_multiply_fusion
  112.8 0.2 fusion.58
  113.0 0.8 maximum_maximum_fusion.refs_4_
  113.8 1.1 concatenate.28.refs_5_
  114.9 10.5 %shard_map.219 = (f32[32,8,384]{2,1,0:T(8,128)}, bf16[32,384,128]{2,1,0:T(8,128)(2,1)}) custom-call(s32[32]{0:T(128)} %get-tuple-element.57.rows_ref, bf16[32,399,128]{2,1,0:T(8,128)(2,1)} %all-to-all-done.2.refs_0_.refs_1_.refs_2_.refs_3_, bf16[32,399,128]{2,1,0:T(8,128)(2,1)} %all-to-all-done.2.refs_0_.refs_1_.refs_2_.refs_3_, ...), custom_call_target="tpu_custom_call" | custom-call | tf_op jit(solution)/shard_map/pallas_call | solution.py:113
  125.5 1.4 fusion.36
  126.9 1.5 fusion.35
  128.4 0.3 select_convert_fusion
  129.0 0.4 fusion.61
  129.5 1.0 pad_maximum_fusion.1
  130.5 0.4 fusion.23
  130.9 0.6 copy.142
  131.5 0.3 fusion.29
  131.8 0.6 copy.143
  132.4 36.4 %reduce-scatter.2.cloned.1.call-done = f32[16,1664]{1,0:T(8,128)} async-done(((f32[128,1664]{1,0:T(8,128)}), f32[16,1664]{1,0:T(8,128)}) %reduce-scatter.2.cloned.1.call-update) | async-done | bytes 106512 | tf_op jit(solution)/shard_map/reduce_scatter | solution.py:284
  168.8 0.9 fusion.46
  169.7 1.6 fusion.19
  (102 shorter events, 4.8 us)
Async XLA Ops:
  7.2 121.9 %copy-start = (bf16[384,1536]{1,0:T(8,128)(2,1)S(1)}, bf16[384,1536]{1,0:T(8,128)(2,1)}, u32[]{:S(2)}) copy-start(bf16[384,1536]{1,0:T(8,128)(2,1)} %param.32) | copy-start | bytes 3538948
  14.4 24.1 %all-to-all-start = ((bf16[32,2,798]{2,1,0:T(2,128)(2,1)}), bf16[32,2,798]{2,1,0:T(2,128)(2,1)S(1)}, u32[]{:S(2)}, u32[]{:S(2)}) async-start(bf16[32,2,798]{2,1,0:T(2,128)(2,1)} %reshape.430), calls=%async_computation | async-start | bytes 229376 | tf_op jit(solution)/shard_map/all_to_all | solution.py:127
  33.9 13.9 %copy-start.2 = (bf16[16,1536]{1,0:T(8,128)(2,1)S(1)}, bf16[16,1536]{1,0:T(8,128)(2,1)}, u32[]{:S(2)}) copy-start(bf16[16,1536]{1,0:T(8,128)(2,1)} %param.20) | copy-start | bytes 147460
  40.4 13.9 %all-to-all-start.1 = ((bf16[32,2,798]{2,1,0:T(2,128)(2,1)}), bf16[32,2,798]{2,1,0:T(2,128)(2,1)S(1)}, u32[]{:S(2)}, u32[]{:S(2)}) async-start(bf16[32,2,798]{2,1,0:T(2,128)(2,1)} %reshape.432), calls=%async_computation.1 | async-start | bytes 229376 | tf_op jit(solution)/shard_map/all_to_all | solution.py:132
  59.2 6.0 %copy-start.3 = (f32[1536]{0:T(1024)S(1)}, f32[1536]{0:T(1024)}, u32[]{:S(2)}) copy-start(f32[1536]{0:T(1024)} %param.21) | copy-start | bytes 18436
  59.2 35.0 %copy-start.1 = (bf16[1536,304]{0,1:T(8,128)(2,1)S(1)}, bf16[1536,304]{0,1:T(8,128)(2,1)}, u32[]{:S(2)}) copy-start(bf16[1536,304]{0,1:T(8,128)(2,1)} %param.23) | copy-start | bytes 2801668
  59.3 35.6 %copy-start.8 = (s32[32]{0:T(128)S(1)}, s32[32]{0:T(128)}, u32[]{:S(2)}) copy-start(s32[32]{0:T(128)} %param.36) | copy-start | bytes 388
  59.3 47.2 %all-to-all-start.2 = ((bf16[32,399,128]{2,1,0:T(8,128)(2,1)}), bf16[32,399,128]{2,1,0:T(8,128)(2,1)}, u32[]{:S(2)}, u32[]{:S(2)}) async-start(bf16[32,399,128]{2,1,0:T(8,128)(2,1)} %broadcast_select_fusion), calls=%async_computation.2 | async-start | bytes 6553600 | tf_op jit(solution)/shard_map/all_to_all | solution.py:213
  65.2 103.6 %reduce-scatter.2.cloned.1.call-start = ((), (), s32[]{:S(2)}) async-start(), calls=%async_computation.4 | async-start | bytes 958464 | tf_op jit(solution)/shard_map/reduce_scatter | solution.py:284
  95.1 2.9 %copy-start.12 = (f32[6]{0:T(128)S(1)}, f32[6]{0:T(128)}, u32[]{:S(2)}) copy-start(f32[6]{0:T(128)} %param.29) | copy-start | bytes 76
  95.1 2.9 %copy-start.10 = (f32[6]{0:T(128)S(1)}, f32[6]{0:T(128)}, u32[]{:S(2)}) copy-start(f32[6]{0:T(128)} %param.28) | copy-start | bytes 76
  97.2 1.6 copy-start.11
  97.2 4.1 %copy-start.4 = (f32[4,384]{1,0:T(4,128)S(1)}, f32[4,384]{1,0:T(4,128)}, u32[]{:S(2)}) copy-start(f32[4,384]{1,0:T(4,128)} %param.24) | copy-start | bytes 18436
  97.3 4.1 %copy-start.5 = (f32[4,256]{1,0:T(4,128)S(1)}, f32[4,256]{1,0:T(4,128)}, u32[]{:S(2)}) copy-start(f32[4,256]{1,0:T(4,128)} %param.26) | copy-start | bytes 12292
  97.3 10.9 %copy-start.9 = (f32[256]{0:T(256)S(1)}, f32[256]{0:T(256)}, u32[]{:S(2)}) copy-start(f32[256]{0:T(256)} %param.27) | copy-start | bytes 3076
  108.0 4.5 %copy-start.6 = (f32[384]{0:T(512)S(1)}, f32[384]{0:T(512)}, u32[]{:S(2)}) copy-start(f32[384]{0:T(512)} %param.25) | copy-start | bytes 4612
  114.9 13.5 %copy-start.7 = (f32[384]{0:T(512)S(1)}, f32[384]{0:T(512)}, u32[]{:S(2)}) copy-start(f32[384]{0:T(512)} %param.31) | copy-start | bytes 4612
Sparse Core Ops, SparseCore 0:
  130.6 38.1 reduce-scatter.1

commit v5 on v4

--- a/solution.py
+++ b/solution.py
@@ -119,6 +119,55 @@
         ],
     )(rows, *([received] * group), mix, weight)
 
+MESH = pl.DeviceIdType.MESH
+
+
+def scatter_sum_kernel(x_ref, out_ref, slots, send_sem, recv_sem, *, n, rows):
+    me = lax.axis_index("head")
+    group = lax.axis_index("req")
+    barrier = pltpu.get_barrier_semaphore()
+    for k in range(1, n):
+        pl.semaphore_signal(
+            barrier, inc=1, device_id=(group, lax.rem(me + k, n)), device_id_type=MESH
+        )
+    pl.semaphore_wait(barrier, n - 1)
+    copies = []
+    for k in range(1, n):
+        peer = lax.rem(me + k, n)
+        start = pl.multiple_of(peer * rows, rows)
+        copy = pltpu.make_async_remote_copy(
+            src_ref=x_ref.at[pl.ds(start, rows)],
+            dst_ref=slots.at[k - 1],
+            send_sem=send_sem.at[k - 1],
+            recv_sem=recv_sem.at[k - 1],
+            device_id=(group, peer),
+            device_id_type=MESH,
+        )
+        copy.start()
+        copies.append(copy)
+    own = pl.multiple_of(me * rows, rows)
+    total = x_ref[pl.ds(own, rows)].astype(jnp.float32)
+    for k, copy in enumerate(copies):
+        copy.wait()
+        total = total + slots[k].astype(jnp.float32)
+    out_ref[...] = total
+
+
+def scatter_sum(x, n):
+    rows = x.shape[0] // n
+    return pl.pallas_call(
+        functools.partial(scatter_sum_kernel, n=n, rows=rows),
+        out_shape=jax.ShapeDtypeStruct((rows, x.shape[1]), jnp.float32),
+        in_specs=[pl.BlockSpec(memory_space=pltpu.VMEM)],
+        out_specs=pl.BlockSpec(memory_space=pltpu.VMEM),
+        scratch_shapes=[
+            pltpu.VMEM((n - 1, rows, x.shape[1]), x.dtype),
+            pltpu.SemaphoreType.DMA((n - 1,)),
+            pltpu.SemaphoreType.DMA((n - 1,)),
+        ],
+        compiler_params=pltpu.CompilerParams(collective_id=0, has_side_effects=True),
+    )(x)
+
 
 def migrate(item, mig_dest, slot_count, groups, device):
     length = item.shape[0]
@@ -279,12 +328,18 @@
         .reshape(slot_count * window, inner_here)
     )
     partial = jnp.dot(pre_scaled, out_weight, preferred_element_type=jnp.float32)
-    extra = jnp.broadcast_to(square_part, (partial.shape[0], 128))
-    combined = jnp.concatenate([partial, extra], axis=1)
-    reduced = lax.psum_scatter(combined, "head", scatter_dimension=0, tiled=True)
+    square_hi = square_part.astype(jnp.bfloat16)
+    square_lo = (square_part - square_hi.astype(jnp.float32)).astype(jnp.bfloat16)
+    extra = jnp.pad(
+        jnp.concatenate([square_hi, square_lo], axis=1), ((0, 0), (0, 126))
+    )
+    combined = jnp.concatenate([partial.astype(jnp.bfloat16), extra], axis=1)
+    reduced = scatter_sum(combined, lax.axis_size("head"))
     full_inner = inner_here * lax.axis_size("head")
-    scale = lax.rsqrt(reduced[:, -1:] / full_inner + EPS)
-    hidden_out = (rows_in + reduced[:, : partial.shape[1]] * scale).astype(jnp.bfloat16)
+    width = partial.shape[1]
+    square_sum = reduced[:, width : width + 1] + reduced[:, width + 1 : width + 2]
+    scale = lax.rsqrt(square_sum / full_inner + EPS)
+    hidden_out = (rows_in + reduced[:, :width] * scale).astype(jnp.bfloat16)
     return (hidden_out, states_out, edge_inner_out, edge_shared_out)
 
 

time: 179 us -> 145 us (0.81)
  waiting for transfers between devices: 47.8 us -> 7 us
  Pallas kernels: 10.5 us -> 29.4 us
  between operations: 18 us -> 4.65 us
    reduce_scatter x1 -> x0, waiting for transfers between devices: 36.4 us -> none  [local(): lax.psum_scatter(combined, 'head', scatter_dimension=0, tiled=True)]
    pallas_call x0 -> x1, Pallas kernels: none -> 18.8 us  [scatter_sum(): pl.pallas_call(functools.partial(scatter_sum_kernel, n=n, rows=rows), out...]
    all_to_all x1, waiting for transfers between devices: 6.37 us -> 1.88 us  [migrate(): second = lax.all_to_all(routed, 'req', 0, 0, tiled=True)]
  transfers between devices with their start and end apart: 4 -> 3, of which waited for: 3 -> 2; matrix products, arithmetic and copies ran while one was open for 13% -> 15% of each run, Pallas kernels for 0% -> 0%
where the time goes in v5:
time: 145 us; the launch traced here: 143 us
  Pallas kernels  29.4 us (20%)
  blocking collectives  28.9 us (20%)
  local copies, waits for them, and re-layouts  26.3 us (18%)
  other arithmetic  24.6 us (17%)
  starting transfers between devices  20.9 us (14%)
  waiting for transfers between devices  7 us (5%)
  between operations  4.65 us (3%)
  matrix products  1.8 us (1%)
    all_gather x1, blocking collectives, local(): piece_rows = lax.all_gather(normed, 'head', axis=0, tiled=True)  28.9 us
    pallas_call x1, Pallas kernels, scatter_sum(): pl.pallas_call(functools.partial(scatter_sum_kernel, n=n, rows=rows), out...  18.8 us
    pallas_call x1, Pallas kernels, recurrence(): pl.pallas_call(functools.partial(recurrence_kernel, group=group, window=w...  10.5 us
    all_to_all x1, starting transfers between devices, migrate(): first = lax.all_to_all(padded, 'req', 0, 0, tiled=True)  7.62 us
    all_to_all x1, starting transfers between devices, migrate(): second = lax.all_to_all(routed, 'req', 0, 0, tiled=True)  7.38 us
    unnamed x35, local copies, waits for them, and re-layouts  7.26 us
    all_to_all x1, starting transfers between devices, local(): received = lax.all_to_all(send_buf, 'req', 0, 0, tiled=True)  5.94 us
    all_to_all x1, waiting for transfers between devices, local(): received = lax.all_to_all(send_buf, 'req', 0, 0, tiled=True)  5.11 us
  transfers between devices with their start and end apart: 3, of which 2 were waited for; matrix products, arithmetic and copies ran while one was open for 15% of the time, Pallas kernels for 0%

profile of v5, /device:TPU:2, one launch (start us, length us, event | category | flops | bytes accessed | tf_op | source)
XLA Modules:
  0.0 143.5 jit_solution(4838806918914560630)
XLA Ops:
  0.7 1.3 dynamic_slice.31
  2.6 0.9 constant_dynamic-slice_fusion
  3.5 0.8 dynamic-slice_reduce_fusion
  4.3 0.7 dynamic-slice_reduce_fusion.1
  5.1 0.2 all_to_all.23
  5.3 0.5 broadcast.341
  5.8 1.3 reduce.35
  7.1 0.8 reshape.468
  7.9 7.6 %all-to-all-start = ((bf16[32,2,798]{2,1,0:T(2,128)(2,1)}), bf16[32,2,798]{2,1,0:T(2,128)(2,1)S(1)}, u32[]{:S(2)}, u32[]{:S(2)}) async-start(bf16[32,2,798]{2,1,0:T(2,128)(2,1)} %reshape.468), calls=%async_computation | async-start | bytes 229376 | tf_op jit(solution)/shard_map/all_to_all | solution.py:176
  15.5 0.7 and_select_fusion
  16.3 0.6 dynamic_slice.29
  18.2 0.9 copy.133
  19.2 0.8 copy.134
  20.7 1.2 dynamic_slice.30
  22.5 0.9 select_reduce_fusion
  23.4 0.2 convert_reduce_fusion
  23.9 0.9 fusion.18
  24.8 3.4 %pad_maximum_fusion = bf16[32,399,128]{2,1,0:T(8,128)(2,1)} fusion(bf16[32,6,128]{2,1,0:T(8,128)(2,1)S(1)} %reshape.387, bf16[32,9,128]{2,1,0:T(8,128)(2,1)S(1)} %reshape.386, bf16[32,384,128]{2,1,0:T(8,128)(2,1)} %bitcast.70), kind=kLoop, calls=%fused_computation.2 | loop fusion | flops 9805824 | bytes 6537216 | tf_op jit(solution)/shard_map/concatenate | solution.py:234
  28.3 0.2 reshape.469
  28.5 0.2 fusion
  28.7 0.7 reduce.36
  29.4 0.8 reshape.470
  30.2 7.4 %all-to-all-start.1 = ((bf16[32,2,798]{2,1,0:T(2,128)(2,1)}), bf16[32,2,798]{2,1,0:T(2,128)(2,1)S(1)}, u32[]{:S(2)}, u32[]{:S(2)}) async-start(bf16[32,2,798]{2,1,0:T(2,128)(2,1)} %reshape.470), calls=%async_computation.1 | async-start | bytes 229376 | tf_op jit(solution)/shard_map/all_to_all | solution.py:181
  37.6 4.6 %gather_fusion = bf16[32,399,128]{2,1,0:T(8,128)(2,1)} fusion(bf16[32,399,128]{2,1,0:T(8,128)(2,1)} %pad_maximum_fusion, s32[1024]{0:T(1024)S(1)} %pad_clamp_fusion.1), kind=kCustom, calls=%fused_computation | custom fusion | bytes 6537344 | tf_op jit(solution)/shard_map/gather | solution.py:260
  42.2 1.9 %all-to-all-done.1 = bf16[32,2,798]{2,1,0:T(2,128)(2,1)S(1)} async-done(((bf16[32,2,798]{2,1,0:T(2,128)(2,1)}), bf16[32,2,798]{2,1,0:T(2,128)(2,1)S(1)}, u32[]{:S(2)}, u32[]{:S(2)}) %all-to-all-start.1) | async-done | bytes 102176 | tf_op jit(solution)/shard_map/all_to_all | solution.py:181
  44.1 0.2 reshape.471
  44.2 0.6 reduce.2
  44.9 0.2 broadcast_in_dim.214
  45.1 3.9 %broadcast_select_fusion = bf16[32,399,128]{2,1,0:T(8,128)(2,1)} fusion(bf16[32,399,128]{2,1,0:T(8,128)(2,1)} %gather_fusion, pred[32]{0:T(512)(128)(4,1)S(1)} %broadcast_compare_fusion.3, bf16[399,128]{1,0:T(8,128)(2,1)S(1)} %broadcast_in_dim.214), kind=kLoop, calls=%fused_computation.3 | loop fusion | flops 1634304 | bytes 6639392 | tf_op jit(solution)/shard_map/jit(_where)/select_n | solution.py:259
  49.0 5.9 %all-to-all-start.2 = ((bf16[32,399,128]{2,1,0:T(8,128)(2,1)}), bf16[32,399,128]{2,1,0:T(8,128)(2,1)}, u32[]{:S(2)}, u32[]{:S(2)}) async-start(bf16[32,399,128]{2,1,0:T(8,128)(2,1)} %broadcast_select_fusion), calls=%async_computation.2 | async-start | bytes 6553600 | tf_op jit(solution)/shard_map/all_to_all | solution.py:262
  55.1 28.9 %all_gather.3 = bf16[128,1536]{1,0:T(8,128)(2,1)S(1)} all-gather(bf16[16,1536]{1,0:T(8,128)(2,1)S(1)} %fusion.20), channel_id=1, replica_groups=mesh['req'=32,'head'=8] {'head'}, dimensions={0}, use_global_device_ids=true | all-gather | bytes 442368 | tf_op jit(solution)/shard_map/all_gather | solution.py:223
  84.0 0.4 convolution_convert_fusion.3
  84.4 0.1 copy.129
  84.8 2.2 %copy.155 = bf16[192,8,2,384]{3,1,2,0:T(8,128)(2,1)S(1)} copy(bf16[192,8,2,384]{3,2,1,0:T(2,128)(2,1)} %bitcast.71) | data formatting | bytes 4718592
  87.0 0.5 convolution_convert_fusion.2
  87.8 0.2 broadcast_in_dim.220
  88.0 0.1 reshape.390
  88.8 0.8 and_select_fusion.3
  89.6 0.2 convert_reduce_fusion.1
  89.8 1.3 compare_select_fusion.1
  91.1 5.1 %all-to-all-done.2.refs_0_.refs_1_.refs_2_.refs_3_ = bf16[32,399,128]{2,1,0:T(8,128)(2,1)} async-done(((bf16[32,399,128]{2,1,0:T(8,128)(2,1)}), bf16[32,399,128]{2,1,0:T(8,128)(2,1)}, u32[]{:S(2)}, u32[]{:S(2)}) %all-to-all-start.2) | async-done | bytes 3268640 | tf_op jit(solution)/shard_map/all_to_all | solution.py:262
  96.3 0.9 slice.274
  97.2 0.6 gather_fusion.1
  98.0 0.2 divide_multiply_fusion.1
  98.1 0.3 fusion.49
  98.7 0.4 fusion.25
  99.1 0.3 fusion.31
  99.3 1.0 slice_reduce_fusion.9
  102.9 0.3 copy_multiply_fusion
  103.3 0.2 fusion.57
  103.5 0.8 maximum_maximum_fusion.refs_4_
  104.3 1.1 concatenate.31.refs_5_
  105.4 10.5 %shard_map.219 = (f32[32,8,384]{2,1,0:T(8,128)}, bf16[32,384,128]{2,1,0:T(8,128)(2,1)}) custom-call(s32[32]{0:T(128)} %get-tuple-element.57.rows_ref, bf16[32,399,128]{2,1,0:T(8,128)(2,1)} %all-to-all-done.2.refs_0_.refs_1_.refs_2_.refs_3_, bf16[32,399,128]{2,1,0:T(8,128)(2,1)} %all-to-all-done.2.refs_0_.refs_1_.refs_2_.refs_3_, ...), custom_call_target="tpu_custom_call" | custom-call | tf_op jit(solution)/shard_map/pallas_call | solution.py:113
  115.9 1.4 fusion.38
  117.3 1.5 %fusion.37 = (f32[32,1,384]{2,1,0:T(1,128)S(1)}, f32[32,1,384]{2,1,0:T(1,128)S(1)}) fusion(f32[32,4,384]{2,1,0:T(4,128)S(1)} %get-tuple-element.49, f32[32,1,384]{2,1,0:T(1,128)S(1)} %reshape.438, f32[32,1,384]{2,1,0:T(1,128)S(1)} %reshape.437, f32[32,8,384]{2,1,0:T(8,128)} %get-tuple-element.6, f32[32]{0:T(128)S(1)} %get-tuple-element.40, f32[384]{0:T(512)S(1)} %mul.376, ...), kind=kLoop, calls=%fused_computation.82 | loop fusion | flops 221184 | bytes 788224 | tf_op jit(solution)/shard_map/add | solution.py:320
  118.9 0.3 select_convert_fusion
  119.5 0.1 copy.149
  119.6 0.4 convolution_convert_fusion
  120.0 0.8 fusion.2.x_ref
  120.8 18.8 %shard_map.220 = f32[16,1664]{1,0:T(8,128)} custom-call(bf16[128,1664]{1,0:T(8,128)(2,1)} %fusion.2.x_ref), custom_call_target="tpu_custom_call" | custom-call | tf_op jit(solution)/shard_map/pallas_call | solution.py:158
  139.6 1.0 rsqrt_reduce_fusion
  140.6 1.6 %fusion.21 = bf16[16,1536]{1,0:T(8,128)(2,1)} fusion(bf16[16,1536]{1,0:T(8,128)(2,1)S(1)} %copy-done.2, f32[16,1664]{1,0:T(8,128)} %shard_map.220, f32[16]{0:T(128)S(1)} %rsqrt_reduce_fusion), kind=kLoop, calls=%fused_computation.62 | loop fusion | flops 98304 | bytes 196672 | tf_op jit(solution)/shard_map/convert_element_type | solution.py:342
  142.2 0.6 copy.150
  142.8 0.6 copy.151
  (102 shorter events, 4.8 us)
Async XLA Ops:
  0.6 119.0 %copy-start = (bf16[384,1536]{1,0:T(8,128)(2,1)S(1)}, bf16[384,1536]{1,0:T(8,128)(2,1)}, u32[]{:S(2)}) copy-start(bf16[384,1536]{1,0:T(8,128)(2,1)} %param.32) | copy-start | bytes 3538948
  7.9 20.4 %all-to-all-start = ((bf16[32,2,798]{2,1,0:T(2,128)(2,1)}), bf16[32,2,798]{2,1,0:T(2,128)(2,1)S(1)}, u32[]{:S(2)}, u32[]{:S(2)}) async-start(bf16[32,2,798]{2,1,0:T(2,128)(2,1)} %reshape.468), calls=%async_computation | async-start | bytes 229376 | tf_op jit(solution)/shard_map/all_to_all | solution.py:176
  30.2 13.9 %all-to-all-start.1 = ((bf16[32,2,798]{2,1,0:T(2,128)(2,1)}), bf16[32,2,798]{2,1,0:T(2,128)(2,1)S(1)}, u32[]{:S(2)}, u32[]{:S(2)}) async-start(bf16[32,2,798]{2,1,0:T(2,128)(2,1)} %reshape.470), calls=%async_computation.1 | async-start | bytes 229376 | tf_op jit(solution)/shard_map/all_to_all | solution.py:181
  49.0 6.0 %copy-start.2 = (bf16[16,1536]{1,0:T(8,128)(2,1)S(1)}, bf16[16,1536]{1,0:T(8,128)(2,1)}, u32[]{:S(2)}) copy-start(bf16[16,1536]{1,0:T(8,128)(2,1)} %param.20) | copy-start | bytes 147460
  49.0 6.0 %copy-start.3 = (f32[1536]{0:T(1024)S(1)}, f32[1536]{0:T(1024)}, u32[]{:S(2)}) copy-start(f32[1536]{0:T(1024)} %param.21) | copy-start | bytes 18436
  49.0 34.9 %copy-start.1 = (bf16[1536,304]{0,1:T(8,128)(2,1)S(1)}, bf16[1536,304]{0,1:T(8,128)(2,1)}, u32[]{:S(2)}) copy-start(bf16[1536,304]{0,1:T(8,128)(2,1)} %param.23) | copy-start | bytes 2801668
  49.0 35.6 %copy-start.8 = (s32[32]{0:T(128)S(1)}, s32[32]{0:T(128)}, u32[]{:S(2)}) copy-start(s32[32]{0:T(128)} %param.36) | copy-start | bytes 388
  49.0 47.2 %all-to-all-start.2 = ((bf16[32,399,128]{2,1,0:T(8,128)(2,1)}), bf16[32,399,128]{2,1,0:T(8,128)(2,1)}, u32[]{:S(2)}, u32[]{:S(2)}) async-start(bf16[32,399,128]{2,1,0:T(8,128)(2,1)} %broadcast_select_fusion), calls=%async_computation.2 | async-start | bytes 6553600 | tf_op jit(solution)/shard_map/all_to_all | solution.py:262
  84.8 2.9 %copy-start.12 = (f32[6]{0:T(128)S(1)}, f32[6]{0:T(128)}, u32[]{:S(2)}) copy-start(f32[6]{0:T(128)} %param.29) | copy-start | bytes 76
  84.8 2.9 %copy-start.10 = (f32[6]{0:T(128)S(1)}, f32[6]{0:T(128)}, u32[]{:S(2)}) copy-start(f32[6]{0:T(128)} %param.28) | copy-start | bytes 76
  87.0 1.6 %copy-start.11 = (f32[6]{0:T(128)S(1)}, f32[6]{0:T(128)}, u32[]{:S(2)}) copy-start(f32[6]{0:T(128)} %param.30) | copy-start | bytes 76
  87.0 4.1 %copy-start.4 = (f32[4,384]{1,0:T(4,128)S(1)}, f32[4,384]{1,0:T(4,128)}, u32[]{:S(2)}) copy-start(f32[4,384]{1,0:T(4,128)} %param.24) | copy-start | bytes 18436
  87.0 4.1 %copy-start.5 = (f32[4,256]{1,0:T(4,128)S(1)}, f32[4,256]{1,0:T(4,128)}, u32[]{:S(2)}) copy-start(f32[4,256]{1,0:T(4,128)} %param.26) | copy-start | bytes 12292
  87.0 10.9 %copy-start.9 = (f32[256]{0:T(256)S(1)}, f32[256]{0:T(256)}, u32[]{:S(2)}) copy-start(f32[256]{0:T(256)} %param.27) | copy-start | bytes 3076
  97.9 5.0 %copy-start.6 = (f32[384]{0:T(512)S(1)}, f32[384]{0:T(512)}, u32[]{:S(2)}) copy-start(f32[384]{0:T(512)} %param.25) | copy-start | bytes 4612
  105.4 13.5 %copy-start.7 = (f32[384]{0:T(512)S(1)}, f32[384]{0:T(512)}, u32[]{:S(2)}) copy-start(f32[384]{0:T(512)} %param.31) | copy-start | bytes 4612

commit v6 on v5

--- a/solution.py
+++ b/solution.py
@@ -169,16 +169,62 @@
     )(x)
 
 
+def exchange_kernel(x_ref, out_ref, send_sem, recv_sem, local_sem, *, n):
+    me = lax.axis_index("req")
+    head = lax.axis_index("head")
+    barrier = pltpu.get_barrier_semaphore()
+    for k in range(1, n):
+        pl.semaphore_signal(
+            barrier, inc=1, device_id=(lax.rem(me + k, n), head), device_id_type=MESH
+        )
+    pl.semaphore_wait(barrier, n - 1)
+    own = pltpu.make_async_copy(x_ref.at[me], out_ref.at[me], local_sem.at[0])
+    own.start()
+    copies = []
+    for k in range(1, n):
+        peer = lax.rem(me + k, n)
+        copy = pltpu.make_async_remote_copy(
+            src_ref=x_ref.at[peer],
+            dst_ref=out_ref.at[me],
+            send_sem=send_sem.at[k - 1],
+            recv_sem=recv_sem.at[k - 1],
+            device_id=(peer, head),
+            device_id_type=MESH,
+        )
+        copy.start()
+        copies.append(copy)
+    own.wait()
+    for copy in copies:
+        copy.wait()
+
+
+def exchange(x, tag):
+    n = x.shape[0]
+    return pl.pallas_call(
+        functools.partial(exchange_kernel, n=n),
+        out_shape=jax.ShapeDtypeStruct(x.shape, x.dtype),
+        in_specs=[pl.BlockSpec(memory_space=pl.ANY)],
+        out_specs=pl.BlockSpec(memory_space=pl.ANY),
+        scratch_shapes=[
+            pltpu.SemaphoreType.DMA((n - 1,)),
+            pltpu.SemaphoreType.DMA((n - 1,)),
+            pltpu.SemaphoreType.DMA((1,)),
+        ],
+        compiler_params=pltpu.CompilerParams(collective_id=tag, has_side_effects=True),
+    )(x)
+
+
 def migrate(item, mig_dest, slot_count, groups, device):
     length = item.shape[0]
-    piece = -(-length // groups)
-    padded = jnp.pad(item, (0, piece * groups - length)).reshape(groups, piece)
-    first = lax.all_to_all(padded, "req", 0, 0, tiled=True)
+    lanes = 128
+    piece = -(-length // (groups * lanes)) * lanes
+    padded = jnp.pad(item, (0, piece * groups - length)).reshape(groups, piece // lanes, lanes)
+    first = exchange(padded, 1).reshape(groups, piece)
     dest_dev = mig_dest // slot_count
     order = invert(dest_dev, groups)
     pick = (order[:, None] == jnp.arange(groups, dtype=jnp.int32)[None, :]).astype(first.dtype)
     routed = jnp.dot(pick, first, preferred_element_type=jnp.float32).astype(first.dtype)
-    second = lax.all_to_all(routed, "req", 0, 0, tiled=True)
+    second = exchange(routed.reshape(groups, piece // lanes, lanes), 2)
     arrived = second.reshape(-1)[:length]
     target_local = mig_dest[order[device]] - device * slot_count
     return arrived, target_local
@@ -259,7 +305,7 @@
     send_buf = jnp.where(
         (send_idx == target_local)[:, None, None], arrived[None], packed[send_idx]
     )
-    received = lax.all_to_all(send_buf, "req", 0, 0, tiled=True)
+    received = exchange(send_buf, 3)
     moved = received[:, state_rows:][recv_rows]
     moved_inner = moved[:, :inner_edge_rows].reshape(edge_inner.shape)
     moved_shared = moved[:, inner_edge_rows:].reshape(edge_shared.shape)

time: 145 us -> 184 us (1.27)
  Pallas kernels: 29.4 us -> 98.5 us
  starting transfers between devices: 20.9 us -> 0 us
  waiting for transfers between devices: 7 us -> 0 us
  other arithmetic: 24.6 us -> 21.8 us
    pallas_call x0 -> x3, Pallas kernels: none -> 75.8 us  [exchange(): pl.pallas_call(functools.partial(exchange_kernel, n=n), out_shape=jax.Sha...]
    all_to_all x3 -> x0, starting transfers between devices: 20.9 us -> none  [the longest x1 7.62 us: migrate(): first = lax.all_to_all(padded, 'req', 0, 0, tiled=True)]
    all_to_all x3 -> x0, waiting for transfers between devices: 7 us -> none  [the longest x1 5.11 us: local(): received = lax.all_to_all(send_buf, 'req', 0, 0, tiled=True)]
    pallas_call x1, Pallas kernels: 18.8 us -> 12.1 us  [scatter_sum(): pl.pallas_call(functools.partial(scatter_sum_kernel, n=n, rows=rows), out...]
    all_to_all x3 -> x0, other arithmetic: 2.59 us -> none  [the longest x2 1.31 us: migrate(): second = lax.all_to_all(routed, 'req', 0, 0, tiled=True)]
    unnamed x35 -> x51, local copies, waits for them, and re-layouts: 7.26 us -> 5.31 us
  transfers between devices with their start and end apart: 3 -> 0, of which waited for: 2 -> 0; matrix products, arithmetic and copies ran while one was open for 15% -> 0% of each run, Pallas kernels for 0% -> 0%
where the time goes in v6:
time: 184 us; the launch traced here: 183 us
  Pallas kernels  98.5 us (54%)
  blocking collectives  29.1 us (16%)
  local copies, waits for them, and re-layouts  26.4 us (14%)
  other arithmetic  21.8 us (12%)
  between operations  4.71 us (3%)
  matrix products  2.71 us (1%)
    pallas_call x3, Pallas kernels, exchange(): pl.pallas_call(functools.partial(exchange_kernel, n=n), out_shape=jax.Sha...  75.8 us
    all_gather x1, blocking collectives, local(): piece_rows = lax.all_gather(normed, 'head', axis=0, tiled=True)  29.1 us
    pallas_call x1, Pallas kernels, scatter_sum(): pl.pallas_call(functools.partial(scatter_sum_kernel, n=n, rows=rows), out...  12.1 us
    pallas_call x1, Pallas kernels, recurrence(): pl.pallas_call(functools.partial(recurrence_kernel, group=group, window=w...  10.5 us
    unnamed x51, local copies, waits for them, and re-layouts  5.31 us
    gather x1, local copies, waits for them, and re-layouts, local(): packed[send_idx]  4.61 us
    select_n x1, other arithmetic, local(): jnp.where((send_idx == target_local)[:, None, None], arrived[None], packe...  3.94 us

profile of v6, /device:TPU:2, one launch (start us, length us, event | category | flops | bytes accessed | tf_op | source)
XLA Modules:
  0.0 183.2 jit_solution(9357458613802532091)
XLA Ops:
  0.7 1.3 dynamic_slice.31
  2.6 0.9 constant_dynamic-slice_fusion
  3.5 0.8 dynamic-slice_reduce_fusion
  4.3 0.7 dynamic-slice_reduce_fusion.1
  5.1 0.7 reshape.390.x_ref
  5.8 10.0 %shard_map.219 = bf16[32,13,128]{2,1,0:T(8,128)(2,1)} custom-call(bf16[32,13,128]{2,1,0:T(8,128)(2,1)} %reshape.390.x_ref), custom_call_target="tpu_custom_call" | custom-call | tf_op jit(solution)/shard_map/pallas_call | solution.py:203
  15.8 0.8 and_select_fusion.3
  16.6 0.2 convert_reduce_fusion.1
  16.7 1.3 compare_select_fusion.1
  18.2 1.1 convolution_convert_fusion.1
  19.3 0.8 reshape.392.x_ref
  20.1 9.1 %shard_map.220 = bf16[32,13,128]{2,1,0:T(8,128)(2,1)} custom-call(bf16[32,13,128]{2,1,0:T(8,128)(2,1)} %reshape.392.x_ref), custom_call_target="tpu_custom_call" | custom-call | tf_op jit(solution)/shard_map/pallas_call | solution.py:203
  29.2 1.0 slice.214
  30.1 0.6 dynamic_slice.29
  32.7 1.2 dynamic_slice.30
  34.6 0.9 select_reduce_fusion
  35.5 0.2 convert_reduce_fusion
  35.8 0.9 copy.103
  36.8 0.8 copy.104
  37.7 3.4 %pad_maximum_fusion = bf16[32,399,128]{2,1,0:T(8,128)(2,1)} fusion(bf16[32,6,128]{2,1,0:T(8,128)(2,1)S(1)} %reshape.395, bf16[32,9,128]{2,1,0:T(8,128)(2,1)S(1)} %reshape.394, bf16[32,384,128]{2,1,0:T(8,128)(2,1)} %bitcast.69), kind=kLoop, calls=%fused_computation.2 | loop fusion | flops 9805824 | bytes 6537216 | tf_op jit(solution)/shard_map/concatenate | solution.py:280
  41.2 4.6 %gather_fusion = bf16[32,399,128]{2,1,0:T(8,128)(2,1)} fusion(bf16[32,399,128]{2,1,0:T(8,128)(2,1)} %pad_maximum_fusion, s32[1024]{0:T(1024)S(1)} %pad_clamp_fusion.1), kind=kCustom, calls=%fused_computation | custom fusion | bytes 6537344 | tf_op jit(solution)/shard_map/gather | solution.py:306
  45.8 3.9 %broadcast_select_fusion.x_ref = bf16[32,399,128]{2,1,0:T(8,128)(2,1)} fusion(bf16[32,399,128]{2,1,0:T(8,128)(2,1)} %gather_fusion, pred[32]{0:T(512)(128)(4,1)S(1)} %broadcast_compare_fusion.3, bf16[399,128]{1,0:T(8,128)(2,1)S(1)} %slice.282), kind=kLoop, calls=%fused_computation.3 | loop fusion | flops 1634304 | bytes 6639392 | tf_op jit(solution)/shard_map/jit(_where)/select_n | solution.py:305
  49.7 56.7 %shard_map.221.refs_0_.refs_1_.refs_2_.refs_3_ = bf16[32,399,128]{2,1,0:T(8,128)(2,1)} custom-call(bf16[32,399,128]{2,1,0:T(8,128)(2,1)} %broadcast_select_fusion.x_ref), custom_call_target="tpu_custom_call" | custom-call | tf_op jit(solution)/shard_map/pallas_call | solution.py:203
  106.5 0.9 slice.216
  107.5 0.6 gather_fusion.1
  108.2 0.1 fusion.22
  108.4 29.1 %all_gather.3 = bf16[128,1536]{1,0:T(8,128)(2,1)S(1)} all-gather(bf16[16,1536]{1,0:T(8,128)(2,1)S(1)} %fusion.24), channel_id=1, replica_groups=mesh['req'=32,'head'=8] {'head'}, dimensions={0}, use_global_device_ids=true | all-gather | bytes 442368 | tf_op jit(solution)/shard_map/all_gather | solution.py:269
  137.5 0.4 convolution_convert_fusion.3
  137.9 0.1 copy.101
  138.2 0.2 divide_multiply_fusion.1
  138.4 0.4 fusion.53
  138.7 1.6 slice_reduce_fusion.9
  140.7 0.7 fusion.44
  141.5 0.1 reshape.442
  141.7 0.1 reshape.443
  141.9 2.1 %copy.125 = bf16[192,8,2,384]{3,1,2,0:T(8,128)(2,1)S(1)} copy(bf16[192,8,2,384]{3,2,1,0:T(2,128)(2,1)} %bitcast.70) | data formatting | bytes 4718592
  144.1 0.5 convolution_convert_fusion.2
  144.8 0.2 broadcast_in_dim.217
  145.0 0.1 reshape.398
  145.2 1.0 copy_multiply_fusion
  146.3 0.1 reshape.444
  146.4 0.2 fusion.61
  146.6 1.1 concatenate.31.refs_5_
  147.8 0.8 maximum_maximum_fusion.refs_4_
  148.7 10.5 %shard_map.222 = (f32[32,8,384]{2,1,0:T(8,128)}, bf16[32,384,128]{2,1,0:T(8,128)(2,1)}) custom-call(s32[32]{0:T(128)} %get-tuple-element.53.rows_ref, bf16[32,399,128]{2,1,0:T(8,128)(2,1)} %shard_map.221.refs_0_.refs_1_.refs_2_.refs_3_, bf16[32,399,128]{2,1,0:T(8,128)(2,1)} %shard_map.221.refs_0_.refs_1_.refs_2_.refs_3_, ...), custom_call_target="tpu_custom_call" | custom-call | tf_op jit(solution)/shard_map/pallas_call | solution.py:113
  159.3 0.1 reshape.447
  159.5 0.1 reshape.448
  159.8 0.1 reshape.449
  160.0 0.1 reshape.441
  160.3 1.4 fusion.42
  161.9 0.1 reshape.452
  162.6 0.1 reshape.450
  163.1 1.5 fusion.41
  164.7 0.3 select_convert_fusion
  165.1 0.4 convolution_convert_fusion
  165.7 0.1 copy.119
  165.8 0.8 fusion.1.x_ref
  166.6 12.1 %shard_map.223 = f32[16,1664]{1,0:T(8,128)} custom-call(bf16[128,1664]{1,0:T(8,128)(2,1)} %fusion.1.x_ref), custom_call_target="tpu_custom_call" | custom-call | tf_op jit(solution)/shard_map/pallas_call | solution.py:158
  178.8 1.0 rsqrt_reduce_fusion
  179.7 1.6 fusion.25
  181.3 0.4 fusion.29
  181.7 0.6 copy.120
  182.3 0.3 fusion.35
  182.6 0.6 copy.121
  (112 shorter events, 3.7 us)
Async XLA Ops:
  0.6 164.4 %copy-start = (bf16[384,1536]{1,0:T(8,128)(2,1)S(1)}, bf16[384,1536]{1,0:T(8,128)(2,1)}, u32[]{:S(2)}) copy-start(bf16[384,1536]{1,0:T(8,128)(2,1)} %param.32) | copy-start | bytes 3538948
  49.7 58.4 %copy-start.2 = (bf16[16,1536]{1,0:T(8,128)(2,1)S(1)}, bf16[16,1536]{1,0:T(8,128)(2,1)}, u32[]{:S(2)}) copy-start(bf16[16,1536]{1,0:T(8,128)(2,1)} %param.20) | copy-start | bytes 147460
  49.7 58.6 %copy-start.8 = (f32[1536]{0:T(1024)S(1)}, f32[1536]{0:T(1024)}, u32[]{:S(2)}) copy-start(f32[1536]{0:T(1024)} %param.21) | copy-start | bytes 18436
  49.7 87.7 %copy-start.1 = (bf16[1536,304]{0,1:T(8,128)(2,1)S(1)}, bf16[1536,304]{0,1:T(8,128)(2,1)}, u32[]{:S(2)}) copy-start(bf16[1536,304]{0,1:T(8,128)(2,1)} %param.23) | copy-start | bytes 2801668
  106.5 31.7 %copy-start.10 = (f32[4,256]{1,0:T(4,128)S(1)}, f32[4,256]{1,0:T(4,128)}, u32[]{:S(2)}) copy-start(f32[4,256]{1,0:T(4,128)} %param.26) | copy-start | bytes 12292
  106.5 31.7 %copy-start.19 = (f32[256]{0:T(256)S(1)}, f32[256]{0:T(256)}, u32[]{:S(2)}) copy-start(f32[256]{0:T(256)} %param.27) | copy-start | bytes 3076
  106.5 33.9 %copy-start.17 = (s32[32]{0:T(128)S(1)}, s32[32]{0:T(128)}, u32[]{:S(2)}) copy-start(s32[32]{0:T(128)} %param.36) | copy-start | bytes 388
  106.5 34.1 %copy-start.22 = (f32[6]{0:T(128)S(1)}, f32[6]{0:T(128)}, u32[]{:S(2)}) copy-start(f32[6]{0:T(128)} %param.29) | copy-start | bytes 76
  106.5 34.1 %copy-start.20 = (f32[6]{0:T(128)S(1)}, f32[6]{0:T(128)}, u32[]{:S(2)}) copy-start(f32[6]{0:T(128)} %param.28) | copy-start | bytes 76
  140.5 1.4 copy-start.6
  144.1 1.0 copy-start.9
  148.6 10.6 %copy-start.5 = (f32[32,6]{1,0:T(8,128)S(1)}, f32[32,6]{1,0:T(8,128)}, u32[]{:S(2)}) copy-start(f32[32,6]{1,0:T(8,128)} %get-tuple-element.73) | copy-start | bytes 2308
  148.6 10.8 %copy-start.4 = (f32[32,6]{1,0:T(8,128)S(1)}, f32[32,6]{1,0:T(8,128)}, u32[]{:S(2)}) copy-start(f32[32,6]{1,0:T(8,128)} %get-tuple-element.71) | copy-start | bytes 2308
  148.6 11.1 %copy-start.3 = (f32[32,6]{1,0:T(8,128)S(1)}, f32[32,6]{1,0:T(8,128)}, u32[]{:S(2)}) copy-start(f32[32,6]{1,0:T(8,128)} %get-tuple-element.67) | copy-start | bytes 2308
  148.6 11.5 %copy-start.21 = (f32[6]{0:T(128)S(1)}, f32[6]{0:T(128)}, u32[]{:S(2)}) copy-start(f32[6]{0:T(128)} %param.30) | copy-start | bytes 76
  148.6 11.7 %copy-start.15 = (f32[32]{0:T(128)S(1)}, f32[32]{0:T(128)}, u32[]{:S(2)}) copy-start(f32[32]{0:T(128)} %get-tuple-element.28) | copy-start | bytes 388
  148.6 11.7 %copy-start.16 = (f32[32]{0:T(128)S(1)}, f32[32]{0:T(128)}, u32[]{:S(2)}) copy-start(f32[32]{0:T(128)} %get-tuple-element.33) | copy-start | bytes 388
  148.6 13.1 %copy-start.14 = (f32[32]{0:T(128)S(1)}, f32[32]{0:T(128)}, u32[]{:S(2)}) copy-start(f32[32]{0:T(128)} %get-tuple-element.31) | copy-start | bytes 388
  159.2 3.9 %copy-start.12 = (f32[32]{0:T(128)S(1)}, f32[32]{0:T(128)}, u32[]{:S(2)}) copy-start(f32[32]{0:T(128)} %get-tuple-element.29) | copy-start | bytes 388
  159.2 3.9 %copy-start.13 = (f32[32]{0:T(128)S(1)}, f32[32]{0:T(128)}, u32[]{:S(2)}) copy-start(f32[32]{0:T(128)} %get-tuple-element.36) | copy-start | bytes 388
  159.2 5.5 %copy-start.7 = (pred[32,4]{1,0:T(8,128)(4,1)S(1)}, pred[32,4]{1,0:T(8,128)(4,1)}, u32[]{:S(2)}) copy-start(pred[32,4]{1,0:T(8,128)(4,1)} %copy-done.6) | copy-start | bytes 388
  159.2 5.5 %copy-start.11 = (f32[384]{0:T(512)S(1)}, f32[384]{0:T(512)}, u32[]{:S(2)}) copy-start(f32[384]{0:T(512)} %param.31) | copy-start | bytes 4612
  162.1 19.2 %copy-start.18 = (s32[32]{0:T(128)S(1)}, s32[32]{0:T(128)}, u32[]{:S(2)}) copy-start(s32[32]{0:T(128)} %param.36) | copy-start | bytes 388

commit v7 on v6

--- a/solution.py
+++ b/solution.py
@@ -302,10 +302,10 @@
     send_rows, recv_rows = route_rows(reorder, first_slot, slot_count, all_slots, stride)
     buffer_rows = groups * stride
     send_idx = invert(send_rows, buffer_rows)
-    send_buf = jnp.where(
-        (send_idx == target_local)[:, None, None], arrived[None], packed[send_idx]
-    )
-    received = exchange(send_buf, 3)
+    send_base = packed[send_idx]
+    target_row = lax.dynamic_index_in_dim(send_rows, target_local, 0, keepdims=False)
+    send_buf = lax.dynamic_update_slice(send_base, arrived[None], (target_row, 0, 0))
+    received = lax.all_to_all(send_buf, "req", 0, 0, tiled=True)
     moved = received[:, state_rows:][recv_rows]
     moved_inner = moved[:, :inner_edge_rows].reshape(edge_inner.shape)
     moved_shared = moved[:, inner_edge_rows:].reshape(edge_shared.shape)

time: 184 us -> 144 us (0.78)
  Pallas kernels: 98.5 us -> 48.5 us
  starting transfers between devices: 0 us -> 6.81 us
  waiting for transfers between devices: 0 us -> 4.88 us
  other arithmetic: 21.8 us -> 17.3 us
    pallas_call x3 -> x2, Pallas kernels: 75.8 us -> 19.1 us  [exchange(): pl.pallas_call(functools.partial(exchange_kernel, n=n), out_shape=jax.Sha...]
    all_to_all x0 -> x1, starting transfers between devices: none -> 6.81 us  [local(): received = lax.all_to_all(send_buf, 'req', 0, 0, tiled=True)]
    pallas_call x1, Pallas kernels: 12.1 us -> 18.9 us  [scatter_sum(): pl.pallas_call(functools.partial(scatter_sum_kernel, n=n, rows=rows), out...]
    all_to_all x0 -> x1, waiting for transfers between devices: none -> 4.88 us  [local(): received = lax.all_to_all(send_buf, 'req', 0, 0, tiled=True)]
    select_n x2 -> x1, other arithmetic: 3.95 us -> 0.01 us  [local(): send_base = packed[send_idx]]
    unnamed x51 -> x31, local copies, waits for them, and re-layouts: 5.31 us -> 5.29 us
  transfers between devices with their start and end apart: 0 -> 1, of which waited for: 0 -> 1; matrix products, arithmetic and copies ran while one was open for 0% -> 5% of each run, Pallas kernels for 0% -> 0%
where the time goes in v7:
time: 144 us; the launch traced here: 143 us
  Pallas kernels  48.5 us (34%)
  blocking collectives  28.9 us (20%)
  local copies, waits for them, and re-layouts  27 us (19%)
  other arithmetic  17.3 us (12%)
  starting transfers between devices  6.81 us (5%)
  between operations  6.55 us (5%)
  waiting for transfers between devices  4.88 us (3%)
  matrix products  2.71 us (2%)
    all_gather x1, blocking collectives, local(): piece_rows = lax.all_gather(normed, 'head', axis=0, tiled=True)  28.9 us
    pallas_call x2, Pallas kernels, exchange(): pl.pallas_call(functools.partial(exchange_kernel, n=n), out_shape=jax.Sha...  19.1 us
    pallas_call x1, Pallas kernels, scatter_sum(): pl.pallas_call(functools.partial(scatter_sum_kernel, n=n, rows=rows), out...  18.9 us
    pallas_call x1, Pallas kernels, recurrence(): pl.pallas_call(functools.partial(recurrence_kernel, group=group, window=w...  10.5 us
    all_to_all x1, starting transfers between devices, local(): received = lax.all_to_all(send_buf, 'req', 0, 0, tiled=True)  6.81 us
    unnamed x31, local copies, waits for them, and re-layouts  5.29 us
    all_to_all x1, waiting for transfers between devices, local(): received = lax.all_to_all(send_buf, 'req', 0, 0, tiled=True)  4.88 us
    gather x1, local copies, waits for them, and re-layouts, local(): send_base = packed[send_idx]  4.61 us
  transfers between devices with their start and end apart: 1, of which 1 were waited for; matrix products, arithmetic and copies ran while one was open for 5% of the time, Pallas kernels for 0%

profile of v7, /device:TPU:2, one launch (start us, length us, event | category | flops | bytes accessed | tf_op | source)
XLA Modules:
  0.0 142.6 jit_solution(8630057204983111543)
XLA Ops:
  0.7 1.0 select_reduce_fusion
  1.6 0.7 and_select_fusion.1
  2.4 0.6 dynamic_slice.37
  5.0 1.2 dynamic_slice.38
  6.9 0.2 convert_reduce_fusion
  7.0 0.6 dynamic_slice.39
  8.9 1.2 dynamic_slice.33
  10.9 0.9 copy.103
  11.9 0.8 dynamic-slice_reduce_fusion
  12.6 0.7 dynamic-slice_reduce_fusion.1
  13.4 0.8 copy.104
  14.2 0.9 constant_dynamic-slice_fusion
  15.2 0.7 reshape.389.x_ref
  15.9 10.0 %shard_map.219 = bf16[32,13,128]{2,1,0:T(8,128)(2,1)} custom-call(bf16[32,13,128]{2,1,0:T(8,128)(2,1)} %reshape.389.x_ref), custom_call_target="tpu_custom_call" | custom-call | tf_op jit(solution)/shard_map/pallas_call | solution.py:203
  25.9 1.1 convolution_convert_fusion.1
  27.0 0.8 reshape.391.x_ref
  27.8 9.1 %shard_map.220 = bf16[32,13,128]{2,1,0:T(8,128)(2,1)} custom-call(bf16[32,13,128]{2,1,0:T(8,128)(2,1)} %reshape.391.x_ref), custom_call_target="tpu_custom_call" | custom-call | tf_op jit(solution)/shard_map/pallas_call | solution.py:203
  36.9 1.0 reshape.392
  38.6 3.4 %pad_maximum_fusion = bf16[32,399,128]{2,1,0:T(8,128)(2,1)} fusion(bf16[32,6,128]{2,1,0:T(8,128)(2,1)S(1)} %reshape.385, bf16[32,9,128]{2,1,0:T(8,128)(2,1)S(1)} %reshape.384, bf16[32,384,128]{2,1,0:T(8,128)(2,1)} %bitcast.74), kind=kLoop, calls=%fused_computation.2 | loop fusion | flops 9805824 | bytes 6537216 | tf_op jit(solution)/shard_map/concatenate | solution.py:280
  42.1 4.6 %gather_fusion = bf16[32,399,128]{2,1,0:T(8,128)(2,1)} fusion(bf16[32,399,128]{2,1,0:T(8,128)(2,1)} %pad_maximum_fusion, s32[1024]{0:T(1024)S(1)} %pad_clamp_fusion.1), kind=kCustom, calls=%fused_computation | custom fusion | bytes 6537344 | tf_op jit(solution)/shard_map/gather | solution.py:305
  46.7 0.7 fusion.22
  47.3 6.8 %all-to-all-start = ((bf16[32,399,128]{2,1,0:T(8,128)(2,1)}), bf16[32,399,128]{2,1,0:T(8,128)(2,1)}, u32[]{:S(2)}, u32[]{:S(2)}) async-start(bf16[32,399,128]{2,1,0:T(8,128)(2,1)} %fusion.22), calls=%async_computation | async-start | bytes 6553600 | tf_op jit(solution)/shard_map/all_to_all | solution.py:308
  54.2 0.1 fusion.23
  54.4 28.9 %all_gather.3 = bf16[128,1536]{1,0:T(8,128)(2,1)S(1)} all-gather(bf16[16,1536]{1,0:T(8,128)(2,1)S(1)} %fusion.25), channel_id=1, replica_groups=mesh['req'=32,'head'=8] {'head'}, dimensions={0}, use_global_device_ids=true | all-gather | bytes 442368 | tf_op jit(solution)/shard_map/all_gather | solution.py:269
  83.3 0.4 convolution_convert_fusion.3
  83.7 0.1 copy.101
  84.1 2.2 %copy.125 = bf16[192,8,2,384]{3,1,2,0:T(8,128)(2,1)S(1)} copy(bf16[192,8,2,384]{3,2,1,0:T(2,128)(2,1)} %bitcast.75) | data formatting | bytes 4718592
  86.3 0.5 convolution_convert_fusion.2
  87.1 0.2 broadcast_in_dim.198
  87.3 0.1 reshape.395
  87.6 0.1 reshape.441
  87.8 0.1 reshape.438
  88.1 0.8 and_select_fusion.3
  88.9 0.2 convert_reduce_fusion.1
  89.1 1.3 compare_select_fusion.1
  90.5 4.9 %all-to-all-done.refs_0_.refs_1_.refs_2_.refs_3_ = bf16[32,399,128]{2,1,0:T(8,128)(2,1)} async-done(((bf16[32,399,128]{2,1,0:T(8,128)(2,1)}), bf16[32,399,128]{2,1,0:T(8,128)(2,1)}, u32[]{:S(2)}, u32[]{:S(2)}) %all-to-all-start) | async-done | bytes 3268640 | tf_op jit(solution)/shard_map/all_to_all | solution.py:308
  95.3 0.9 slice.279
  96.3 0.6 gather_fusion.1
  97.0 0.2 divide_multiply_fusion.1
  97.2 0.3 fusion.54
  97.8 0.4 fusion.30
  98.1 0.3 fusion.36
  98.4 1.0 slice_reduce_fusion.9
  99.6 0.1 reshape.439
  99.8 0.1 reshape.440
  100.5 0.1 reshape.446
  100.8 0.1 reshape.449
  101.5 0.1 reshape.447
  102.0 0.3 copy_multiply_fusion
  102.3 0.2 fusion.62
  102.5 0.8 maximum_maximum_fusion.refs_4_
  103.3 1.1 concatenate.31.refs_5_
  104.5 10.5 %shard_map.221 = (f32[32,8,384]{2,1,0:T(8,128)}, bf16[32,384,128]{2,1,0:T(8,128)(2,1)}) custom-call(s32[32]{0:T(128)} %get-tuple-element.53.rows_ref, bf16[32,399,128]{2,1,0:T(8,128)(2,1)} %all-to-all-done.refs_0_.refs_1_.refs_2_.refs_3_, bf16[32,399,128]{2,1,0:T(8,128)(2,1)} %all-to-all-done.refs_0_.refs_1_.refs_2_.refs_3_, ...), custom_call_target="tpu_custom_call" | custom-call | tf_op jit(solution)/shard_map/pallas_call | solution.py:113
  115.0 1.4 fusion.43
  116.4 1.5 %fusion.42 = (f32[32,1,384]{2,1,0:T(1,128)S(1)}, f32[32,1,384]{2,1,0:T(1,128)S(1)}) fusion(f32[32,4,384]{2,1,0:T(4,128)S(1)} %get-tuple-element.45, f32[32,1,384]{2,1,0:T(1,128)S(1)} %reshape.443, f32[32,1,384]{2,1,0:T(1,128)S(1)} %reshape.442, f32[32,8,384]{2,1,0:T(8,128)} %get-tuple-element.6, f32[32]{0:T(128)S(1)} %get-tuple-element.36, f32[384]{0:T(512)S(1)} %mul.376, ...), kind=kLoop, calls=%fused_computation.87 | loop fusion | flops 221184 | bytes 788224 | tf_op jit(solution)/shard_map/add | solution.py:366
  117.9 0.3 select_convert_fusion
  118.6 0.1 copy.119
  118.7 0.4 convolution_convert_fusion
  119.1 0.8 fusion.1.x_ref
  119.9 18.9 %shard_map.222 = f32[16,1664]{1,0:T(8,128)} custom-call(bf16[128,1664]{1,0:T(8,128)(2,1)} %fusion.1.x_ref), custom_call_target="tpu_custom_call" | custom-call | tf_op jit(solution)/shard_map/pallas_call | solution.py:158
  138.8 1.0 rsqrt_reduce_fusion
  139.7 1.6 %fusion.26 = bf16[16,1536]{1,0:T(8,128)(2,1)} fusion(bf16[16,1536]{1,0:T(8,128)(2,1)S(1)} %copy-done.2, f32[16,1664]{1,0:T(8,128)} %shard_map.222, f32[16]{0:T(128)S(1)} %rsqrt_reduce_fusion), kind=kLoop, calls=%fused_computation.67 | loop fusion | flops 98304 | bytes 196672 | tf_op jit(solution)/shard_map/convert_element_type | solution.py:388
  141.3 0.6 copy.120
  142.0 0.6 copy.121
  (92 shorter events, 4.0 us)
Async XLA Ops:
  0.6 118.1 %copy-start = (bf16[384,1536]{1,0:T(8,128)(2,1)S(1)}, bf16[384,1536]{1,0:T(8,128)(2,1)}, u32[]{:S(2)}) copy-start(bf16[384,1536]{1,0:T(8,128)(2,1)} %param.32) | copy-start | bytes 3538948
  47.3 6.8 %copy-start.2 = (bf16[16,1536]{1,0:T(8,128)(2,1)S(1)}, bf16[16,1536]{1,0:T(8,128)(2,1)}, u32[]{:S(2)}) copy-start(bf16[16,1536]{1,0:T(8,128)(2,1)} %param.20) | copy-start | bytes 147460
  47.3 7.0 %copy-start.3 = (f32[1536]{0:T(1024)S(1)}, f32[1536]{0:T(1024)}, u32[]{:S(2)}) copy-start(f32[1536]{0:T(1024)} %param.21) | copy-start | bytes 18436
  47.3 35.9 %copy-start.1 = (bf16[1536,304]{0,1:T(8,128)(2,1)S(1)}, bf16[1536,304]{0,1:T(8,128)(2,1)}, u32[]{:S(2)}) copy-start(bf16[1536,304]{0,1:T(8,128)(2,1)} %param.23) | copy-start | bytes 2801668
  47.3 36.6 %copy-start.8 = (s32[32]{0:T(128)S(1)}, s32[32]{0:T(128)}, u32[]{:S(2)}) copy-start(s32[32]{0:T(128)} %param.36) | copy-start | bytes 388
  47.3 48.0 %all-to-all-start = ((bf16[32,399,128]{2,1,0:T(8,128)(2,1)}), bf16[32,399,128]{2,1,0:T(8,128)(2,1)}, u32[]{:S(2)}, u32[]{:S(2)}) async-start(bf16[32,399,128]{2,1,0:T(8,128)(2,1)} %fusion.22), calls=%async_computation | async-start | bytes 6553600 | tf_op jit(solution)/shard_map/all_to_all | solution.py:308
  84.1 2.9 %copy-start.12 = (f32[6]{0:T(128)S(1)}, f32[6]{0:T(128)}, u32[]{:S(2)}) copy-start(f32[6]{0:T(128)} %param.29) | copy-start | bytes 76
  84.1 2.9 %copy-start.10 = (f32[6]{0:T(128)S(1)}, f32[6]{0:T(128)}, u32[]{:S(2)}) copy-start(f32[6]{0:T(128)} %param.28) | copy-start | bytes 76
  86.3 1.6 %copy-start.11 = (f32[6]{0:T(128)S(1)}, f32[6]{0:T(128)}, u32[]{:S(2)}) copy-start(f32[6]{0:T(128)} %param.30) | copy-start | bytes 76
  86.3 4.1 %copy-start.4 = (f32[4,384]{1,0:T(4,128)S(1)}, f32[4,384]{1,0:T(4,128)}, u32[]{:S(2)}) copy-start(f32[4,384]{1,0:T(4,128)} %param.24) | copy-start | bytes 18436
  86.3 4.1 %copy-start.5 = (f32[4,256]{1,0:T(4,128)S(1)}, f32[4,256]{1,0:T(4,128)}, u32[]{:S(2)}) copy-start(f32[4,256]{1,0:T(4,128)} %param.26) | copy-start | bytes 12292
  86.3 10.7 %copy-start.9 = (f32[256]{0:T(256)S(1)}, f32[256]{0:T(256)}, u32[]{:S(2)}) copy-start(f32[256]{0:T(256)} %param.27) | copy-start | bytes 3076
  97.0 5.0 %copy-start.6 = (f32[384]{0:T(512)S(1)}, f32[384]{0:T(512)}, u32[]{:S(2)}) copy-start(f32[384]{0:T(512)} %param.25) | copy-start | bytes 4612
  104.5 13.5 %copy-start.7 = (f32[384]{0:T(512)S(1)}, f32[384]{0:T(512)}, u32[]{:S(2)}) copy-start(f32[384]{0:T(512)} %param.31) | copy-start | bytes 4612

commit v8 on v7

--- a/solution.py
+++ b/solution.py
@@ -90,7 +90,7 @@
             )
 
 
-def recurrence(received, rows, mix, weight, state_rows, heads, group=4):
+def recurrence(received, rows, mix, weight, state_rows, heads, group=8):
     slot_count, _, lanes = received.shape
     window = mix.shape[1] // 4
     held_specs = [

time: 144 us -> 143 us (level)
  no operation moved by 1% of the time
where the time goes in v8:
time: 143 us; the launch traced here: 142 us
  Pallas kernels  47.9 us (33%)
  blocking collectives  28.9 us (20%)
  local copies, waits for them, and re-layouts  26.9 us (19%)
  other arithmetic  17.3 us (12%)
  starting transfers between devices  6.8 us (5%)
  between operations  6.55 us (5%)
  waiting for transfers between devices  4.88 us (3%)
  matrix products  2.71 us (2%)
    all_gather x1, blocking collectives, local(): piece_rows = lax.all_gather(normed, 'head', axis=0, tiled=True)  28.9 us
    pallas_call x2, Pallas kernels, exchange(): pl.pallas_call(functools.partial(exchange_kernel, n=n), out_shape=jax.Sha...  19.1 us
    pallas_call x1, Pallas kernels, scatter_sum(): pl.pallas_call(functools.partial(scatter_sum_kernel, n=n, rows=rows), out...  18.9 us
    pallas_call x1, Pallas kernels, recurrence(): pl.pallas_call(functools.partial(recurrence_kernel, group=group, window=w...  9.93 us
    all_to_all x1, starting transfers between devices, local(): received = lax.all_to_all(send_buf, 'req', 0, 0, tiled=True)  6.8 us
    unnamed x31, local copies, waits for them, and re-layouts  5.29 us
    all_to_all x1, waiting for transfers between devices, local(): received = lax.all_to_all(send_buf, 'req', 0, 0, tiled=True)  4.88 us
    gather x1, local copies, waits for them, and re-layouts, local(): send_base = packed[send_idx]  4.61 us
  transfers between devices with their start and end apart: 1, of which 1 were waited for; matrix products, arithmetic and copies ran while one was open for 5% of the time, Pallas kernels for 0%

profile of v8, /device:TPU:2, one launch (start us, length us, event | category | flops | bytes accessed | tf_op | source)
XLA Modules:
  0.0 142.0 jit_solution(10609464628856837417)
XLA Ops:
  0.7 1.0 select_reduce_fusion
  1.6 0.7 and_select_fusion.1
  2.4 0.6 dynamic_slice.37
  5.0 1.2 dynamic_slice.38
  6.9 0.2 convert_reduce_fusion
  7.0 0.6 dynamic_slice.39
  8.9 1.2 dynamic_slice.33
  10.9 0.9 copy.103
  11.9 0.8 dynamic-slice_reduce_fusion
  12.6 0.7 dynamic-slice_reduce_fusion.1
  13.4 0.8 copy.104
  14.2 0.9 constant_dynamic-slice_fusion
  15.2 0.7 reshape.389.x_ref
  15.9 10.0 %shard_map.219 = bf16[32,13,128]{2,1,0:T(8,128)(2,1)} custom-call(bf16[32,13,128]{2,1,0:T(8,128)(2,1)} %reshape.389.x_ref), custom_call_target="tpu_custom_call" | custom-call | tf_op jit(solution)/shard_map/pallas_call | solution.py:203
  25.9 1.1 convolution_convert_fusion.1
  27.0 0.8 reshape.391.x_ref
  27.8 9.1 %shard_map.220 = bf16[32,13,128]{2,1,0:T(8,128)(2,1)} custom-call(bf16[32,13,128]{2,1,0:T(8,128)(2,1)} %reshape.391.x_ref), custom_call_target="tpu_custom_call" | custom-call | tf_op jit(solution)/shard_map/pallas_call | solution.py:203
  36.9 1.0 reshape.392
  38.6 3.4 %pad_maximum_fusion = bf16[32,399,128]{2,1,0:T(8,128)(2,1)} fusion(bf16[32,6,128]{2,1,0:T(8,128)(2,1)S(1)} %reshape.385, bf16[32,9,128]{2,1,0:T(8,128)(2,1)S(1)} %reshape.384, bf16[32,384,128]{2,1,0:T(8,128)(2,1)} %bitcast.74), kind=kLoop, calls=%fused_computation.2 | loop fusion | flops 9805824 | bytes 6537216 | tf_op jit(solution)/shard_map/concatenate | solution.py:280
  42.1 4.6 %gather_fusion = bf16[32,399,128]{2,1,0:T(8,128)(2,1)} fusion(bf16[32,399,128]{2,1,0:T(8,128)(2,1)} %pad_maximum_fusion, s32[1024]{0:T(1024)S(1)} %pad_clamp_fusion.1), kind=kCustom, calls=%fused_computation | custom fusion | bytes 6537344 | tf_op jit(solution)/shard_map/gather | solution.py:305
  46.7 0.6 fusion.22
  47.3 6.8 %all-to-all-start = ((bf16[32,399,128]{2,1,0:T(8,128)(2,1)}), bf16[32,399,128]{2,1,0:T(8,128)(2,1)}, u32[]{:S(2)}, u32[]{:S(2)}) async-start(bf16[32,399,128]{2,1,0:T(8,128)(2,1)} %fusion.22), calls=%async_computation | async-start | bytes 6553600 | tf_op jit(solution)/shard_map/all_to_all | solution.py:308
  54.1 0.1 fusion.23
  54.4 28.9 %all_gather.3 = bf16[128,1536]{1,0:T(8,128)(2,1)S(1)} all-gather(bf16[16,1536]{1,0:T(8,128)(2,1)S(1)} %fusion.25), channel_id=1, replica_groups=mesh['req'=32,'head'=8] {'head'}, dimensions={0}, use_global_device_ids=true | all-gather | bytes 442368 | tf_op jit(solution)/shard_map/all_gather | solution.py:269
  83.3 0.4 convolution_convert_fusion.3
  83.7 0.1 copy.101
  84.1 2.2 %copy.125 = bf16[192,8,2,384]{3,1,2,0:T(8,128)(2,1)S(1)} copy(bf16[192,8,2,384]{3,2,1,0:T(2,128)(2,1)} %bitcast.75) | data formatting | bytes 4718592
  86.3 0.5 convolution_convert_fusion.2
  87.1 0.2 broadcast_in_dim.198
  87.3 0.1 reshape.395
  87.6 0.1 reshape.441
  87.8 0.1 reshape.438
  88.1 0.8 and_select_fusion.3
  88.9 0.2 convert_reduce_fusion.1
  89.1 1.3 compare_select_fusion.1
  90.4 4.9 %all-to-all-done.refs_0_.refs_1_.refs_2_.refs_3_.refs_4_.refs_5_.refs_6_.refs_7_ = bf16[32,399,128]{2,1,0:T(8,128)(2,1)} async-done(((bf16[32,399,128]{2,1,0:T(8,128)(2,1)}), bf16[32,399,128]{2,1,0:T(8,128)(2,1)}, u32[]{:S(2)}, u32[]{:S(2)}) %all-to-all-start) | async-done | bytes 3268640 | tf_op jit(solution)/shard_map/all_to_all | solution.py:308
  95.3 0.9 slice.279
  96.2 0.6 gather_fusion.1
  97.0 0.2 divide_multiply_fusion.1
  97.2 0.3 fusion.54
  97.8 0.4 fusion.30
  98.1 0.3 fusion.36
  98.4 1.0 slice_reduce_fusion.9
  100.0 0.1 reshape.444
  100.8 0.1 reshape.449
  101.0 0.1 reshape.442
  101.4 0.1 reshape.447
  101.7 0.1 reshape.448
  102.0 0.3 copy_multiply_fusion
  102.3 0.2 fusion.62
  102.5 0.8 maximum_maximum_fusion.refs_8_
  103.3 1.1 concatenate.31.refs_9_
  104.4 9.9 %shard_map.221 = (f32[32,8,384]{2,1,0:T(8,128)}, bf16[32,384,128]{2,1,0:T(8,128)(2,1)}) custom-call(s32[32]{0:T(128)} %get-tuple-element.53.rows_ref, bf16[32,399,128]{2,1,0:T(8,128)(2,1)} %all-to-all-done.refs_0_.refs_1_.refs_2_.refs_3_.refs_4_.refs_5_.refs_6_.refs_7_, ...), custom_call_target="tpu_custom_call" | custom-call | tf_op jit(solution)/shard_map/pallas_call | solution.py:113
  114.4 1.4 fusion.43
  115.8 1.5 %fusion.42 = (f32[32,1,384]{2,1,0:T(1,128)S(1)}, f32[32,1,384]{2,1,0:T(1,128)S(1)}) fusion(f32[32,4,384]{2,1,0:T(4,128)S(1)} %get-tuple-element.45, f32[32,1,384]{2,1,0:T(1,128)S(1)} %reshape.443, f32[32,1,384]{2,1,0:T(1,128)S(1)} %reshape.442, f32[32,8,384]{2,1,0:T(8,128)} %get-tuple-element.6, f32[32]{0:T(128)S(1)} %get-tuple-element.36, f32[384]{0:T(512)S(1)} %mul.376, ...), kind=kLoop, calls=%fused_computation.87 | loop fusion | flops 221184 | bytes 788224 | tf_op jit(solution)/shard_map/add | solution.py:366
  117.3 0.3 select_convert_fusion
  117.9 0.1 copy.119
  118.1 0.4 convolution_convert_fusion
  118.5 0.8 fusion.1.x_ref
  119.2 18.9 %shard_map.222 = f32[16,1664]{1,0:T(8,128)} custom-call(bf16[128,1664]{1,0:T(8,128)(2,1)} %fusion.1.x_ref), custom_call_target="tpu_custom_call" | custom-call | tf_op jit(solution)/shard_map/pallas_call | solution.py:158
  138.2 1.0 rsqrt_reduce_fusion
  139.1 1.6 %fusion.26 = bf16[16,1536]{1,0:T(8,128)(2,1)} fusion(bf16[16,1536]{1,0:T(8,128)(2,1)S(1)} %copy-done.2, f32[16,1664]{1,0:T(8,128)} %shard_map.222, f32[16]{0:T(128)S(1)} %rsqrt_reduce_fusion), kind=kLoop, calls=%fused_computation.67 | loop fusion | flops 98304 | bytes 196672 | tf_op jit(solution)/shard_map/convert_element_type | solution.py:388
  140.7 0.6 copy.120
  141.4 0.6 copy.121
  (92 shorter events, 4.0 us)
Async XLA Ops:
  0.6 117.5 %copy-start = (bf16[384,1536]{1,0:T(8,128)(2,1)S(1)}, bf16[384,1536]{1,0:T(8,128)(2,1)}, u32[]{:S(2)}) copy-start(bf16[384,1536]{1,0:T(8,128)(2,1)} %param.32) | copy-start | bytes 3538948
  47.3 6.8 %copy-start.2 = (bf16[16,1536]{1,0:T(8,128)(2,1)S(1)}, bf16[16,1536]{1,0:T(8,128)(2,1)}, u32[]{:S(2)}) copy-start(bf16[16,1536]{1,0:T(8,128)(2,1)} %param.20) | copy-start | bytes 147460
  47.3 7.0 %copy-start.3 = (f32[1536]{0:T(1024)S(1)}, f32[1536]{0:T(1024)}, u32[]{:S(2)}) copy-start(f32[1536]{0:T(1024)} %param.21) | copy-start | bytes 18436
  47.3 35.9 %copy-start.1 = (bf16[1536,304]{0,1:T(8,128)(2,1)S(1)}, bf16[1536,304]{0,1:T(8,128)(2,1)}, u32[]{:S(2)}) copy-start(bf16[1536,304]{0,1:T(8,128)(2,1)} %param.23) | copy-start | bytes 2801668
  47.3 36.6 %copy-start.8 = (s32[32]{0:T(128)S(1)}, s32[32]{0:T(128)}, u32[]{:S(2)}) copy-start(s32[32]{0:T(128)} %param.36) | copy-start | bytes 388
  47.3 48.0 %all-to-all-start = ((bf16[32,399,128]{2,1,0:T(8,128)(2,1)}), bf16[32,399,128]{2,1,0:T(8,128)(2,1)}, u32[]{:S(2)}, u32[]{:S(2)}) async-start(bf16[32,399,128]{2,1,0:T(8,128)(2,1)} %fusion.22), calls=%async_computation | async-start | bytes 6553600 | tf_op jit(solution)/shard_map/all_to_all | solution.py:308
  84.1 2.9 %copy-start.12 = (f32[6]{0:T(128)S(1)}, f32[6]{0:T(128)}, u32[]{:S(2)}) copy-start(f32[6]{0:T(128)} %param.29) | copy-start | bytes 76
  84.1 2.9 %copy-start.10 = (f32[6]{0:T(128)S(1)}, f32[6]{0:T(128)}, u32[]{:S(2)}) copy-start(f32[6]{0:T(128)} %param.28) | copy-start | bytes 76
  86.3 1.6 %copy-start.11 = (f32[6]{0:T(128)S(1)}, f32[6]{0:T(128)}, u32[]{:S(2)}) copy-start(f32[6]{0:T(128)} %param.30) | copy-start | bytes 76
  86.3 4.1 %copy-start.4 = (f32[4,384]{1,0:T(4,128)S(1)}, f32[4,384]{1,0:T(4,128)}, u32[]{:S(2)}) copy-start(f32[4,384]{1,0:T(4,128)} %param.24) | copy-start | bytes 18436
  86.3 4.1 %copy-start.5 = (f32[4,256]{1,0:T(4,128)S(1)}, f32[4,256]{1,0:T(4,128)}, u32[]{:S(2)}) copy-start(f32[4,256]{1,0:T(4,128)} %param.26) | copy-start | bytes 12292
  86.3 10.7 %copy-start.9 = (f32[256]{0:T(256)S(1)}, f32[256]{0:T(256)}, u32[]{:S(2)}) copy-start(f32[256]{0:T(256)} %param.27) | copy-start | bytes 3076
  97.0 5.0 %copy-start.6 = (f32[384]{0:T(512)S(1)}, f32[384]{0:T(512)}, u32[]{:S(2)}) copy-start(f32[384]{0:T(512)} %param.25) | copy-start | bytes 4612
  104.4 12.9 %copy-start.7 = (f32[384]{0:T(512)S(1)}, f32[384]{0:T(512)}, u32[]{:S(2)}) copy-start(f32[384]{0:T(512)} %param.31) | copy-start | bytes 4612

commit v9 on v8

--- a/solution.py
+++ b/solution.py
@@ -226,7 +226,7 @@
     routed = jnp.dot(pick, first, preferred_element_type=jnp.float32).astype(first.dtype)
     second = exchange(routed.reshape(groups, piece // lanes, lanes), 2)
     arrived = second.reshape(-1)[:length]
-    target_local = mig_dest[order[device]] - device * slot_count
+    target_local = jnp.sum(jnp.where(dest_dev == device, mig_dest, 0)) - device * slot_count
     return arrived, target_local
 
 
@@ -288,7 +288,7 @@
     row_total = packed.shape[1]
 
     moving = mig_ids.shape[0] // groups
-    own_id = mig_ids[device * moving]
+    own_id = jnp.sum(jnp.where(jnp.arange(mig_ids.shape[0]) == device * moving, mig_ids, 0))
     mig_local = own_id - first_slot
     item = jnp.concatenate(
         [
@@ -303,7 +303,7 @@
     buffer_rows = groups * stride
     send_idx = invert(send_rows, buffer_rows)
     send_base = packed[send_idx]
-    target_row = lax.dynamic_index_in_dim(send_rows, target_local, 0, keepdims=False)
+    target_row = jnp.sum(jnp.where(jnp.arange(slot_count) == target_local, send_rows, 0))
     send_buf = lax.dynamic_update_slice(send_base, arrived[None], (target_row, 0, 0))
     received = lax.all_to_all(send_buf, "req", 0, 0, tiled=True)
     moved = received[:, state_rows:][recv_rows]

time: 143 us -> 139 us (0.972)
  local copies, waits for them, and re-layouts: 26.9 us -> 23.3 us
  between operations: 6.55 us -> 4.58 us
  waiting for transfers between devices: 4.88 us -> 6.41 us
    dynamic_slice x4 -> x0, local copies, waits for them, and re-layouts: 3.66 us -> none  [the longest x2 1.83 us: migrate(): target_local = mig_dest[order[device]] - device * slot_count]
    reduce_sum x0 -> x2, other arithmetic: none -> 2.05 us  [the longest x1 1.41 us: migrate(): jnp.sum(jnp.where(dest_dev == device, mig_dest, 0)) - device * slot_count]
    all_to_all x1, waiting for transfers between devices: 4.88 us -> 6.41 us  [local(): received = lax.all_to_all(send_buf, 'req', 0, 0, tiled=True)]
  transfers between devices with their start and end apart: 1 -> 1, of which waited for: 1 -> 1; matrix products, arithmetic and copies ran while one was open for 5% -> 4% of each run, Pallas kernels for 0% -> 0%
where the time goes in v9:
time: 139 us; the launch traced here: 138 us
  Pallas kernels  47.9 us (34%)
  blocking collectives  28.9 us (21%)
  local copies, waits for them, and re-layouts  23.3 us (17%)
  other arithmetic  17.8 us (13%)
  starting transfers between devices  6.82 us (5%)
  waiting for transfers between devices  6.41 us (5%)
  between operations  4.58 us (3%)
  matrix products  2.71 us (2%)
    all_gather x1, blocking collectives, local(): piece_rows = lax.all_gather(normed, 'head', axis=0, tiled=True)  28.9 us
    pallas_call x2, Pallas kernels, exchange(): pl.pallas_call(functools.partial(exchange_kernel, n=n), out_shape=jax.Sha...  19.1 us
    pallas_call x1, Pallas kernels, scatter_sum(): pl.pallas_call(functools.partial(scatter_sum_kernel, n=n, rows=rows), out...  18.9 us
    pallas_call x1, Pallas kernels, recurrence(): pl.pallas_call(functools.partial(recurrence_kernel, group=group, window=w...  9.93 us
    all_to_all x1, starting transfers between devices, local(): received = lax.all_to_all(send_buf, 'req', 0, 0, tiled=True)  6.82 us
    all_to_all x1, waiting for transfers between devices, local(): received = lax.all_to_all(send_buf, 'req', 0, 0, tiled=True)  6.41 us
    unnamed x31, local copies, waits for them, and re-layouts  5.29 us
    gather x1, local copies, waits for them, and re-layouts, local(): send_base = packed[send_idx]  4.61 us
  transfers between devices with their start and end apart: 1, of which 1 were waited for; matrix products, arithmetic and copies ran while one was open for 4% of the time, Pallas kernels for 0%

profile of v9, /device:TPU:2, one launch (start us, length us, event | category | flops | bytes accessed | tf_op | source)
XLA Modules:
  0.0 138.4 jit_solution(14548857807685955709)
XLA Ops:
  0.7 1.4 %fusion.53 = (s32[]{:T(128)}, s32[32]{0:T(128)S(1)}, s32[]{:T(128)}) fusion(s32[32]{0:T(128)} %param.38, s32[]{:T(128)S(6)} %axis_index.25, s32[32]{0:T(128)} %param.37), kind=kLoop, calls=%fused_computation.156 | loop fusion | flops 670 | bytes 396 | tf_op jit(solution)/shard_map/reduce_sum | solution.py:229
  2.7 0.9 select_reduce_fusion
  3.6 0.8 and_select_fusion.1
  4.4 0.2 convert_reduce_fusion
  4.6 0.6 fusion.54
  7.1 0.9 copy.103
  8.1 0.8 dynamic-slice_reduce_fusion
  8.9 0.7 dynamic-slice_reduce_fusion.1
  9.6 0.8 copy.104
  10.4 0.9 constant_dynamic-slice_fusion
  11.4 0.7 reshape.389.x_ref
  12.1 10.0 %shard_map.219 = bf16[32,13,128]{2,1,0:T(8,128)(2,1)} custom-call(bf16[32,13,128]{2,1,0:T(8,128)(2,1)} %reshape.389.x_ref), custom_call_target="tpu_custom_call" | custom-call | tf_op jit(solution)/shard_map/pallas_call | solution.py:203
  22.2 1.1 convolution_convert_fusion.1
  23.3 0.8 reshape.391.x_ref
  24.1 9.1 %shard_map.220 = bf16[32,13,128]{2,1,0:T(8,128)(2,1)} custom-call(bf16[32,13,128]{2,1,0:T(8,128)(2,1)} %reshape.391.x_ref), custom_call_target="tpu_custom_call" | custom-call | tf_op jit(solution)/shard_map/pallas_call | solution.py:203
  33.2 1.0 reshape.392
  35.0 3.4 %pad_maximum_fusion = bf16[32,399,128]{2,1,0:T(8,128)(2,1)} fusion(bf16[32,6,128]{2,1,0:T(8,128)(2,1)S(1)} %reshape.385, bf16[32,9,128]{2,1,0:T(8,128)(2,1)S(1)} %reshape.384, bf16[32,384,128]{2,1,0:T(8,128)(2,1)} %bitcast.70), kind=kLoop, calls=%fused_computation.2 | loop fusion | flops 9805824 | bytes 6537216 | tf_op jit(solution)/shard_map/concatenate | solution.py:280
  38.5 4.6 %gather_fusion = bf16[32,399,128]{2,1,0:T(8,128)(2,1)} fusion(bf16[32,399,128]{2,1,0:T(8,128)(2,1)} %pad_maximum_fusion, s32[1024]{0:T(1024)S(1)} %pad_clamp_fusion.1), kind=kCustom, calls=%fused_computation | custom fusion | bytes 6537344 | tf_op jit(solution)/shard_map/gather | solution.py:305
  43.1 0.6 fusion.22
  43.7 6.8 %all-to-all-start = ((bf16[32,399,128]{2,1,0:T(8,128)(2,1)}), bf16[32,399,128]{2,1,0:T(8,128)(2,1)}, u32[]{:S(2)}, u32[]{:S(2)}) async-start(bf16[32,399,128]{2,1,0:T(8,128)(2,1)} %fusion.22), calls=%async_computation | async-start | bytes 6553600 | tf_op jit(solution)/shard_map/all_to_all | solution.py:308
  50.6 0.1 fusion.23
  50.8 28.9 %all_gather.3 = bf16[128,1536]{1,0:T(8,128)(2,1)S(1)} all-gather(bf16[16,1536]{1,0:T(8,128)(2,1)S(1)} %fusion.25), channel_id=1, replica_groups=mesh['req'=32,'head'=8] {'head'}, dimensions={0}, use_global_device_ids=true | all-gather | bytes 442368 | tf_op jit(solution)/shard_map/all_gather | solution.py:269
  79.7 0.4 convolution_convert_fusion.3
  80.1 0.1 copy.101
  80.5 2.2 %copy.125 = bf16[192,8,2,384]{3,1,2,0:T(8,128)(2,1)S(1)} copy(bf16[192,8,2,384]{3,2,1,0:T(2,128)(2,1)} %bitcast.71) | data formatting | bytes 4718592
  82.8 0.5 convolution_convert_fusion.2
  83.6 0.2 broadcast_in_dim.202
  83.8 0.1 reshape.395
  84.0 0.1 reshape.441
  84.2 0.1 reshape.438
  84.6 0.2 convert_reduce_fusion.1
  84.8 0.5 compare_select_fusion.1
  85.4 6.4 %all-to-all-done.refs_0_.refs_1_.refs_2_.refs_3_.refs_4_.refs_5_.refs_6_.refs_7_ = bf16[32,399,128]{2,1,0:T(8,128)(2,1)} async-done(((bf16[32,399,128]{2,1,0:T(8,128)(2,1)}), bf16[32,399,128]{2,1,0:T(8,128)(2,1)}, u32[]{:S(2)}, u32[]{:S(2)}) %all-to-all-start) | async-done | bytes 3268640 | tf_op jit(solution)/shard_map/all_to_all | solution.py:308
  91.8 0.9 slice.279
  92.7 0.6 gather_fusion.1
  93.5 0.2 divide_multiply_fusion.1
  93.6 0.3 fusion.57
  94.2 0.4 fusion.30
  94.6 0.3 fusion.36
  94.8 1.0 slice_reduce_fusion.9
  96.0 0.1 reshape.439
  96.3 0.1 reshape.440
  96.5 0.1 reshape.444
  96.7 0.1 reshape.445
  96.9 0.1 reshape.446
  97.2 0.1 reshape.449
  97.4 0.1 reshape.442
  98.1 0.1 reshape.448
  98.5 0.3 copy_multiply_fusion
  98.8 0.2 fusion.65
  99.0 0.8 maximum_maximum_fusion.refs_8_
  99.8 1.1 concatenate.31.refs_9_
  100.9 9.9 %shard_map.221 = (f32[32,8,384]{2,1,0:T(8,128)}, bf16[32,384,128]{2,1,0:T(8,128)(2,1)}) custom-call(s32[32]{0:T(128)} %get-tuple-element.53.rows_ref, bf16[32,399,128]{2,1,0:T(8,128)(2,1)} %all-to-all-done.refs_0_.refs_1_.refs_2_.refs_3_.refs_4_.refs_5_.refs_6_.refs_7_, ...), custom_call_target="tpu_custom_call" | custom-call | tf_op jit(solution)/shard_map/pallas_call | solution.py:113
  110.8 1.4 %fusion.43 = (f32[32,1,384]{2,1,0:T(1,128)S(1)}, f32[32,1,384]{2,1,0:T(1,128)S(1)}) fusion(f32[32,4,384]{2,1,0:T(4,128)S(1)} %get-tuple-element.45, f32[32,1,384]{2,1,0:T(1,128)S(1)} %reshape.438, f32[32,8,384]{2,1,0:T(8,128)} %get-tuple-element.6, f32[32]{0:T(128)S(1)} %get-tuple-element.28, f32[384]{0:T(512)S(1)} %mul.376, ...), kind=kLoop, calls=%fused_computation.89 | loop fusion | flops 172032 | bytes 640768 | tf_op jit(solution)/shard_map/add | solution.py:366
  112.2 1.5 %fusion.42 = (f32[32,1,384]{2,1,0:T(1,128)S(1)}, f32[32,1,384]{2,1,0:T(1,128)S(1)}) fusion(f32[32,4,384]{2,1,0:T(4,128)S(1)} %get-tuple-element.45, f32[32,1,384]{2,1,0:T(1,128)S(1)} %reshape.443, f32[32,1,384]{2,1,0:T(1,128)S(1)} %reshape.442, f32[32,8,384]{2,1,0:T(8,128)} %get-tuple-element.6, f32[32]{0:T(128)S(1)} %get-tuple-element.36, f32[384]{0:T(512)S(1)} %mul.376, ...), kind=kLoop, calls=%fused_computation.87 | loop fusion | flops 221184 | bytes 788224 | tf_op jit(solution)/shard_map/add | solution.py:366
  113.8 0.3 select_convert_fusion
  114.4 0.1 copy.119
  114.5 0.4 convolution_convert_fusion
  114.9 0.8 fusion.1.x_ref
  115.7 18.9 %shard_map.222 = f32[16,1664]{1,0:T(8,128)} custom-call(bf16[128,1664]{1,0:T(8,128)(2,1)} %fusion.1.x_ref), custom_call_target="tpu_custom_call" | custom-call | tf_op jit(solution)/shard_map/pallas_call | solution.py:158
  134.6 1.0 rsqrt_reduce_fusion
  135.6 1.6 %fusion.26 = bf16[16,1536]{1,0:T(8,128)(2,1)} fusion(bf16[16,1536]{1,0:T(8,128)(2,1)S(1)} %copy-done.2, f32[16,1664]{1,0:T(8,128)} %shard_map.222, f32[16]{0:T(128)S(1)} %rsqrt_reduce_fusion), kind=kLoop, calls=%fused_computation.67 | loop fusion | flops 98304 | bytes 196672 | tf_op jit(solution)/shard_map/convert_element_type | solution.py:388
  137.2 0.6 copy.120
  137.8 0.6 copy.121
  (88 shorter events, 3.6 us)
Async XLA Ops:
  0.6 113.9 %copy-start = (bf16[384,1536]{1,0:T(8,128)(2,1)S(1)}, bf16[384,1536]{1,0:T(8,128)(2,1)}, u32[]{:S(2)}) copy-start(bf16[384,1536]{1,0:T(8,128)(2,1)} %param.32) | copy-start | bytes 3538948
  43.7 6.8 %copy-start.2 = (bf16[16,1536]{1,0:T(8,128)(2,1)S(1)}, bf16[16,1536]{1,0:T(8,128)(2,1)}, u32[]{:S(2)}) copy-start(bf16[16,1536]{1,0:T(8,128)(2,1)} %param.20) | copy-start | bytes 147460
  43.7 7.0 %copy-start.3 = (f32[1536]{0:T(1024)S(1)}, f32[1536]{0:T(1024)}, u32[]{:S(2)}) copy-start(f32[1536]{0:T(1024)} %param.21) | copy-start | bytes 18436
  43.7 36.0 %copy-start.1 = (bf16[1536,304]{0,1:T(8,128)(2,1)S(1)}, bf16[1536,304]{0,1:T(8,128)(2,1)}, u32[]{:S(2)}) copy-start(bf16[1536,304]{0,1:T(8,128)(2,1)} %param.23) | copy-start | bytes 2801668
  43.7 36.6 %copy-start.8 = (s32[32]{0:T(128)S(1)}, s32[32]{0:T(128)}, u32[]{:S(2)}) copy-start(s32[32]{0:T(128)} %param.36) | copy-start | bytes 388
  43.7 48.0 %all-to-all-start = ((bf16[32,399,128]{2,1,0:T(8,128)(2,1)}), bf16[32,399,128]{2,1,0:T(8,128)(2,1)}, u32[]{:S(2)}, u32[]{:S(2)}) async-start(bf16[32,399,128]{2,1,0:T(8,128)(2,1)} %fusion.22), calls=%async_computation | async-start | bytes 6553600 | tf_op jit(solution)/shard_map/all_to_all | solution.py:308
  80.5 2.9 %copy-start.12 = (f32[6]{0:T(128)S(1)}, f32[6]{0:T(128)}, u32[]{:S(2)}) copy-start(f32[6]{0:T(128)} %param.29) | copy-start | bytes 76
  80.5 2.9 %copy-start.10 = (f32[6]{0:T(128)S(1)}, f32[6]{0:T(128)}, u32[]{:S(2)}) copy-start(f32[6]{0:T(128)} %param.28) | copy-start | bytes 76
  82.7 1.6 %copy-start.11 = (f32[6]{0:T(128)S(1)}, f32[6]{0:T(128)}, u32[]{:S(2)}) copy-start(f32[6]{0:T(128)} %param.30) | copy-start | bytes 76
  82.7 2.6 %copy-start.4 = (f32[4,384]{1,0:T(4,128)S(1)}, f32[4,384]{1,0:T(4,128)}, u32[]{:S(2)}) copy-start(f32[4,384]{1,0:T(4,128)} %param.24) | copy-start | bytes 18436
  82.7 2.6 %copy-start.5 = (f32[4,256]{1,0:T(4,128)S(1)}, f32[4,256]{1,0:T(4,128)}, u32[]{:S(2)}) copy-start(f32[4,256]{1,0:T(4,128)} %param.26) | copy-start | bytes 12292
  82.7 10.7 %copy-start.9 = (f32[256]{0:T(256)S(1)}, f32[256]{0:T(256)}, u32[]{:S(2)}) copy-start(f32[256]{0:T(256)} %param.27) | copy-start | bytes 3076
  93.5 5.0 %copy-start.6 = (f32[384]{0:T(512)S(1)}, f32[384]{0:T(512)}, u32[]{:S(2)}) copy-start(f32[384]{0:T(512)} %param.25) | copy-start | bytes 4612
  100.9 12.9 %copy-start.7 = (f32[384]{0:T(512)S(1)}, f32[384]{0:T(512)}, u32[]{:S(2)}) copy-start(f32[384]{0:T(512)} %param.31) | copy-start | bytes 4612

commit v10 on v9

--- a/solution.py
+++ b/solution.py
@@ -277,15 +277,15 @@
     state_rows = heads_here * head_dim * state_dim // lanes
     inner_edge_rows = edge_inner.shape[1] * edge_inner.shape[2] // lanes
     shared_edge_rows = edge_shared.shape[1] * edge_shared.shape[2] // lanes
-    packed = jnp.concatenate(
+    state_block = states.reshape(slot_count, state_rows, lanes)
+    edge_block = jnp.concatenate(
         [
-            states.reshape(slot_count, state_rows, lanes),
             edge_inner.reshape(slot_count, inner_edge_rows, lanes),
             edge_shared.reshape(slot_count, shared_edge_rows, lanes),
         ],
         axis=1,
     )
-    row_total = packed.shape[1]
+    row_total = state_rows + edge_block.shape[1]
 
     moving = mig_ids.shape[0] // groups
     own_id = jnp.sum(jnp.where(jnp.arange(mig_ids.shape[0]) == device * moving, mig_ids, 0))
@@ -302,11 +302,16 @@
     send_rows, recv_rows = route_rows(reorder, first_slot, slot_count, all_slots, stride)
     buffer_rows = groups * stride
     send_idx = invert(send_rows, buffer_rows)
-    send_base = packed[send_idx]
     target_row = jnp.sum(jnp.where(jnp.arange(slot_count) == target_local, send_rows, 0))
-    send_buf = lax.dynamic_update_slice(send_base, arrived[None], (target_row, 0, 0))
-    received = lax.all_to_all(send_buf, "req", 0, 0, tiled=True)
-    moved = received[:, state_rows:][recv_rows]
+    send_edges = lax.dynamic_update_slice(
+        edge_block[send_idx], arrived[None, state_rows:], (target_row, 0, 0)
+    )
+    send_states = lax.dynamic_update_slice(
+        state_block[send_idx], arrived[None, :state_rows], (target_row, 0, 0)
+    )
+    received_edges = exchange(send_edges, 3)
+    received = lax.all_to_all(send_states, "req", 0, 0, tiled=True)
+    moved = received_edges[recv_rows]
     moved_inner = moved[:, :inner_edge_rows].reshape(edge_inner.shape)
     moved_shared = moved[:, inner_edge_rows:].reshape(edge_shared.shape)
 

time: 139 us -> 222 us (1.60); the launches traced: 138 us -> 219 us
  local copies, waits for them, and re-layouts: 23.3 us -> 88.7 us
  other arithmetic: 17.8 us -> 29.2 us
  Pallas kernels: 47.9 us -> 54.4 us
  waiting for transfers between devices: 6.41 us -> 0.01 us
  matrix products: 2.71 us -> 6.49 us
    reshape x14, local copies, waits for them, and re-layouts: 1.62 us -> 23.1 us  [per_head(): return jnp.repeat(v, head_dim, axis=-1)]
    broadcast_in_dim x14, local copies, waits for them, and re-layouts: 1.34 us -> 18 us  [per_head(): return jnp.repeat(v, head_dim, axis=-1)]
    pallas_call x2 -> x3, Pallas kernels: 19.1 us -> 28.9 us  [exchange(): pl.pallas_call(functools.partial(exchange_kernel, n=n), out_shape=jax.Sha...]
    all_to_all x1, waiting for transfers between devices: 6.41 us -> 0.01 us  [local(): received = lax.all_to_all(send_states, 'req', 0, 0, tiled=True)]
    pallas_call x1, Pallas kernels: 18.9 us -> 15.7 us  [scatter_sum(): pl.pallas_call(functools.partial(scatter_sum_kernel, n=n, rows=rows), out...]
    gather x2 -> x3, local copies, waits for them, and re-layouts: 5.2 us -> 6.88 us  [the longest x1 2.61 us: local(): state_block[send_idx]]
    unnamed x31 -> x49, local copies, waits for them, and re-layouts: 5.29 us -> 6.11 us
  transfers between devices with their start and end apart: 1 -> 1, of which waited for: 1 -> 0; matrix products, arithmetic and copies ran while one was open for 4% -> 46% of each run, Pallas kernels for 0% -> 5%
where the time goes in v10:
time: 222 us; the launch traced here: 219 us
  local copies, waits for them, and re-layouts  88.7 us (40%)
  Pallas kernels  54.4 us (25%)
  other arithmetic  29.2 us (13%)
  blocking collectives  28.9 us (13%)
  starting transfers between devices  6.79 us (3%)
  matrix products  6.49 us (3%)
  between operations  4.23 us (2%)
    pallas_call x3, Pallas kernels, exchange(): pl.pallas_call(functools.partial(exchange_kernel, n=n), out_shape=jax.Sha...  28.9 us
    all_gather x1, blocking collectives, local(): piece_rows = lax.all_gather(normed, 'head', axis=0, tiled=True)  28.9 us
    reshape x14, local copies, waits for them, and re-layouts, per_head(): return jnp.repeat(v, head_dim, axis=-1)  23.1 us
    broadcast_in_dim x14, local copies, waits for them, and re-layouts, per_head(): return jnp.repeat(v, head_dim, axis=-1)  18 us
    pallas_call x1, Pallas kernels, scatter_sum(): pl.pallas_call(functools.partial(scatter_sum_kernel, n=n, rows=rows), out...  15.7 us
    pallas_call x1, Pallas kernels, recurrence(): pl.pallas_call(functools.partial(recurrence_kernel, group=group, window=w...  9.81 us
    all_to_all x1, starting transfers between devices, local(): received = lax.all_to_all(send_states, 'req', 0, 0, tiled=True)  6.79 us
    unnamed x49, local copies, waits for them, and re-layouts  6.11 us
  transfers between devices with their start and end apart: 1, of which 0 were waited for; matrix products, arithmetic and copies ran while one was open for 46% of the time, Pallas kernels for 5%

profile of v10, /device:TPU:2, one launch (start us, length us, event | category | flops | bytes accessed | tf_op | source)
XLA Modules:
  0.0 218.7 jit_solution(5743258540522512247)
XLA Ops:
  0.7 1.5 fusion.54
  9.5 10.0 %shard_map.219 = bf16[32,13,128]{2,1,0:T(8,128)(2,1)} custom-call(bf16[32,13,128]{2,1,0:T(8,128)(2,1)} %reshape.392.x_ref), custom_call_target="tpu_custom_call" | custom-call | tf_op jit(solution)/shard_map/pallas_call | solution.py:203
  21.5 9.1 %shard_map.220 = bf16[32,13,128]{2,1,0:T(8,128)(2,1)} custom-call(bf16[32,13,128]{2,1,0:T(8,128)(2,1)} %reshape.394.x_ref), custom_call_target="tpu_custom_call" | custom-call | tf_op jit(solution)/shard_map/pallas_call | solution.py:203
  32.3 2.6 %gather_fusion = bf16[32,384,128]{2,1,0:T(8,128)(2,1)} fusion(bf16[32,384,128]{2,1,0:T(8,128)(2,1)S(1)} %bitcast.73, s32[1024]{0:T(1024)S(1)} %pad_clamp_fusion.1), kind=kCustom, calls=%fused_computation | custom fusion | bytes 6291584 | tf_op jit(solution)/shard_map/gather | solution.py:310
  35.6 6.8 %all-to-all-start = ((bf16[32,384,128]{2,1,0:T(8,128)(2,1)}), bf16[32,384,128]{2,1,0:T(8,128)(2,1)}, u32[]{:S(2)}, u32[]{:S(2)}) async-start(bf16[32,384,128]{2,1,0:T(8,128)(2,1)} %fusion.32), calls=%async_computation | async-start | bytes 6291456 | tf_op jit(solution)/shard_map/all_to_all | solution.py:313
  44.0 28.9 %all_gather.3 = bf16[128,1536]{1,0:T(8,128)(2,1)S(1)} all-gather(bf16[16,1536]{1,0:T(8,128)(2,1)S(1)} %fusion.24), channel_id=1, replica_groups=mesh['req'=32,'head'=8] {'head'}, dimensions={0}, use_global_device_ids=true | all-gather | bytes 442368 | tf_op jit(solution)/shard_map/all_gather | solution.py:269
  72.9 2.2 %convolution_convert_fusion.3 = bf16[128,304]{0,1:T(8,128)(2,1)} fusion(bf16[128,1536]{1,0:T(8,128)(2,1)S(1)} %all_gather.3, bf16[1536,304]{0,1:T(8,128)(2,1)} %param.23), kind=kOutput, calls=%fused_computation.6 | convolution fusion | flops 119576576 | bytes 1404928 | tf_op jit(solution)/shard_map/dot_general | solution.py:273
  75.1 1.6 copy.101
  76.8 1.6 reshape.386
  78.3 1.5 slice.288
  79.8 1.4 slice.283
  81.2 1.6 reshape.396
  82.8 1.5 reshape.397
  84.3 1.6 pad_maximum_fusion.2
  85.9 2.1 gather_fusion.1
  88.1 1.3 fusion.52.x_ref
  89.3 9.8 %shard_map.221 = bf16[32,15,128]{2,1,0:T(8,128)(2,1)} custom-call(bf16[32,15,128]{2,1,0:T(8,128)(2,1)} %fusion.52.x_ref), custom_call_target="tpu_custom_call" | custom-call | tf_op jit(solution)/shard_map/pallas_call | solution.py:203
  99.9 2.1 gather_fusion.2
  102.1 1.5 slice.287
  103.5 1.5 reshape.398
  107.9 1.6 slice_reduce_fusion.9
  111.2 1.4 multiply_exponential_fusion
  113.2 1.4 fusion.45
  115.3 1.6 reshape.452
  116.9 1.5 broadcast_in_dim.212
  118.4 1.6 reshape.453
  120.0 1.6 reshape.401
  121.6 2.1 copy.125
  123.8 1.2 convolution_convert_fusion.2
  126.6 1.8 broadcast_in_dim.211
  128.4 1.9 reshape.400
  130.3 1.3 slice_bitcast_fusion.4
  132.4 1.6 reshape.454
  134.0 1.5 broadcast_in_dim.218
  135.5 1.6 reshape.457
  137.1 1.5 broadcast_in_dim.219
  138.6 1.6 reshape.458
  140.2 1.5 broadcast_in_dim.220
  141.7 1.6 reshape.459
  143.3 1.5 broadcast_in_dim.201
  144.8 1.6 reshape.451
  146.4 1.3 broadcast_in_dim.215
  147.7 1.3 mul.376
  150.6 1.6 reshape.462
  152.2 1.5 broadcast_in_dim.216
  153.7 1.6 reshape.455
  155.3 1.5 broadcast_in_dim.217
  156.8 1.6 reshape.456
  159.8 1.6 reshape.460
  161.4 1.5 broadcast_in_dim.222
  162.9 1.6 reshape.461
  164.5 1.5 broadcast_in_dim.224
  166.0 1.6 reshape.463
  168.3 1.4 fusion.29
  170.3 1.3 fusion.36
  174.7 1.9 copy_multiply_fusion
  178.2 2.0 concatenate.31.refs_9_
  181.0 1.4 maximum_maximum_fusion.refs_8_
  182.5 9.8 %shard_map.222 = (f32[32,8,384]{2,1,0:T(8,128)}, bf16[32,384,128]{2,1,0:T(8,128)(2,1)}) custom-call(s32[32]{0:T(128)} %get-tuple-element.53.rows_ref, bf16[32,384,128]{2,1,0:T(8,128)(2,1)} %all-to-all-done.refs_0_.refs_1_.refs_2_.refs_3_.refs_4_.refs_5_.refs_6_.refs_7_, ...), custom_call_target="tpu_custom_call" | custom-call | tf_op jit(solution)/shard_map/pallas_call | solution.py:113
  192.3 1.6 fusion.43
  193.9 1.8 fusion.42
  198.0 1.6 convolution_convert_fusion
  200.4 15.7 %shard_map.223 = f32[16,1664]{1,0:T(8,128)} custom-call(bf16[128,1664]{1,0:T(8,128)(2,1)} %fusion.1.x_ref), custom_call_target="tpu_custom_call" | custom-call | tf_op jit(solution)/shard_map/pallas_call | solution.py:158
  217.1 1.6 fusion.25
  (108 shorter events, 32.8 us)
Async XLA Ops:
  0.6 6.6 %copy-start = (bf16[32,6,64,128]{3,2,1,0:T(8,128)(2,1)S(1)}, bf16[32,6,64,128]{3,2,1,0:T(8,128)(2,1)}, u32[]{:S(2)}) copy-start(bf16[32,6,64,128]{3,2,1,0:T(8,128)(2,1)} %param.33) | copy-start | bytes 9437188
  31.5 3.4 %copy-start.6 = (bf16[53248]{0:T(1024)(128)(2,1)}, bf16[53248]{0:T(1024)(128)(2,1)S(1)}, u32[]{:S(2)}) copy-start(bf16[53248]{0:T(1024)(128)(2,1)S(1)} %reshape.395) | copy-start | bytes 319492
  35.6 6.8 %copy-start.11 = (bf16[32,3,384]{2,0,1:T(8,128)(2,1)S(1)}, bf16[32,3,384]{2,0,1:T(8,128)(2,1)}, u32[]{:S(2)}) copy-start(bf16[32,3,384]{2,0,1:T(8,128)(2,1)} %param.34) | copy-start | bytes 221188
  35.6 7.5 %copy-start.13 = (bf16[32,3,256]{2,0,1:T(8,128)(2,1)S(1)}, bf16[32,3,256]{2,0,1:T(8,128)(2,1)}, u32[]{:S(2)}) copy-start(bf16[32,3,256]{2,0,1:T(8,128)(2,1)} %param.35) | copy-start | bytes 147460
  35.6 8.2 %copy-start.4 = (bf16[16,1536]{1,0:T(8,128)(2,1)S(1)}, bf16[16,1536]{1,0:T(8,128)(2,1)}, u32[]{:S(2)}) copy-start(bf16[16,1536]{1,0:T(8,128)(2,1)} %param.20) | copy-start | bytes 147460
  35.6 8.3 %copy-start.17 = (f32[1536]{0:T(1024)S(1)}, f32[1536]{0:T(1024)}, u32[]{:S(2)}) copy-start(f32[1536]{0:T(1024)} %param.21) | copy-start | bytes 18436
  35.6 146.8 %all-to-all-start = ((bf16[32,384,128]{2,1,0:T(8,128)(2,1)}), bf16[32,384,128]{2,1,0:T(8,128)(2,1)}, u32[]{:S(2)}, u32[]{:S(2)}) async-start(bf16[32,384,128]{2,1,0:T(8,128)(2,1)} %fusion.32), calls=%async_computation | async-start | bytes 6291456 | tf_op jit(solution)/shard_map/all_to_all | solution.py:313
  42.4 62.6 %copy-start.18 = (f32[4,256]{1,0:T(4,128)S(1)}, f32[4,256]{1,0:T(4,128)}, u32[]{:S(2)}) copy-start(f32[4,256]{1,0:T(4,128)} %param.26) | copy-start | bytes 12292
  42.4 67.0 %copy-start.21 = (s32[32]{0:T(128)S(1)}, s32[32]{0:T(128)}, u32[]{:S(2)}) copy-start(s32[32]{0:T(128)} %param.36) | copy-start | bytes 388
  106.9 0.7 copy-start.1
  109.6 3.0 %copy-start.14 = (pred[32,4]{1,0:T(8,128)(4,1)}, pred[32,4]{1,0:T(8,128)(4,1)S(1)}, u32[]{:S(2)}) copy-start(pred[32,4]{1,0:T(8,128)(4,1)S(1)} %iota_compare_fusion.6) | copy-start | bytes 388
  112.5 0.6 copy-start.7
  124.9 43.4 %copy-start.3 = (bf16[32,3,384]{2,1,0:T(4,128)(2,1)S(1)}, bf16[32,3,384]{2,1,0:T(4,128)(2,1)}, u32[]{:S(2)}) copy-start(bf16[32,3,384]{2,1,0:T(4,128)(2,1)} %reshape.401) | copy-start | bytes 221188
  124.9 45.4 %copy-start.2 = (bf16[32,4,304]{2,1,0:T(4,128)(2,1)S(1)}, bf16[32,4,304]{2,1,0:T(4,128)(2,1)}, u32[]{:S(2)}) copy-start(bf16[32,4,304]{2,1,0:T(4,128)(2,1)} %reshape.386) | copy-start | bytes 233476
  159.8 21.3 %copy-start.12 = (f32[32,128]{1,0:T(8,128)S(1)}, f32[32,128]{1,0:T(8,128)}, u32[]{:S(2)}) copy-start(f32[32,128]{1,0:T(8,128)} %pad.13) | copy-start | bytes 49156
  167.6 9.0 %copy-start.8 = (f32[32,1,384]{2,1,0:T(1,128)S(1)}, f32[32,1,384]{2,1,0:T(1,128)}, u32[]{:S(2)}) copy-start(f32[32,1,384]{2,1,0:T(1,128)} %reshape.452) | copy-start | bytes 147460
  167.6 9.0 %copy-start.9 = (f32[32,1,384]{2,1,0:T(1,128)S(1)}, f32[32,1,384]{2,1,0:T(1,128)}, u32[]{:S(2)}) copy-start(f32[32,1,384]{2,1,0:T(1,128)} %reshape.453) | copy-start | bytes 147460
  167.6 9.0 %copy-start.10 = (f32[32,1,384]{2,1,0:T(1,128)S(1)}, f32[32,1,384]{2,1,0:T(1,128)}, u32[]{:S(2)}) copy-start(f32[32,1,384]{2,1,0:T(1,128)} %reshape.454) | copy-start | bytes 147460
  182.5 9.8 %copy-start.16 = (f32[384]{0:T(512)S(1)}, f32[384]{0:T(512)}, u32[]{:S(2)}) copy-start(f32[384]{0:T(512)} %mul.376) | copy-start | bytes 4612
  182.5 11.5 %copy-start.20 = (f32[32]{0:T(128)S(1)}, f32[32]{0:T(128)}, u32[]{:S(2)}) copy-start(f32[32]{0:T(128)} %get-tuple-element.29) | copy-start | bytes 388
  182.5 13.3 %copy-start.15 = (pred[32,4]{1,0:T(8,128)(4,1)S(1)}, pred[32,4]{1,0:T(8,128)(4,1)}, u32[]{:S(2)}) copy-start(pred[32,4]{1,0:T(8,128)(4,1)} %copy-done.14) | copy-start | bytes 388
  182.5 13.3 %copy-start.19 = (f32[384]{0:T(512)S(1)}, f32[384]{0:T(512)}, u32[]{:S(2)}) copy-start(f32[384]{0:T(512)} %param.31) | copy-start | bytes 4612
  196.7 20.4 %copy-start.5 = (bf16[16,1536]{1,0:T(8,128)(2,1)S(1)}, bf16[16,1536]{1,0:T(8,128)(2,1)}, u32[]{:S(2)}) copy-start(bf16[16,1536]{1,0:T(8,128)(2,1)} %param.20) | copy-start | bytes 147460

commit v11 on v9

--- a/solution.py
+++ b/solution.py
@@ -214,12 +214,79 @@
     )(x)
 
 
-def migrate(item, mig_dest, slot_count, groups, device):
+def exchange_pack_kernel(
+    idx_ref, x_ref, states_ref, edges_ref, out_ref, send_ref, send_sem, recv_sem, local_sem, *, n
+):
+    me = lax.axis_index("req")
+    head = lax.axis_index("head")
+    barrier = pltpu.get_barrier_semaphore()
+    for k in range(1, n):
+        pl.semaphore_signal(
+            barrier, inc=1, device_id=(lax.rem(me + k, n), head), device_id_type=MESH
+        )
+    pl.semaphore_wait(barrier, n - 1)
+    own = pltpu.make_async_copy(x_ref.at[me], out_ref.at[me], local_sem.at[0])
+    own.start()
+    copies = []
+    for k in range(1, n):
+        peer = lax.rem(me + k, n)
+        copy = pltpu.make_async_remote_copy(
+            src_ref=x_ref.at[peer],
+            dst_ref=out_ref.at[me],
+            send_sem=send_sem.at[k - 1],
+            recv_sem=recv_sem.at[k - 1],
+            device_id=(peer, head),
+            device_id_type=MESH,
+        )
+        copy.start()
+        copies.append(copy)
+    state_rows = states_ref.shape[1]
+    for r in range(send_ref.shape[0]):
+        row = idx_ref[r]
+        send_ref[r, :state_rows] = states_ref[row]
+        send_ref[r, state_rows:] = edges_ref[row]
+    own.wait()
+    for copy in copies:
+        copy.wait()
+
+
+def exchange_pack(x, idx, states_block, edges_block, tag):
+    n = x.shape[0]
+    slots, state_rows, lanes = states_block.shape
+    return pl.pallas_call(
+        functools.partial(exchange_pack_kernel, n=n),
+        out_shape=[
+            jax.ShapeDtypeStruct(x.shape, x.dtype),
+            jax.ShapeDtypeStruct(
+                (idx.shape[0], state_rows + edges_block.shape[1], lanes), states_block.dtype
+            ),
+        ],
+        in_specs=[
+            pl.BlockSpec(memory_space=pltpu.SMEM),
+            pl.BlockSpec(memory_space=pl.ANY),
+            pl.BlockSpec(memory_space=pltpu.VMEM),
+            pl.BlockSpec(memory_space=pltpu.VMEM),
+        ],
+        out_specs=[
+            pl.BlockSpec(memory_space=pl.ANY),
+            pl.BlockSpec(memory_space=pltpu.VMEM),
+        ],
+        scratch_shapes=[
+            pltpu.SemaphoreType.DMA((n - 1,)),
+            pltpu.SemaphoreType.DMA((n - 1,)),
+            pltpu.SemaphoreType.DMA((1,)),
+        ],
+        compiler_params=pltpu.CompilerParams(collective_id=tag, has_side_effects=True),
+    )(idx, x, states_block, edges_block)
+
+
+def migrate(item, mig_dest, slot_count, groups, device, pack):
     length = item.shape[0]
     lanes = 128
     piece = -(-length // (groups * lanes)) * lanes
     padded = jnp.pad(item, (0, piece * groups - length)).reshape(groups, piece // lanes, lanes)
-    first = exchange(padded, 1).reshape(groups, piece)
+    first, send_base = pack(padded)
+    first = first.reshape(groups, piece)
     dest_dev = mig_dest // slot_count
     order = invert(dest_dev, groups)
     pick = (order[:, None] == jnp.arange(groups, dtype=jnp.int32)[None, :]).astype(first.dtype)
@@ -227,7 +294,7 @@
     second = exchange(routed.reshape(groups, piece // lanes, lanes), 2)
     arrived = second.reshape(-1)[:length]
     target_local = jnp.sum(jnp.where(dest_dev == device, mig_dest, 0)) - device * slot_count
-    return arrived, target_local
+    return arrived, target_local, send_base
 
 
 def local(
@@ -277,15 +344,18 @@
     state_rows = heads_here * head_dim * state_dim // lanes
     inner_edge_rows = edge_inner.shape[1] * edge_inner.shape[2] // lanes
     shared_edge_rows = edge_shared.shape[1] * edge_shared.shape[2] // lanes
-    packed = jnp.concatenate(
+    state_block = states.reshape(slot_count, state_rows, lanes)
+    edge_block = jnp.concatenate(
         [
-            states.reshape(slot_count, state_rows, lanes),
             edge_inner.reshape(slot_count, inner_edge_rows, lanes),
             edge_shared.reshape(slot_count, shared_edge_rows, lanes),
         ],
         axis=1,
     )
-    row_total = packed.shape[1]
+    row_total = state_rows + edge_block.shape[1]
+    send_rows, recv_rows = route_rows(reorder, first_slot, slot_count, all_slots, stride)
+    buffer_rows = groups * stride
+    send_idx = invert(send_rows, buffer_rows)
 
     moving = mig_ids.shape[0] // groups
     own_id = jnp.sum(jnp.where(jnp.arange(mig_ids.shape[0]) == device * moving, mig_ids, 0))
@@ -296,13 +366,16 @@
             for part in (states, edge_inner, edge_shared)
         ]
     )
-    arrived, target_local = migrate(item, mig_dest, slot_count, groups, device)
+    arrived, target_local, send_base = migrate(
+        item,
+        mig_dest,
+        slot_count,
+        groups,
+        device,
+        lambda x: exchange_pack(x, send_idx, state_block, edge_block, 1),
+    )
     arrived = arrived.reshape(row_total, lanes)
 
-    send_rows, recv_rows = route_rows(reorder, first_slot, slot_count, all_slots, stride)
-    buffer_rows = groups * stride
-    send_idx = invert(send_rows, buffer_rows)
-    send_base = packed[send_idx]
     target_row = jnp.sum(jnp.where(jnp.arange(slot_count) == target_local, send_rows, 0))
     send_buf = lax.dynamic_update_slice(send_base, arrived[None], (target_row, 0, 0))
     received = lax.all_to_all(send_buf, "req", 0, 0, tiled=True)

time: 139 us -> 136 us (0.978)
  local copies, waits for them, and re-layouts: 23.3 us -> 18.8 us
  Pallas kernels: 47.9 us -> 51.6 us
  other arithmetic: 17.8 us -> 15.6 us
    pallas_call x0 -> x1, Pallas kernels: none -> 13.7 us  [exchange_pack(): pl.pallas_call(functools.partial(exchange_pack_kernel, n=n), out_shape=[j...]
    pallas_call x2 -> x1, Pallas kernels: 19.1 us -> 9.06 us  [exchange(): pl.pallas_call(functools.partial(exchange_kernel, n=n), out_shape=jax.Sha...]
    gather x1 -> x0, local copies, waits for them, and re-layouts: 4.61 us -> none  [local(): send_base = packed[send_idx]]
    concatenate x1, other arithmetic: 3.44 us -> 0.7 us  [local(): jnp.concatenate([edge_inner.reshape(slot_count, inner_edge_rows, lanes),...]
    unnamed x31 -> x35, local copies, waits for them, and re-layouts: 5.29 us -> 5.28 us
where the time goes in v11:
time: 136 us; the launch traced here: 135 us
  Pallas kernels  51.6 us (38%)
  blocking collectives  28.9 us (21%)
  local copies, waits for them, and re-layouts  18.8 us (14%)
  other arithmetic  15.6 us (11%)
  starting transfers between devices  6.79 us (5%)
  waiting for transfers between devices  6.27 us (5%)
  between operations  4.63 us (3%)
  matrix products  2.7 us (2%)
    all_gather x1, blocking collectives, local(): piece_rows = lax.all_gather(normed, 'head', axis=0, tiled=True)  28.9 us
    pallas_call x1, Pallas kernels, scatter_sum(): pl.pallas_call(functools.partial(scatter_sum_kernel, n=n, rows=rows), out...  18.9 us
    pallas_call x1, Pallas kernels, exchange_pack(): pl.pallas_call(functools.partial(exchange_pack_kernel, n=n), out_shape=[j...  13.7 us
    pallas_call x1, Pallas kernels, recurrence(): pl.pallas_call(functools.partial(recurrence_kernel, group=group, window=w...  9.93 us
    pallas_call x1, Pallas kernels, exchange(): pl.pallas_call(functools.partial(exchange_kernel, n=n), out_shape=jax.Sha...  9.06 us
    all_to_all x1, starting transfers between devices, local(): received = lax.all_to_all(send_buf, 'req', 0, 0, tiled=True)  6.79 us
    all_to_all x1, waiting for transfers between devices, local(): received = lax.all_to_all(send_buf, 'req', 0, 0, tiled=True)  6.27 us
    unnamed x35, local copies, waits for them, and re-layouts  5.28 us
  transfers between devices with their start and end apart: 1, of which 1 were waited for; matrix products, arithmetic and copies ran while one was open for 4% of the time, Pallas kernels for 0%

profile of v11, /device:TPU:2, one launch (start us, length us, event | category | flops | bytes accessed | tf_op | source)
XLA Modules:
  0.0 135.3 jit_solution(12496589753353121216)
XLA Ops:
  0.7 1.4 %fusion.53 = (s32[]{:T(128)}, s32[32]{0:T(128)S(1)}, s32[]{:T(128)}) fusion(s32[32]{0:T(128)} %param.38, s32[]{:T(128)S(6)} %axis_index.25, s32[32]{0:T(128)} %param.37), kind=kLoop, calls=%fused_computation.153 | loop fusion | flops 670 | bytes 396 | tf_op jit(solution)/shard_map/reduce_sum | solution.py:296
  2.7 0.9 select_reduce_fusion
  3.6 0.8 and_select_fusion.1
  4.4 0.2 convert_reduce_fusion
  4.6 0.6 fusion.54
  7.2 0.9 copy.105
  8.1 0.8 dynamic-slice_reduce_fusion
  8.9 0.7 dynamic-slice_reduce_fusion.1
  9.6 0.8 copy.106
  10.4 0.9 constant_dynamic-slice_fusion
  11.4 0.7 reshape.373.x_ref
  12.1 0.6 select_reduce_fusion.2.idx_ref
  12.9 0.7 pad_maximum_fusion.2.edges_ref
  13.6 13.7 %shard_map.219 = (bf16[32,13,128]{2,1,0:T(8,128)(2,1)}, bf16[32,399,128]{2,1,0:T(8,128)(2,1)}) custom-call(s32[32]{0:T(128)} %select_reduce_fusion.2.idx_ref, bf16[32,13,128]{2,1,0:T(8,128)(2,1)} %reshape.373.x_ref, bf16[32,384,128]{2,1,0:T(8,128)(2,1)} %bitcast.66, bf16[32,15,128]{2,1,0:T(8,128)(2,1)} %pad_maximum_fusion.2.edges_ref), custom_call_target="tpu_custom_call" | custom-call | tf_op jit(solution)/shard_map/pallas_call | solution.py:256
  27.4 1.1 convolution_convert_fusion.1
  28.5 0.8 reshape.378.x_ref
  29.3 9.1 %shard_map.220 = bf16[32,13,128]{2,1,0:T(8,128)(2,1)} custom-call(bf16[32,13,128]{2,1,0:T(8,128)(2,1)} %reshape.378.x_ref), custom_call_target="tpu_custom_call" | custom-call | tf_op jit(solution)/shard_map/pallas_call | solution.py:203
  38.4 1.0 reshape.379
  40.0 0.6 fusion.22
  40.6 6.8 %all-to-all-start = ((bf16[32,399,128]{2,1,0:T(8,128)(2,1)}), bf16[32,399,128]{2,1,0:T(8,128)(2,1)}, u32[]{:S(2)}, u32[]{:S(2)}) async-start(bf16[32,399,128]{2,1,0:T(8,128)(2,1)} %fusion.22), calls=%async_computation | async-start | bytes 6553600 | tf_op jit(solution)/shard_map/all_to_all | solution.py:381
  47.4 0.1 fusion.23
  47.7 28.9 %all_gather.3 = bf16[128,1536]{1,0:T(8,128)(2,1)S(1)} all-gather(bf16[16,1536]{1,0:T(8,128)(2,1)S(1)} %fusion.25), channel_id=1, replica_groups=mesh['req'=32,'head'=8] {'head'}, dimensions={0}, use_global_device_ids=true | all-gather | bytes 442368 | tf_op jit(solution)/shard_map/all_gather | solution.py:336
  76.5 0.4 convolution_convert_fusion.3
  76.9 0.1 copy.103
  77.3 2.1 %copy.127 = bf16[192,8,2,384]{3,1,2,0:T(8,128)(2,1)S(1)} copy(bf16[192,8,2,384]{3,2,1,0:T(2,128)(2,1)} %bitcast.67) | data formatting | bytes 4718592
  79.6 0.5 convolution_convert_fusion.2
  80.2 0.1 slice-done
  80.5 0.2 broadcast_in_dim.201
  80.7 0.1 reshape.382
  81.0 0.1 reshape.420
  81.2 0.1 reshape.417
  81.5 0.2 convert_reduce_fusion.1
  81.7 0.5 compare_select_fusion.1
  82.3 6.3 %all-to-all-done.refs_0_.refs_1_.refs_2_.refs_3_.refs_4_.refs_5_.refs_6_.refs_7_ = bf16[32,399,128]{2,1,0:T(8,128)(2,1)} async-done(((bf16[32,399,128]{2,1,0:T(8,128)(2,1)}), bf16[32,399,128]{2,1,0:T(8,128)(2,1)}, u32[]{:S(2)}, u32[]{:S(2)}) %all-to-all-start) | async-done | bytes 3268640 | tf_op jit(solution)/shard_map/all_to_all | solution.py:381
  88.6 0.9 slice.277
  89.5 0.6 gather_fusion
  90.3 0.2 divide_multiply_fusion.1
  90.5 0.3 fusion.56
  91.0 0.4 fusion.30
  91.4 0.3 fusion.36
  91.7 1.0 slice_reduce_fusion.9
  92.9 0.1 reshape.418
  93.1 0.1 reshape.419
  93.3 0.1 reshape.423
  93.5 0.1 reshape.424
  93.8 0.1 reshape.425
  94.5 0.1 reshape.422
  95.2 0.1 reshape.429
  95.3 0.3 copy_multiply_fusion
  95.6 0.2 fusion.64
  95.8 0.8 maximum_maximum_fusion.refs_8_
  96.6 1.1 concatenate.31.refs_9_
  97.7 9.9 %shard_map.221 = (f32[32,8,384]{2,1,0:T(8,128)}, bf16[32,384,128]{2,1,0:T(8,128)(2,1)}) custom-call(s32[32]{0:T(128)} %get-tuple-element.57.rows_ref, bf16[32,399,128]{2,1,0:T(8,128)(2,1)} %all-to-all-done.refs_0_.refs_1_.refs_2_.refs_3_.refs_4_.refs_5_.refs_6_.refs_7_, ...), custom_call_target="tpu_custom_call" | custom-call | tf_op jit(solution)/shard_map/pallas_call | solution.py:113
  107.7 1.4 %fusion.43 = (f32[32,1,384]{2,1,0:T(1,128)S(1)}, f32[32,1,384]{2,1,0:T(1,128)S(1)}) fusion(f32[32,4,384]{2,1,0:T(4,128)S(1)} %get-tuple-element.49, f32[32,1,384]{2,1,0:T(1,128)S(1)} %reshape.417, f32[32,8,384]{2,1,0:T(8,128)} %get-tuple-element.10, f32[32]{0:T(128)S(1)} %get-tuple-element.32, f32[384]{0:T(512)S(1)} %mul.376, ...), kind=kLoop, calls=%fused_computation.88 | loop fusion | flops 172032 | bytes 640768 | tf_op jit(solution)/shard_map/add | solution.py:439
  109.1 1.5 %fusion.42 = (f32[32,1,384]{2,1,0:T(1,128)S(1)}, f32[32,1,384]{2,1,0:T(1,128)S(1)}) fusion(f32[32,4,384]{2,1,0:T(4,128)S(1)} %get-tuple-element.49, f32[32,1,384]{2,1,0:T(1,128)S(1)} %reshape.422, f32[32,1,384]{2,1,0:T(1,128)S(1)} %reshape.421, f32[32,8,384]{2,1,0:T(8,128)} %get-tuple-element.10, f32[32]{0:T(128)S(1)} %get-tuple-element.40, ...), kind=kLoop, calls=%fused_computation.86 | loop fusion | flops 221184 | bytes 788224 | tf_op jit(solution)/shard_map/add | solution.py:439
  110.6 0.3 select_convert_fusion
  111.3 0.1 copy.121
  111.4 0.4 convolution_convert_fusion
  111.8 0.8 fusion.1.x_ref
  112.6 18.9 %shard_map.222 = f32[16,1664]{1,0:T(8,128)} custom-call(bf16[128,1664]{1,0:T(8,128)(2,1)} %fusion.1.x_ref), custom_call_target="tpu_custom_call" | custom-call | tf_op jit(solution)/shard_map/pallas_call | solution.py:158
  131.5 1.0 rsqrt_reduce_fusion
  132.4 1.6 %fusion.26 = bf16[16,1536]{1,0:T(8,128)(2,1)} fusion(bf16[16,1536]{1,0:T(8,128)(2,1)S(1)} %copy-done.4, f32[16,1664]{1,0:T(8,128)} %shard_map.222, f32[16]{0:T(128)S(1)} %rsqrt_reduce_fusion), kind=kLoop, calls=%fused_computation.66 | loop fusion | flops 98304 | bytes 196672 | tf_op jit(solution)/shard_map/convert_element_type | solution.py:461
  134.0 0.6 copy.122
  134.7 0.6 copy.123
  (90 shorter events, 3.6 us)
Async XLA Ops:
  0.6 110.8 %copy-start = (bf16[384,1536]{1,0:T(8,128)(2,1)S(1)}, bf16[384,1536]{1,0:T(8,128)(2,1)}, u32[]{:S(2)}) copy-start(bf16[384,1536]{1,0:T(8,128)(2,1)} %param.32) | copy-start | bytes 3538948
  40.6 6.8 %copy-start.4 = (bf16[16,1536]{1,0:T(8,128)(2,1)S(1)}, bf16[16,1536]{1,0:T(8,128)(2,1)}, u32[]{:S(2)}) copy-start(bf16[16,1536]{1,0:T(8,128)(2,1)} %param.20) | copy-start | bytes 147460
  40.6 7.0 %copy-start.5 = (f32[1536]{0:T(1024)S(1)}, f32[1536]{0:T(1024)}, u32[]{:S(2)}) copy-start(f32[1536]{0:T(1024)} %param.21) | copy-start | bytes 18436
  40.6 35.9 %copy-start.3 = (bf16[1536,304]{0,1:T(8,128)(2,1)S(1)}, bf16[1536,304]{0,1:T(8,128)(2,1)}, u32[]{:S(2)}) copy-start(bf16[1536,304]{0,1:T(8,128)(2,1)} %param.23) | copy-start | bytes 2801668
  40.6 48.0 %all-to-all-start = ((bf16[32,399,128]{2,1,0:T(8,128)(2,1)}), bf16[32,399,128]{2,1,0:T(8,128)(2,1)}, u32[]{:S(2)}, u32[]{:S(2)}) async-start(bf16[32,399,128]{2,1,0:T(8,128)(2,1)} %fusion.22), calls=%async_computation | async-start | bytes 6553600 | tf_op jit(solution)/shard_map/all_to_all | solution.py:381
  47.4 29.8 %copy-start.10 = (s32[32]{0:T(128)S(1)}, s32[32]{0:T(128)}, u32[]{:S(2)}) copy-start(s32[32]{0:T(128)} %param.36) | copy-start | bytes 388
  77.1 2.4 %copy-start.1 = (bf16[32,4,304]{2,1,0:T(4,128)(2,1)}, bf16[32,4,304]{2,1,0:T(4,128)(2,1)S(1)}, u32[]{:S(2)}) copy-start(bf16[32,4,304]{2,1,0:T(4,128)(2,1)S(1)} %reshape.368) | copy-start | bytes 233476
  79.5 0.9 copy-start.14
  79.5 0.9 copy-start.12
  79.5 0.8 slice-start
  79.5 1.8 %copy-start.13 = (f32[6]{0:T(128)S(1)}, f32[6]{0:T(128)}, u32[]{:S(2)}) copy-start(f32[6]{0:T(128)} %param.30) | copy-start | bytes 76
  79.6 2.7 %copy-start.6 = (f32[4,384]{1,0:T(4,128)S(1)}, f32[4,384]{1,0:T(4,128)}, u32[]{:S(2)}) copy-start(f32[4,384]{1,0:T(4,128)} %param.24) | copy-start | bytes 18436
  79.6 2.7 %copy-start.7 = (f32[4,256]{1,0:T(4,128)S(1)}, f32[4,256]{1,0:T(4,128)}, u32[]{:S(2)}) copy-start(f32[4,256]{1,0:T(4,128)} %param.26) | copy-start | bytes 12292
  80.1 10.2 %copy-start.11 = (f32[256]{0:T(256)S(1)}, f32[256]{0:T(256)}, u32[]{:S(2)}) copy-start(f32[256]{0:T(256)} %param.27) | copy-start | bytes 3076
  80.8 10.5 %copy-start.2 = (bf16[32,4,304]{2,1,0:T(4,128)(2,1)S(1)}, bf16[32,4,304]{2,1,0:T(4,128)(2,1)}, u32[]{:S(2)}) copy-start(bf16[32,4,304]{2,1,0:T(4,128)(2,1)} %copy-done.1) | copy-start | bytes 233476
  91.0 4.3 %copy-start.8 = (f32[384]{0:T(512)S(1)}, f32[384]{0:T(512)}, u32[]{:S(2)}) copy-start(f32[384]{0:T(512)} %param.25) | copy-start | bytes 4612
  97.7 12.9 %copy-start.9 = (f32[384]{0:T(512)S(1)}, f32[384]{0:T(512)}, u32[]{:S(2)}) copy-start(f32[384]{0:T(512)} %param.31) | copy-start | bytes 4612

commit v12 on v11

--- a/solution.py
+++ b/solution.py
@@ -363,7 +363,7 @@
     item = jnp.concatenate(
         [
             lax.dynamic_index_in_dim(part, mig_local, 0, keepdims=False).reshape(-1)
-            for part in (states, edge_inner, edge_shared)
+            for part in (states, edge_block)
         ]
     )
     arrived, target_local, send_base = migrate(

time: 136 us -> 135 us (level)
  local copies, waits for them, and re-layouts: 18.8 us -> 17.3 us
    dynamic_slice x3 -> x1, local copies, waits for them, and re-layouts: 2.39 us -> 0.91 us  [local(): lax.dynamic_index_in_dim(part, mig_local, 0, keepdims=False).reshape(-1)]
where the time goes in v12:
time: 135 us; the launch traced here: 134 us
  Pallas kernels  51.8 us (38%)
  blocking collectives  28.9 us (21%)
  local copies, waits for them, and re-layouts  17.3 us (13%)
  other arithmetic  15.6 us (12%)
  starting transfers between devices  6.78 us (5%)
  waiting for transfers between devices  6.26 us (5%)
  between operations  4.62 us (3%)
  matrix products  2.71 us (2%)
    all_gather x1, blocking collectives, local(): piece_rows = lax.all_gather(normed, 'head', axis=0, tiled=True)  28.9 us
    pallas_call x1, Pallas kernels, scatter_sum(): pl.pallas_call(functools.partial(scatter_sum_kernel, n=n, rows=rows), out...  18.9 us
    pallas_call x1, Pallas kernels, exchange_pack(): pl.pallas_call(functools.partial(exchange_pack_kernel, n=n), out_shape=[j...  13.9 us
    pallas_call x1, Pallas kernels, recurrence(): pl.pallas_call(functools.partial(recurrence_kernel, group=group, window=w...  9.93 us
    pallas_call x1, Pallas kernels, exchange(): pl.pallas_call(functools.partial(exchange_kernel, n=n), out_shape=jax.Sha...  9.06 us
    all_to_all x1, starting transfers between devices, local(): received = lax.all_to_all(send_buf, 'req', 0, 0, tiled=True)  6.78 us
    all_to_all x1, waiting for transfers between devices, local(): received = lax.all_to_all(send_buf, 'req', 0, 0, tiled=True)  6.26 us
    unnamed x35, local copies, waits for them, and re-layouts  5.28 us
  transfers between devices with their start and end apart: 1, of which 1 were waited for; matrix products, arithmetic and copies ran while one was open for 4% of the time, Pallas kernels for 0%

profile of v12, /device:TPU:2, one launch (start us, length us, event | category | flops | bytes accessed | tf_op | source)
XLA Modules:
  0.0 133.9 jit_solution(1610957350714050304)
XLA Ops:
  0.7 1.4 %fusion.53 = (s32[]{:T(128)}, s32[32]{0:T(128)S(1)}, s32[]{:T(128)}) fusion(s32[32]{0:T(128)} %param.38, s32[]{:T(128)S(6)} %axis_index.25, s32[32]{0:T(128)} %param.37), kind=kLoop, calls=%fused_computation.153 | loop fusion | flops 670 | bytes 396 | tf_op jit(solution)/shard_map/reduce_sum | solution.py:296
  2.7 0.9 select_reduce_fusion
  3.6 0.8 and_select_fusion.1
  4.4 0.2 convert_reduce_fusion
  4.6 0.6 fusion.54
  7.2 0.6 select_reduce_fusion.2.idx_ref
  7.8 0.9 copy.105
  8.8 0.8 copy.106
  9.7 0.7 pad_maximum_fusion.2.edges_ref
  10.4 0.9 constant_dynamic-slice_fusion
  11.3 0.7 reshape.370.x_ref
  12.1 13.9 %shard_map.219 = (bf16[32,13,128]{2,1,0:T(8,128)(2,1)}, bf16[32,399,128]{2,1,0:T(8,128)(2,1)}) custom-call(s32[32]{0:T(128)} %select_reduce_fusion.2.idx_ref, bf16[32,13,128]{2,1,0:T(8,128)(2,1)} %reshape.370.x_ref, bf16[32,384,128]{2,1,0:T(8,128)(2,1)} %bitcast.68, bf16[32,15,128]{2,1,0:T(8,128)(2,1)} %pad_maximum_fusion.2.edges_ref), custom_call_target="tpu_custom_call" | custom-call | tf_op jit(solution)/shard_map/pallas_call | solution.py:256
  26.0 1.1 convolution_convert_fusion.1
  27.1 0.8 reshape.373.x_ref
  27.9 9.1 %shard_map.220 = bf16[32,13,128]{2,1,0:T(8,128)(2,1)} custom-call(bf16[32,13,128]{2,1,0:T(8,128)(2,1)} %reshape.373.x_ref), custom_call_target="tpu_custom_call" | custom-call | tf_op jit(solution)/shard_map/pallas_call | solution.py:203
  37.0 1.0 reshape.374
  38.6 0.6 fusion.20
  39.2 6.8 %all-to-all-start = ((bf16[32,399,128]{2,1,0:T(8,128)(2,1)}), bf16[32,399,128]{2,1,0:T(8,128)(2,1)}, u32[]{:S(2)}, u32[]{:S(2)}) async-start(bf16[32,399,128]{2,1,0:T(8,128)(2,1)} %fusion.20), calls=%async_computation | async-start | bytes 6553600 | tf_op jit(solution)/shard_map/all_to_all | solution.py:381
  46.0 0.1 fusion.21
  46.3 28.9 %all_gather.3 = bf16[128,1536]{1,0:T(8,128)(2,1)S(1)} all-gather(bf16[16,1536]{1,0:T(8,128)(2,1)S(1)} %fusion.23), channel_id=1, replica_groups=mesh['req'=32,'head'=8] {'head'}, dimensions={0}, use_global_device_ids=true | all-gather | bytes 442368 | tf_op jit(solution)/shard_map/all_gather | solution.py:336
  75.2 0.4 convolution_convert_fusion.3
  75.6 0.1 copy.103
  76.0 2.1 %copy.127 = bf16[192,8,2,384]{3,1,2,0:T(8,128)(2,1)S(1)} copy(bf16[192,8,2,384]{3,2,1,0:T(2,128)(2,1)} %bitcast.69) | data formatting | bytes 4718592
  78.2 0.5 convolution_convert_fusion.2
  78.8 0.1 slice-done
  79.1 0.2 broadcast_in_dim.201
  79.3 0.1 reshape.377
  79.6 0.1 reshape.415
  79.8 0.1 reshape.412
  80.2 0.2 convert_reduce_fusion.1
  80.3 0.5 compare_select_fusion.1
  80.9 6.3 %all-to-all-done.refs_0_.refs_1_.refs_2_.refs_3_.refs_4_.refs_5_.refs_6_.refs_7_ = bf16[32,399,128]{2,1,0:T(8,128)(2,1)} async-done(((bf16[32,399,128]{2,1,0:T(8,128)(2,1)}), bf16[32,399,128]{2,1,0:T(8,128)(2,1)}, u32[]{:S(2)}, u32[]{:S(2)}) %all-to-all-start) | async-done | bytes 3268640 | tf_op jit(solution)/shard_map/all_to_all | solution.py:381
  87.2 0.9 slice.277
  88.1 0.6 gather_fusion
  88.9 0.2 divide_multiply_fusion.1
  89.1 0.3 fusion.56
  89.6 0.4 fusion.28
  90.0 0.3 fusion.34
  90.3 1.0 slice_reduce_fusion.9
  91.5 0.1 reshape.413
  91.7 0.1 reshape.414
  91.9 0.1 reshape.418
  92.2 0.1 reshape.419
  92.4 0.1 reshape.420
  92.7 0.1 reshape.423
  92.9 0.1 reshape.416
  93.1 0.1 reshape.417
  93.3 0.1 reshape.421
  93.9 0.3 copy_multiply_fusion
  94.2 0.2 fusion.64
  94.4 0.8 maximum_maximum_fusion.refs_8_
  95.2 1.1 concatenate.31.refs_9_
  96.4 9.9 %shard_map.221 = (f32[32,8,384]{2,1,0:T(8,128)}, bf16[32,384,128]{2,1,0:T(8,128)(2,1)}) custom-call(s32[32]{0:T(128)} %get-tuple-element.57.rows_ref, bf16[32,399,128]{2,1,0:T(8,128)(2,1)} %all-to-all-done.refs_0_.refs_1_.refs_2_.refs_3_.refs_4_.refs_5_.refs_6_.refs_7_, ...), custom_call_target="tpu_custom_call" | custom-call | tf_op jit(solution)/shard_map/pallas_call | solution.py:113
  106.3 1.4 %fusion.41 = (f32[32,1,384]{2,1,0:T(1,128)S(1)}, f32[32,1,384]{2,1,0:T(1,128)S(1)}) fusion(f32[32,4,384]{2,1,0:T(4,128)S(1)} %get-tuple-element.49, f32[32,1,384]{2,1,0:T(1,128)S(1)} %reshape.412, f32[32,8,384]{2,1,0:T(8,128)} %get-tuple-element.10, f32[32]{0:T(128)S(1)} %get-tuple-element.32, f32[384]{0:T(512)S(1)} %mul.376, ...), kind=kLoop, calls=%fused_computation.88 | loop fusion | flops 172032 | bytes 640768 | tf_op jit(solution)/shard_map/add | solution.py:439
  107.7 1.5 %fusion.40 = (f32[32,1,384]{2,1,0:T(1,128)S(1)}, f32[32,1,384]{2,1,0:T(1,128)S(1)}) fusion(f32[32,4,384]{2,1,0:T(4,128)S(1)} %get-tuple-element.49, f32[32,1,384]{2,1,0:T(1,128)S(1)} %reshape.417, f32[32,1,384]{2,1,0:T(1,128)S(1)} %reshape.416, f32[32,8,384]{2,1,0:T(8,128)} %get-tuple-element.10, f32[32]{0:T(128)S(1)} %get-tuple-element.40, ...), kind=kLoop, calls=%fused_computation.86 | loop fusion | flops 221184 | bytes 788224 | tf_op jit(solution)/shard_map/add | solution.py:439
  109.3 0.3 select_convert_fusion
  109.9 0.1 copy.121
  110.0 0.4 convolution_convert_fusion
  110.4 0.8 fusion.1.x_ref
  111.2 18.9 %shard_map.222 = f32[16,1664]{1,0:T(8,128)} custom-call(bf16[128,1664]{1,0:T(8,128)(2,1)} %fusion.1.x_ref), custom_call_target="tpu_custom_call" | custom-call | tf_op jit(solution)/shard_map/pallas_call | solution.py:158
  130.1 1.0 rsqrt_reduce_fusion
  131.0 1.6 %fusion.24 = bf16[16,1536]{1,0:T(8,128)(2,1)} fusion(bf16[16,1536]{1,0:T(8,128)(2,1)S(1)} %copy-done.4, f32[16,1664]{1,0:T(8,128)} %shard_map.222, f32[16]{0:T(128)S(1)} %rsqrt_reduce_fusion), kind=kLoop, calls=%fused_computation.66 | loop fusion | flops 98304 | bytes 196672 | tf_op jit(solution)/shard_map/convert_element_type | solution.py:461
  132.6 0.6 copy.122
  133.3 0.6 copy.123
  (87 shorter events, 3.4 us)
Async XLA Ops:
  0.6 109.4 %copy-start = (bf16[384,1536]{1,0:T(8,128)(2,1)S(1)}, bf16[384,1536]{1,0:T(8,128)(2,1)}, u32[]{:S(2)}) copy-start(bf16[384,1536]{1,0:T(8,128)(2,1)} %param.32) | copy-start | bytes 3538948
  39.2 6.8 %copy-start.4 = (bf16[16,1536]{1,0:T(8,128)(2,1)S(1)}, bf16[16,1536]{1,0:T(8,128)(2,1)}, u32[]{:S(2)}) copy-start(bf16[16,1536]{1,0:T(8,128)(2,1)} %param.20) | copy-start | bytes 147460
  39.2 7.0 %copy-start.5 = (f32[1536]{0:T(1024)S(1)}, f32[1536]{0:T(1024)}, u32[]{:S(2)}) copy-start(f32[1536]{0:T(1024)} %param.21) | copy-start | bytes 18436
  39.2 35.9 %copy-start.3 = (bf16[1536,304]{0,1:T(8,128)(2,1)S(1)}, bf16[1536,304]{0,1:T(8,128)(2,1)}, u32[]{:S(2)}) copy-start(bf16[1536,304]{0,1:T(8,128)(2,1)} %param.23) | copy-start | bytes 2801668
  39.2 48.0 %all-to-all-start = ((bf16[32,399,128]{2,1,0:T(8,128)(2,1)}), bf16[32,399,128]{2,1,0:T(8,128)(2,1)}, u32[]{:S(2)}, u32[]{:S(2)}) async-start(bf16[32,399,128]{2,1,0:T(8,128)(2,1)} %fusion.20), calls=%async_computation | async-start | bytes 6553600 | tf_op jit(solution)/shard_map/all_to_all | solution.py:381
  46.0 29.8 %copy-start.10 = (s32[32]{0:T(128)S(1)}, s32[32]{0:T(128)}, u32[]{:S(2)}) copy-start(s32[32]{0:T(128)} %param.36) | copy-start | bytes 388
  75.7 2.4 %copy-start.1 = (bf16[32,4,304]{2,1,0:T(4,128)(2,1)}, bf16[32,4,304]{2,1,0:T(4,128)(2,1)S(1)}, u32[]{:S(2)}) copy-start(bf16[32,4,304]{2,1,0:T(4,128)(2,1)S(1)} %reshape.364) | copy-start | bytes 233476
  78.1 0.9 copy-start.14
  78.1 0.9 copy-start.12
  78.1 0.8 slice-start
  78.2 1.8 %copy-start.13 = (f32[6]{0:T(128)S(1)}, f32[6]{0:T(128)}, u32[]{:S(2)}) copy-start(f32[6]{0:T(128)} %param.30) | copy-start | bytes 76
  78.2 2.7 %copy-start.6 = (f32[4,384]{1,0:T(4,128)S(1)}, f32[4,384]{1,0:T(4,128)}, u32[]{:S(2)}) copy-start(f32[4,384]{1,0:T(4,128)} %param.24) | copy-start | bytes 18436
  78.2 2.7 %copy-start.7 = (f32[4,256]{1,0:T(4,128)S(1)}, f32[4,256]{1,0:T(4,128)}, u32[]{:S(2)}) copy-start(f32[4,256]{1,0:T(4,128)} %param.26) | copy-start | bytes 12292
  78.7 10.2 %copy-start.11 = (f32[256]{0:T(256)S(1)}, f32[256]{0:T(256)}, u32[]{:S(2)}) copy-start(f32[256]{0:T(256)} %param.27) | copy-start | bytes 3076
  79.5 10.5 %copy-start.2 = (bf16[32,4,304]{2,1,0:T(4,128)(2,1)S(1)}, bf16[32,4,304]{2,1,0:T(4,128)(2,1)}, u32[]{:S(2)}) copy-start(bf16[32,4,304]{2,1,0:T(4,128)(2,1)} %copy-done.1) | copy-start | bytes 233476
  89.6 4.3 %copy-start.8 = (f32[384]{0:T(512)S(1)}, f32[384]{0:T(512)}, u32[]{:S(2)}) copy-start(f32[384]{0:T(512)} %param.25) | copy-start | bytes 4612
  96.4 12.9 %copy-start.9 = (f32[384]{0:T(512)S(1)}, f32[384]{0:T(512)}, u32[]{:S(2)}) copy-start(f32[384]{0:T(512)} %param.31) | copy-start | bytes 4612

commit v13 on v12

--- a/solution.py
+++ b/solution.py
@@ -414,13 +414,32 @@
         for s in range(t - 1, -1, -1):
             span[(t, s)] = span[(t, s + 1)] * factor[:, s + 1]
 
-    def per_head(v):
-        return jnp.repeat(v, head_dim, axis=-1)
+    last = window - 1
+    overlap = jnp.einsum("rtn,rsn->rts", readouts, entries, precision=HIGH)
+    names = (
+        [("step", t) for t in range(window)]
+        + [("push", s) for s in range(window)]
+        + [("cum", t) for t in range(window)]
+        + [("pair", t, s) for t in range(window) for s in range(t + 1)]
+    )
+    rows = []
+    for name in names:
+        if name[0] == "step":
+            rows.append(step_size[:, name[1]])
+        elif name[0] == "push":
+            rows.append(span[(last, name[1])])
+        elif name[0] == "cum":
+            rows.append(cum[name[1]])
+        else:
+            rows.append(span[(name[1], name[2])] * overlap[:, name[1], name[2], None])
+    wide = jnp.repeat(jnp.stack(rows, axis=1), head_dim, axis=-1)
+    at = {name: k for k, name in enumerate(names)}
 
     flat_inputs = mixed_inner.reshape(slot_count, window, inner_here)
-    weighted = per_head(step_size) * flat_inputs
-    last = window - 1
-    pushed = jnp.stack([per_head(span[(last, s)]) * weighted[:, s] for s in range(window)], axis=1)
+    weighted = jnp.stack(
+        [wide[:, at[("step", t)]] * flat_inputs[:, t] for t in range(window)], axis=1
+    )
+    pushed = jnp.stack([wide[:, at[("push", s)]] * weighted[:, s] for s in range(window)], axis=1)
     weight = jnp.concatenate([pushed, jnp.zeros_like(pushed)], axis=1)
     carry = jnp.pad(cum[last], ((0, 0), (0, state_dim - heads_here)))[:, None, :]
     mix = jnp.concatenate(
@@ -429,13 +448,12 @@
     )
     read, states_out = recurrence(received, recv_rows, mix, weight, state_rows, heads_here)
     states_out = states_out.reshape(states.shape)
-    overlap = jnp.einsum("rtn,rsn->rts", readouts, entries, precision=HIGH)
     skip_wide = jnp.repeat(skip_gain, head_dim)
     produced = []
     for t in range(window):
-        acc = per_head(cum[t]) * read[:, t]
+        acc = wide[:, at[("cum", t)]] * read[:, t]
         for s in range(t + 1):
-            acc = acc + per_head(span[(t, s)] * overlap[:, t, s, None]) * weighted[:, s]
+            acc = acc + wide[:, at[("pair", t, s)]] * weighted[:, s]
         produced.append(acc + skip_wide * flat_inputs[:, t])
     outputs = jnp.stack(produced, axis=1)
 

time: 135 us -> 138 us (1.022)
  local copies, waits for them, and re-layouts: 17.3 us -> 21.1 us
    unnamed x35 -> x76, local copies, waits for them, and re-layouts: 5.28 us -> 5.65 us
  transfers between devices with their start and end apart: 1 -> 1, of which waited for: 1 -> 1; matrix products, arithmetic and copies ran while one was open for 4% -> 5% of each run, Pallas kernels for 0% -> 0%
where the time goes in v13:
time: 138 us; the launch traced here: 137 us
  Pallas kernels  51.7 us (37%)
  blocking collectives  28.9 us (21%)
  local copies, waits for them, and re-layouts  21.1 us (15%)
  other arithmetic  16 us (12%)
  starting transfers between devices  6.79 us (5%)
  waiting for transfers between devices  5.27 us (4%)
  between operations  4.65 us (3%)
  matrix products  2.7 us (2%)
    all_gather x1, blocking collectives, local(): piece_rows = lax.all_gather(normed, 'head', axis=0, tiled=True)  28.9 us
    pallas_call x1, Pallas kernels, scatter_sum(): pl.pallas_call(functools.partial(scatter_sum_kernel, n=n, rows=rows), out...  18.9 us
    pallas_call x1, Pallas kernels, exchange_pack(): pl.pallas_call(functools.partial(exchange_pack_kernel, n=n), out_shape=[j...  13.8 us
    pallas_call x1, Pallas kernels, recurrence(): pl.pallas_call(functools.partial(recurrence_kernel, group=group, window=w...  9.94 us
    pallas_call x1, Pallas kernels, exchange(): pl.pallas_call(functools.partial(exchange_kernel, n=n), out_shape=jax.Sha...  9.06 us
    all_to_all x1, starting transfers between devices, local(): received = lax.all_to_all(send_buf, 'req', 0, 0, tiled=True)  6.79 us
    unnamed x76, local copies, waits for them, and re-layouts  5.65 us
    all_to_all x1, waiting for transfers between devices, local(): received = lax.all_to_all(send_buf, 'req', 0, 0, tiled=True)  5.27 us
  transfers between devices with their start and end apart: 1, of which 1 were waited for; matrix products, arithmetic and copies ran while one was open for 5% of the time, Pallas kernels for 0%

profile of v13, /device:TPU:2, one launch (start us, length us, event | category | flops | bytes accessed | tf_op | source)
XLA Modules:
  0.0 137.2 jit_solution(13722645132398792887)
XLA Ops:
  0.7 1.4 %fusion.59 = (s32[]{:T(128)}, s32[32]{0:T(128)S(1)}, s32[]{:T(128)}) fusion(s32[32]{0:T(128)} %param.38, s32[]{:T(128)S(6)} %axis_index.25, s32[32]{0:T(128)} %param.37), kind=kLoop, calls=%fused_computation.190 | loop fusion | flops 670 | bytes 396 | tf_op jit(solution)/shard_map/reduce_sum | solution.py:296
  3.4 0.9 select_reduce_fusion
  4.3 0.8 and_select_fusion.2
  5.0 0.2 convert_reduce_fusion.1
  5.2 0.6 fusion.60
  7.2 0.6 select_reduce_fusion.2.idx_ref
  7.8 0.1 select_reduce_fusion.1
  7.9 0.8 copy.115
  8.8 0.9 copy.114
  9.8 0.7 pad_maximum_fusion.2.edges_ref
  10.5 0.9 constant_dynamic-slice_fusion
  11.4 0.7 reshape.310.x_ref
  12.1 13.8 %shard_map.219 = (bf16[32,13,128]{2,1,0:T(8,128)(2,1)}, bf16[32,399,128]{2,1,0:T(8,128)(2,1)}) custom-call(s32[32]{0:T(128)} %select_reduce_fusion.2.idx_ref, bf16[32,13,128]{2,1,0:T(8,128)(2,1)} %reshape.310.x_ref, bf16[32,384,128]{2,1,0:T(8,128)(2,1)} %bitcast.32, bf16[32,15,128]{2,1,0:T(8,128)(2,1)} %pad_maximum_fusion.2.edges_ref), custom_call_target="tpu_custom_call" | custom-call | tf_op jit(solution)/shard_map/pallas_call | solution.py:256
  25.9 1.1 convolution_convert_fusion.1
  27.0 0.8 reshape.313.x_ref
  27.8 9.1 %shard_map.220 = bf16[32,13,128]{2,1,0:T(8,128)(2,1)} custom-call(bf16[32,13,128]{2,1,0:T(8,128)(2,1)} %reshape.313.x_ref), custom_call_target="tpu_custom_call" | custom-call | tf_op jit(solution)/shard_map/pallas_call | solution.py:203
  36.9 1.0 reshape.314
  38.5 0.6 fusion.20
  39.1 6.8 %all-to-all-start = ((bf16[32,399,128]{2,1,0:T(8,128)(2,1)}), bf16[32,399,128]{2,1,0:T(8,128)(2,1)}, u32[]{:S(2)}, u32[]{:S(2)}) async-start(bf16[32,399,128]{2,1,0:T(8,128)(2,1)} %fusion.20), calls=%async_computation | async-start | bytes 6553600 | tf_op jit(solution)/shard_map/all_to_all | solution.py:381
  45.9 0.1 fusion.21
  46.1 0.1 fusion.23
  46.1 28.9 %all_gather.3 = bf16[128,1536]{1,0:T(8,128)(2,1)S(1)} all-gather(bf16[16,1536]{1,0:T(8,128)(2,1)S(1)} %fusion.23), channel_id=1, replica_groups=mesh['req'=32,'head'=8] {'head'}, dimensions={0}, use_global_device_ids=true | all-gather | bytes 442368 | tf_op jit(solution)/shard_map/all_gather | solution.py:336
  75.0 0.4 convolution_convert_fusion.3
  75.4 0.1 copy.112
  75.7 2.1 %copy.166 = bf16[192,8,2,384]{3,1,2,0:T(8,128)(2,1)S(1)} copy(bf16[192,8,2,384]{3,2,1,0:T(2,128)(2,1)} %bitcast.33) | data formatting | bytes 4718592
  77.9 0.5 convolution_convert_fusion.2
  78.6 0.1 copy.111
  78.7 0.7 mul.475
  79.5 0.1 constant_dynamic-slice_fusion.1
  79.6 0.1 multiply_exponential_fusion
  79.8 0.7 pad.28.clone
  80.4 0.2 convert_reduce_fusion
  80.6 0.5 compare_select_fusion.1
  81.2 0.6 slice_reduce_fusion.13
  81.8 5.3 %all-to-all-done.refs_0_.refs_1_.refs_2_.refs_3_.refs_4_.refs_5_.refs_6_.refs_7_ = bf16[32,399,128]{2,1,0:T(8,128)(2,1)} async-done(((bf16[32,399,128]{2,1,0:T(8,128)(2,1)}), bf16[32,399,128]{2,1,0:T(8,128)(2,1)}, u32[]{:S(2)}, u32[]{:S(2)}) %all-to-all-start) | async-done | bytes 3268640 | tf_op jit(solution)/shard_map/all_to_all | solution.py:381
  87.1 0.9 slice.351
  88.0 0.6 gather_fusion
  88.8 0.2 divide_multiply_fusion.1
  89.0 0.3 fusion.61
  89.4 0.3 fusion.34
  89.7 0.4 fusion.28
  90.1 0.1 fusion.7
  90.2 0.9 slice_reduce_fusion
  91.8 2.0 %broadcast_in_dim.170 = f32[32,22,6,64]{3,2,0,1:T(8,128)} broadcast(f32[32,22,6]{2,0,1:T(8,128)S(1)} %constant_dynamic-update-slice_fusion), dimensions={0,1,2} | broadcast | bytes 1098240 | tf_op jit(solution)/shard_map/broadcast_in_dim | solution.py:435
  93.8 2.1 %reshape.316 = f32[32,22,384]{2,0,1:T(8,128)S(1)} reshape(f32[32,22,6,64]{3,2,0,1:T(8,128)} %broadcast_in_dim.170) | data formatting | bytes 2162688 | tf_op jit(solution)/shard_map/reshape | solution.py:435
  96.0 0.8 fusion.65
  96.8 0.6 copy.140
  97.4 0.6 copy.139
  98.0 0.8 maximum_maximum_fusion.refs_8_
  98.8 0.3 divide_multiply_fusion
  99.1 0.4 copy_multiply_fusion.14
  99.5 1.1 concatenate.31.refs_9_
  100.7 9.9 %shard_map.221 = (f32[32,8,384]{2,1,0:T(8,128)}, bf16[32,384,128]{2,1,0:T(8,128)(2,1)}) custom-call(s32[32]{0:T(128)} %get-tuple-element.51.rows_ref, bf16[32,399,128]{2,1,0:T(8,128)(2,1)} %all-to-all-done.refs_0_.refs_1_.refs_2_.refs_3_.refs_4_.refs_5_.refs_6_.refs_7_, ...), custom_call_target="tpu_custom_call" | custom-call | tf_op jit(solution)/shard_map/pallas_call | solution.py:113
  110.7 1.4 %fusion.51 = (f32[32,1,384]{2,1,0:T(1,128)S(1)}, f32[32,1,384]{2,1,0:T(1,128)S(1)}) fusion(f32[32,1,384]{2,1,0:T(1,128)S(1)} %get-tuple-element.89, f32[32,1,384]{2,0,1:T(8,128)S(1)} %copy-done.13, f32[32,1,384]{2,0,1:T(8,128)S(1)} %copy-done.9, f32[32,8,384]{2,1,0:T(8,128)} %get-tuple-element.10, f32[32,4,384]{2,1,0:T(4,128)S(1)} %divide_multiply_fusion, ...), kind=kLoop, calls=%fused_computation.106 | loop fusion | flops 147456 | bytes 640512 | tf_op jit(solution)/shard_map/add | solution.py:457
  112.2 1.6 %fusion.44 = (f32[32,1,384]{2,1,0:T(1,128)S(1)}, f32[32,1,384]{2,1,0:T(1,128)S(1)}) fusion(f32[32,1,384]{2,0,1:T(8,128)S(1)} %copy-done.5, f32[32,1,384]{2,1,0:T(1,128)S(1)} %get-tuple-element.87, f32[32,1,384]{2,0,1:T(8,128)S(1)} %copy-done.6, f32[32,1,384]{2,1,0:T(1,128)S(1)} %get-tuple-element.89, f32[32,1,384]{2,0,1:T(8,128)S(1)} %copy-done.7, ...), kind=kLoop, calls=%fused_computation.92 | loop fusion | flops 270336 | bytes 935424 | tf_op jit(solution)/shard_map/add | solution.py:457
  113.8 0.3 select_convert_fusion
  114.1 0.1 multiply_reduce_fusion
  114.3 0.1 reshape.321
  114.4 0.1 copy.138
  114.5 0.4 convolution_convert_fusion
  114.9 0.8 fusion.1.x_ref
  115.7 18.9 %shard_map.222 = f32[16,1664]{1,0:T(8,128)} custom-call(bf16[128,1664]{1,0:T(8,128)(2,1)} %fusion.1.x_ref), custom_call_target="tpu_custom_call" | custom-call | tf_op jit(solution)/shard_map/pallas_call | solution.py:158
  134.6 1.0 rsqrt_reduce_fusion
  135.6 1.6 %fusion.24 = bf16[16,1536]{1,0:T(8,128)(2,1)} fusion(bf16[16,1536]{1,0:T(8,128)(2,1)S(1)} %copy-done.4, f32[16,1664]{1,0:T(8,128)} %shard_map.222, f32[16]{0:T(128)S(1)} %rsqrt_reduce_fusion), kind=kLoop, calls=%fused_computation.65 | loop fusion | flops 98304 | bytes 196672 | tf_op jit(solution)/shard_map/convert_element_type | solution.py:479
  (112 shorter events, 1.8 us)
Async XLA Ops:
  0.6 113.9 %copy-start = (bf16[384,1536]{1,0:T(8,128)(2,1)S(1)}, bf16[384,1536]{1,0:T(8,128)(2,1)}, u32[]{:S(2)}) copy-start(bf16[384,1536]{1,0:T(8,128)(2,1)} %param.32) | copy-start | bytes 3538948
  39.1 6.8 %copy-start.4 = (bf16[16,1536]{1,0:T(8,128)(2,1)S(1)}, bf16[16,1536]{1,0:T(8,128)(2,1)}, u32[]{:S(2)}) copy-start(bf16[16,1536]{1,0:T(8,128)(2,1)} %param.20) | copy-start | bytes 147460
  39.1 6.9 %copy-start.21 = (f32[1536]{0:T(1024)S(1)}, f32[1536]{0:T(1024)}, u32[]{:S(2)}) copy-start(f32[1536]{0:T(1024)} %param.21) | copy-start | bytes 18436
  39.1 35.9 %copy-start.3 = (bf16[1536,304]{0,1:T(8,128)(2,1)S(1)}, bf16[1536,304]{0,1:T(8,128)(2,1)}, u32[]{:S(2)}) copy-start(bf16[1536,304]{0,1:T(8,128)(2,1)} %param.23) | copy-start | bytes 2801668
  39.1 48.0 %all-to-all-start = ((bf16[32,399,128]{2,1,0:T(8,128)(2,1)}), bf16[32,399,128]{2,1,0:T(8,128)(2,1)}, u32[]{:S(2)}, u32[]{:S(2)}) async-start(bf16[32,399,128]{2,1,0:T(8,128)(2,1)} %fusion.20), calls=%async_computation | async-start | bytes 6553600 | tf_op jit(solution)/shard_map/all_to_all | solution.py:381
  75.6 2.2 %copy-start.1 = (bf16[32,4,304]{2,1,0:T(4,128)(2,1)}, bf16[32,4,304]{2,1,0:T(4,128)(2,1)S(1)}, u32[]{:S(2)}) copy-start(bf16[32,4,304]{2,1,0:T(4,128)(2,1)S(1)} %reshape.305) | copy-start | bytes 233476
  77.8 0.7 copy-start.26
  77.8 0.8 copy-start.30
  77.8 1.7 %copy-start.31 = (f32[6]{0:T(128)S(1)}, f32[6]{0:T(128)}, u32[]{:S(2)}) copy-start(f32[6]{0:T(128)} %param.29) | copy-start | bytes 76
  77.9 1.8 %copy-start.28 = (f32[6]{0:T(128)S(1)}, f32[6]{0:T(128)}, u32[]{:S(2)}) copy-start(f32[6]{0:T(128)} %param.28) | copy-start | bytes 76
  77.9 3.3 %copy-start.22 = (f32[4,384]{1,0:T(4,128)S(1)}, f32[4,384]{1,0:T(4,128)}, u32[]{:S(2)}) copy-start(f32[4,384]{1,0:T(4,128)} %param.24) | copy-start | bytes 18436
  77.9 3.9 %copy-start.23 = (f32[4,256]{1,0:T(4,128)S(1)}, f32[4,256]{1,0:T(4,128)}, u32[]{:S(2)}) copy-start(f32[4,256]{1,0:T(4,128)} %param.26) | copy-start | bytes 12292
  77.9 1.6 %slice-start = ((bf16[32,4,304]{2,1,0:T(4,128)(2,1)}), bf16[32,4,48]{2,1,0:T(4,128)(2,1)S(1)}, s32[]{:S(2)}) async-start(bf16[32,4,304]{2,1,0:T(4,128)(2,1)} %copy-done.1), calls=%async_computation.1 | async-start | bytes 65536 | tf_op jit(solution)/shard_map/slice | solution.py:394
  77.9 10.9 %copy-start.27 = (f32[256]{0:T(256)S(1)}, f32[256]{0:T(256)}, u32[]{:S(2)}) copy-start(f32[256]{0:T(256)} %param.27) | copy-start | bytes 3076
  78.5 10.9 %copy-start.2 = (bf16[32,4,304]{2,1,0:T(4,128)(2,1)S(1)}, bf16[32,4,304]{2,1,0:T(4,128)(2,1)}, u32[]{:S(2)}) copy-start(bf16[32,4,304]{2,1,0:T(4,128)(2,1)} %copy-done.1) | copy-start | bytes 233476
  78.6 0.8 copy-start.14
  95.9 2.1 %copy-start.29 = (f32[16]{0:T(128)S(1)}, f32[16]{0:T(128)}, u32[]{:S(2)}) copy-start(f32[16]{0:T(128)} %pad.28.clone) | copy-start | bytes 196
  95.9 2.9 %copy-start.17 = (f32[384]{0:T(512)S(1)}, f32[384]{0:T(512)}, u32[]{:S(2)}) copy-start(f32[384]{0:T(512)} %get-tuple-element.38) | copy-start | bytes 4612
  96.0 2.9 %copy-start.18 = (f32[384]{0:T(512)S(1)}, f32[384]{0:T(512)}, u32[]{:S(2)}) copy-start(f32[384]{0:T(512)} %get-tuple-element.39) | copy-start | bytes 4612
  96.0 2.9 %copy-start.19 = (f32[384]{0:T(512)S(1)}, f32[384]{0:T(512)}, u32[]{:S(2)}) copy-start(f32[384]{0:T(512)} %get-tuple-element.40) | copy-start | bytes 4612
  96.0 2.8 %copy-start.20 = (f32[384]{0:T(512)S(1)}, f32[384]{0:T(512)}, u32[]{:S(2)}) copy-start(f32[384]{0:T(512)} %get-tuple-element.41) | copy-start | bytes 4612
  96.0 2.8 %copy-start.24 = (f32[384]{0:T(512)S(1)}, f32[384]{0:T(512)}, u32[]{:S(2)}) copy-start(f32[384]{0:T(512)} %param.25) | copy-start | bytes 4612
  100.6 10.0 %copy-start.9 = (f32[32,1,384]{2,0,1:T(8,128)S(1)}, f32[32,1,384]{2,0,1:T(8,128)}, u32[]{:S(2)}) copy-start(f32[32,1,384]{2,0,1:T(8,128)} %get-tuple-element.58) | copy-start | bytes 147460
  100.7 10.0 %copy-start.10 = (f32[32,1,384]{2,0,1:T(8,128)S(1)}, f32[32,1,384]{2,0,1:T(8,128)}, u32[]{:S(2)}) copy-start(f32[32,1,384]{2,0,1:T(8,128)} %get-tuple-element.67) | copy-start | bytes 147460
  100.7 10.0 %copy-start.11 = (f32[32,1,384]{2,0,1:T(8,128)S(1)}, f32[32,1,384]{2,0,1:T(8,128)}, u32[]{:S(2)}) copy-start(f32[32,1,384]{2,0,1:T(8,128)} %get-tuple-element.68) | copy-start | bytes 147460
  100.7 10.1 %copy-start.12 = (f32[32,1,384]{2,0,1:T(8,128)S(1)}, f32[32,1,384]{2,0,1:T(8,128)}, u32[]{:S(2)}) copy-start(f32[32,1,384]{2,0,1:T(8,128)} %get-tuple-element.69) | copy-start | bytes 147460
  100.7 10.1 %copy-start.13 = (f32[32,1,384]{2,0,1:T(8,128)S(1)}, f32[32,1,384]{2,0,1:T(8,128)}, u32[]{:S(2)}) copy-start(f32[32,1,384]{2,0,1:T(8,128)} %get-tuple-element.70) | copy-start | bytes 147460
  100.7 10.1 %copy-start.16 = (f32[384]{0:T(512)S(1)}, f32[384]{0:T(512)}, u32[]{:S(2)}) copy-start(f32[384]{0:T(512)} %mul.475) | copy-start | bytes 4612
  100.7 11.5 %copy-start.5 = (f32[32,1,384]{2,0,1:T(8,128)S(1)}, f32[32,1,384]{2,0,1:T(8,128)}, u32[]{:S(2)}) copy-start(f32[32,1,384]{2,0,1:T(8,128)} %get-tuple-element.63) | copy-start | bytes 147460
  100.7 11.5 %copy-start.6 = (f32[32,1,384]{2,0,1:T(8,128)S(1)}, f32[32,1,384]{2,0,1:T(8,128)}, u32[]{:S(2)}) copy-start(f32[32,1,384]{2,0,1:T(8,128)} %get-tuple-element.64) | copy-start | bytes 147460
  100.7 11.5 %copy-start.7 = (f32[32,1,384]{2,0,1:T(8,128)S(1)}, f32[32,1,384]{2,0,1:T(8,128)}, u32[]{:S(2)}) copy-start(f32[32,1,384]{2,0,1:T(8,128)} %get-tuple-element.65) | copy-start | bytes 147460
  100.7 11.5 %copy-start.8 = (f32[32,1,384]{2,0,1:T(8,128)S(1)}, f32[32,1,384]{2,0,1:T(8,128)}, u32[]{:S(2)}) copy-start(f32[32,1,384]{2,0,1:T(8,128)} %get-tuple-element.66) | copy-start | bytes 147460
  100.7 13.0 %copy-start.15 = (pred[32,4]{1,0:T(8,128)(4,1)S(1)}, pred[32,4]{1,0:T(8,128)(4,1)}, u32[]{:S(2)}) copy-start(pred[32,4]{1,0:T(8,128)(4,1)} %copy-done.14) | copy-start | bytes 388
  100.7 13.0 %copy-start.25 = (f32[384]{0:T(512)S(1)}, f32[384]{0:T(512)}, u32[]{:S(2)}) copy-start(f32[384]{0:T(512)} %param.31) | copy-start | bytes 4612

commit v14 on v12

--- a/solution.py
+++ b/solution.py
@@ -90,7 +90,7 @@
             )
 
 
-def recurrence(received, rows, mix, weight, state_rows, heads, group=8):
+def recurrence(received, rows, mix, weight, state_rows, heads, group=16):
     slot_count, _, lanes = received.shape
     window = mix.shape[1] // 4
     held_specs = [

time: 135 us -> 135 us (level)
  no operation moved by 1% of the time
where the time goes in v14:
time: 135 us; the launch traced here: 134 us
  Pallas kernels  52 us (39%)
  blocking collectives  28.9 us (21%)
  local copies, waits for them, and re-layouts  17.3 us (13%)
  other arithmetic  15.6 us (12%)
  starting transfers between devices  6.77 us (5%)
  waiting for transfers between devices  6.26 us (5%)
  between operations  4.63 us (3%)
  matrix products  2.71 us (2%)
    all_gather x1, blocking collectives, local(): piece_rows = lax.all_gather(normed, 'head', axis=0, tiled=True)  28.9 us
    pallas_call x1, Pallas kernels, scatter_sum(): pl.pallas_call(functools.partial(scatter_sum_kernel, n=n, rows=rows), out...  18.9 us
    pallas_call x1, Pallas kernels, exchange_pack(): pl.pallas_call(functools.partial(exchange_pack_kernel, n=n), out_shape=[j...  13.9 us
    pallas_call x1, Pallas kernels, recurrence(): pl.pallas_call(functools.partial(recurrence_kernel, group=group, window=w...  10.2 us
    pallas_call x1, Pallas kernels, exchange(): pl.pallas_call(functools.partial(exchange_kernel, n=n), out_shape=jax.Sha...  9.06 us
    all_to_all x1, starting transfers between devices, local(): received = lax.all_to_all(send_buf, 'req', 0, 0, tiled=True)  6.77 us
    all_to_all x1, waiting for transfers between devices, local(): received = lax.all_to_all(send_buf, 'req', 0, 0, tiled=True)  6.26 us
    unnamed x35, local copies, waits for them, and re-layouts  5.28 us
  transfers between devices with their start and end apart: 1, of which 1 were waited for; matrix products, arithmetic and copies ran while one was open for 4% of the time, Pallas kernels for 0%

profile of v14, /device:TPU:2, one launch (start us, length us, event | category | flops | bytes accessed | tf_op | source)
XLA Modules:
  0.0 134.2 jit_solution(9329247282793314506)
XLA Ops:
  0.7 1.4 %fusion.53 = (s32[]{:T(128)}, s32[32]{0:T(128)S(1)}, s32[]{:T(128)}) fusion(s32[32]{0:T(128)} %param.38, s32[]{:T(128)S(6)} %axis_index.25, s32[32]{0:T(128)} %param.37), kind=kLoop, calls=%fused_computation.153 | loop fusion | flops 670 | bytes 396 | tf_op jit(solution)/shard_map/reduce_sum | solution.py:296
  2.7 0.9 select_reduce_fusion
  3.6 0.8 and_select_fusion.1
  4.4 0.2 convert_reduce_fusion
  4.6 0.6 fusion.54
  7.2 0.6 select_reduce_fusion.2.idx_ref
  7.8 0.9 copy.105
  8.8 0.8 copy.106
  9.7 0.7 pad_maximum_fusion.2.edges_ref
  10.4 0.9 constant_dynamic-slice_fusion
  11.3 0.7 reshape.370.x_ref
  12.1 13.9 %shard_map.219 = (bf16[32,13,128]{2,1,0:T(8,128)(2,1)}, bf16[32,399,128]{2,1,0:T(8,128)(2,1)}) custom-call(s32[32]{0:T(128)} %select_reduce_fusion.2.idx_ref, bf16[32,13,128]{2,1,0:T(8,128)(2,1)} %reshape.370.x_ref, bf16[32,384,128]{2,1,0:T(8,128)(2,1)} %bitcast.68, bf16[32,15,128]{2,1,0:T(8,128)(2,1)} %pad_maximum_fusion.2.edges_ref), custom_call_target="tpu_custom_call" | custom-call | tf_op jit(solution)/shard_map/pallas_call | solution.py:256
  26.0 1.1 convolution_convert_fusion.1
  27.1 0.8 reshape.373.x_ref
  27.9 9.1 %shard_map.220 = bf16[32,13,128]{2,1,0:T(8,128)(2,1)} custom-call(bf16[32,13,128]{2,1,0:T(8,128)(2,1)} %reshape.373.x_ref), custom_call_target="tpu_custom_call" | custom-call | tf_op jit(solution)/shard_map/pallas_call | solution.py:203
  37.0 1.0 reshape.374
  38.6 0.7 fusion.20
  39.2 6.8 %all-to-all-start = ((bf16[32,399,128]{2,1,0:T(8,128)(2,1)}), bf16[32,399,128]{2,1,0:T(8,128)(2,1)}, u32[]{:S(2)}, u32[]{:S(2)}) async-start(bf16[32,399,128]{2,1,0:T(8,128)(2,1)} %fusion.20), calls=%async_computation | async-start | bytes 6553600 | tf_op jit(solution)/shard_map/all_to_all | solution.py:381
  46.0 0.1 fusion.21
  46.3 28.9 %all_gather.3 = bf16[128,1536]{1,0:T(8,128)(2,1)S(1)} all-gather(bf16[16,1536]{1,0:T(8,128)(2,1)S(1)} %fusion.23), channel_id=1, replica_groups=mesh['req'=32,'head'=8] {'head'}, dimensions={0}, use_global_device_ids=true | all-gather | bytes 442368 | tf_op jit(solution)/shard_map/all_gather | solution.py:336
  75.2 0.4 convolution_convert_fusion.3
  75.6 0.1 copy.103
  76.0 2.1 %copy.127 = bf16[192,8,2,384]{3,1,2,0:T(8,128)(2,1)S(1)} copy(bf16[192,8,2,384]{3,2,1,0:T(2,128)(2,1)} %bitcast.69) | data formatting | bytes 4718592
  78.2 0.5 convolution_convert_fusion.2
  78.8 0.1 slice-done
  79.1 0.2 broadcast_in_dim.201
  79.3 0.1 reshape.377
  79.6 0.1 reshape.415
  79.8 0.1 reshape.412
  80.2 0.2 convert_reduce_fusion.1
  80.3 0.5 compare_select_fusion.1
  80.9 6.3 %all-to-all-done.refs_0_.refs_1_.refs_2_.refs_3_.refs_4_.refs_5_.refs_6_.refs_7_.refs_8_.refs_9_.refs_10_.refs_11_.refs_12_.refs_13_.refs_14_.refs_15_ = bf16[32,399,128]{2,1,0:T(8,128)(2,1)} async-done(((bf16[32,399,128]{2,1,0:T(8,128)(2,1)}), bf16[32,399,128]{2,1,0:T(8,128)(2,1)}, u32[]{:S(2)}, u32[]{:S(2)}) %all-to-all-start) | async-done | bytes 3268640 | tf_op jit(solution)/shard_map/all_to_all | solution.py:381
  87.2 0.9 slice.277
  88.1 0.6 gather_fusion
  88.9 0.2 divide_multiply_fusion.1
  89.1 0.3 fusion.56
  89.6 0.4 fusion.28
  90.0 0.3 fusion.34
  90.3 1.0 slice_reduce_fusion.9
  91.5 0.1 reshape.413
  91.7 0.1 reshape.414
  91.9 0.1 reshape.418
  92.1 0.1 reshape.419
  92.4 0.1 reshape.420
  92.7 0.1 reshape.423
  92.9 0.1 reshape.416
  93.1 0.1 reshape.417
  93.8 0.1 reshape.424
  93.9 0.3 copy_multiply_fusion
  94.2 0.2 fusion.64
  94.4 0.8 maximum_maximum_fusion.refs_16_
  95.2 1.1 concatenate.31.refs_17_
  96.4 10.2 %shard_map.221 = (f32[32,8,384]{2,1,0:T(8,128)}, bf16[32,384,128]{2,1,0:T(8,128)(2,1)}) custom-call(s32[32]{0:T(128)} %get-tuple-element.57.rows_ref, bf16[32,399,128]{2,1,0:T(8,128)(2,1)} %all-to-all-done.refs_0_.refs_1_.refs_2_.refs_3_.refs_4_.refs_5_.refs_6_.refs_7_.refs_8_.refs_9_.refs_10_.refs_11_.refs_12_.refs_13_.refs_14_.refs_15_, ...), custom_call_target="tpu_custom_call" | custom-call | tf_op jit(solution)/shard_map/pallas_call | solution.py:113
  106.5 1.4 %fusion.41 = (f32[32,1,384]{2,1,0:T(1,128)S(1)}, f32[32,1,384]{2,1,0:T(1,128)S(1)}) fusion(f32[32,4,384]{2,1,0:T(4,128)S(1)} %get-tuple-element.49, f32[32,1,384]{2,1,0:T(1,128)S(1)} %reshape.412, f32[32,8,384]{2,1,0:T(8,128)} %get-tuple-element.10, f32[32]{0:T(128)S(1)} %get-tuple-element.32, f32[384]{0:T(512)S(1)} %mul.376, ...), kind=kLoop, calls=%fused_computation.88 | loop fusion | flops 172032 | bytes 640768 | tf_op jit(solution)/shard_map/add | solution.py:439
  107.9 1.5 %fusion.40 = (f32[32,1,384]{2,1,0:T(1,128)S(1)}, f32[32,1,384]{2,1,0:T(1,128)S(1)}) fusion(f32[32,4,384]{2,1,0:T(4,128)S(1)} %get-tuple-element.49, f32[32,1,384]{2,1,0:T(1,128)S(1)} %reshape.417, f32[32,1,384]{2,1,0:T(1,128)S(1)} %reshape.416, f32[32,8,384]{2,1,0:T(8,128)} %get-tuple-element.10, f32[32]{0:T(128)S(1)} %get-tuple-element.40, ...), kind=kLoop, calls=%fused_computation.86 | loop fusion | flops 221184 | bytes 788224 | tf_op jit(solution)/shard_map/add | solution.py:439
  109.5 0.3 select_convert_fusion
  110.1 0.1 copy.121
  110.2 0.4 convolution_convert_fusion
  110.6 0.8 fusion.1.x_ref
  111.4 18.9 %shard_map.222 = f32[16,1664]{1,0:T(8,128)} custom-call(bf16[128,1664]{1,0:T(8,128)(2,1)} %fusion.1.x_ref), custom_call_target="tpu_custom_call" | custom-call | tf_op jit(solution)/shard_map/pallas_call | solution.py:158
  130.3 1.0 rsqrt_reduce_fusion
  131.3 1.6 %fusion.24 = bf16[16,1536]{1,0:T(8,128)(2,1)} fusion(bf16[16,1536]{1,0:T(8,128)(2,1)S(1)} %copy-done.4, f32[16,1664]{1,0:T(8,128)} %shard_map.222, f32[16]{0:T(128)S(1)} %rsqrt_reduce_fusion), kind=kLoop, calls=%fused_computation.66 | loop fusion | flops 98304 | bytes 196672 | tf_op jit(solution)/shard_map/convert_element_type | solution.py:461
  132.9 0.6 copy.122
  133.5 0.6 copy.123
  (87 shorter events, 3.4 us)
Async XLA Ops:
  0.6 109.6 %copy-start = (bf16[384,1536]{1,0:T(8,128)(2,1)S(1)}, bf16[384,1536]{1,0:T(8,128)(2,1)}, u32[]{:S(2)}) copy-start(bf16[384,1536]{1,0:T(8,128)(2,1)} %param.32) | copy-start | bytes 3538948
  39.2 6.8 %copy-start.4 = (bf16[16,1536]{1,0:T(8,128)(2,1)S(1)}, bf16[16,1536]{1,0:T(8,128)(2,1)}, u32[]{:S(2)}) copy-start(bf16[16,1536]{1,0:T(8,128)(2,1)} %param.20) | copy-start | bytes 147460
  39.2 6.9 %copy-start.5 = (f32[1536]{0:T(1024)S(1)}, f32[1536]{0:T(1024)}, u32[]{:S(2)}) copy-start(f32[1536]{0:T(1024)} %param.21) | copy-start | bytes 18436
  39.2 35.9 %copy-start.3 = (bf16[1536,304]{0,1:T(8,128)(2,1)S(1)}, bf16[1536,304]{0,1:T(8,128)(2,1)}, u32[]{:S(2)}) copy-start(bf16[1536,304]{0,1:T(8,128)(2,1)} %param.23) | copy-start | bytes 2801668
  39.2 48.0 %all-to-all-start = ((bf16[32,399,128]{2,1,0:T(8,128)(2,1)}), bf16[32,399,128]{2,1,0:T(8,128)(2,1)}, u32[]{:S(2)}, u32[]{:S(2)}) async-start(bf16[32,399,128]{2,1,0:T(8,128)(2,1)} %fusion.20), calls=%async_computation | async-start | bytes 6553600 | tf_op jit(solution)/shard_map/all_to_all | solution.py:381
  46.0 29.8 %copy-start.10 = (s32[32]{0:T(128)S(1)}, s32[32]{0:T(128)}, u32[]{:S(2)}) copy-start(s32[32]{0:T(128)} %param.36) | copy-start | bytes 388
  75.7 2.4 %copy-start.1 = (bf16[32,4,304]{2,1,0:T(4,128)(2,1)}, bf16[32,4,304]{2,1,0:T(4,128)(2,1)S(1)}, u32[]{:S(2)}) copy-start(bf16[32,4,304]{2,1,0:T(4,128)(2,1)S(1)} %reshape.364) | copy-start | bytes 233476
  78.1 0.9 copy-start.14
  78.1 0.9 copy-start.12
  78.1 0.8 slice-start
  78.1 1.8 %copy-start.13 = (f32[6]{0:T(128)S(1)}, f32[6]{0:T(128)}, u32[]{:S(2)}) copy-start(f32[6]{0:T(128)} %param.30) | copy-start | bytes 76
  78.2 2.7 %copy-start.6 = (f32[4,384]{1,0:T(4,128)S(1)}, f32[4,384]{1,0:T(4,128)}, u32[]{:S(2)}) copy-start(f32[4,384]{1,0:T(4,128)} %param.24) | copy-start | bytes 18436
  78.2 2.7 %copy-start.7 = (f32[4,256]{1,0:T(4,128)S(1)}, f32[4,256]{1,0:T(4,128)}, u32[]{:S(2)}) copy-start(f32[4,256]{1,0:T(4,128)} %param.26) | copy-start | bytes 12292
  78.7 10.2 %copy-start.11 = (f32[256]{0:T(256)S(1)}, f32[256]{0:T(256)}, u32[]{:S(2)}) copy-start(f32[256]{0:T(256)} %param.27) | copy-start | bytes 3076
  79.4 10.5 %copy-start.2 = (bf16[32,4,304]{2,1,0:T(4,128)(2,1)S(1)}, bf16[32,4,304]{2,1,0:T(4,128)(2,1)}, u32[]{:S(2)}) copy-start(bf16[32,4,304]{2,1,0:T(4,128)(2,1)} %copy-done.1) | copy-start | bytes 233476
  89.6 4.3 %copy-start.8 = (f32[384]{0:T(512)S(1)}, f32[384]{0:T(512)}, u32[]{:S(2)}) copy-start(f32[384]{0:T(512)} %param.25) | copy-start | bytes 4612
  96.3 13.1 %copy-start.9 = (f32[384]{0:T(512)S(1)}, f32[384]{0:T(512)}, u32[]{:S(2)}) copy-start(f32[384]{0:T(512)} %param.31) | copy-start | bytes 4612

commit v15 on v12

--- a/solution.py
+++ b/solution.py
@@ -122,7 +122,11 @@
 MESH = pl.DeviceIdType.MESH
 
 
-def scatter_sum_kernel(x_ref, out_ref, slots, send_sem, recv_sem, *, n, rows):
+def scatter_sum_kernel(*refs, n, rows, parts):
+    x_refs = refs[:parts]
+    out_refs = refs[parts : 2 * parts]
+    slots = refs[2 * parts : 3 * parts]
+    send_sem, recv_sem = refs[3 * parts :]
     me = lax.axis_index("head")
     group = lax.axis_index("req")
     barrier = pltpu.get_barrier_semaphore()
@@ -135,38 +139,41 @@
     for k in range(1, n):
         peer = lax.rem(me + k, n)
         start = pl.multiple_of(peer * rows, rows)
-        copy = pltpu.make_async_remote_copy(
-            src_ref=x_ref.at[pl.ds(start, rows)],
-            dst_ref=slots.at[k - 1],
-            send_sem=send_sem.at[k - 1],
-            recv_sem=recv_sem.at[k - 1],
-            device_id=(group, peer),
-            device_id_type=MESH,
-        )
-        copy.start()
-        copies.append(copy)
+        for p in range(parts):
+            copy = pltpu.make_async_remote_copy(
+                src_ref=x_refs[p].at[pl.ds(start, rows)],
+                dst_ref=slots[p].at[k - 1],
+                send_sem=send_sem.at[p, k - 1],
+                recv_sem=recv_sem.at[p, k - 1],
+                device_id=(group, peer),
+                device_id_type=MESH,
+            )
+            copy.start()
+            copies.append((p, k, copy))
     own = pl.multiple_of(me * rows, rows)
-    total = x_ref[pl.ds(own, rows)].astype(jnp.float32)
-    for k, copy in enumerate(copies):
+    totals = [x_refs[p][pl.ds(own, rows)].astype(jnp.float32) for p in range(parts)]
+    for p, k, copy in copies:
         copy.wait()
-        total = total + slots[k].astype(jnp.float32)
-    out_ref[...] = total
-
-
-def scatter_sum(x, n):
-    rows = x.shape[0] // n
+        totals[p] = totals[p] + slots[p][k - 1].astype(jnp.float32)
+    for p in range(parts):
+        out_refs[p][...] = totals[p]
+
+
+def scatter_sum(xs, n):
+    rows = xs[0].shape[0] // n
+    parts = len(xs)
     return pl.pallas_call(
-        functools.partial(scatter_sum_kernel, n=n, rows=rows),
-        out_shape=jax.ShapeDtypeStruct((rows, x.shape[1]), jnp.float32),
-        in_specs=[pl.BlockSpec(memory_space=pltpu.VMEM)],
-        out_specs=pl.BlockSpec(memory_space=pltpu.VMEM),
-        scratch_shapes=[
-            pltpu.VMEM((n - 1, rows, x.shape[1]), x.dtype),
-            pltpu.SemaphoreType.DMA((n - 1,)),
-            pltpu.SemaphoreType.DMA((n - 1,)),
+        functools.partial(scatter_sum_kernel, n=n, rows=rows, parts=parts),
+        out_shape=[jax.ShapeDtypeStruct((rows, x.shape[1]), jnp.float32) for x in xs],
+        in_specs=[pl.BlockSpec(memory_space=pltpu.VMEM)] * parts,
+        out_specs=[pl.BlockSpec(memory_space=pltpu.VMEM)] * parts,
+        scratch_shapes=[pltpu.VMEM((n - 1, rows, x.shape[1]), x.dtype) for x in xs]
+        + [
+            pltpu.SemaphoreType.DMA((parts, n - 1)),
+            pltpu.SemaphoreType.DMA((parts, n - 1)),
         ],
         compiler_params=pltpu.CompilerParams(collective_id=0, has_side_effects=True),
-    )(x)
+    )(*xs)
 
 
 def exchange_kernel(x_ref, out_ref, send_sem, recv_sem, local_sem, *, n):
@@ -452,13 +459,13 @@
     extra = jnp.pad(
         jnp.concatenate([square_hi, square_lo], axis=1), ((0, 0), (0, 126))
     )
-    combined = jnp.concatenate([partial.astype(jnp.bfloat16), extra], axis=1)
-    reduced = scatter_sum(combined, lax.axis_size("head"))
+    reduced, squares = scatter_sum(
+        [partial.astype(jnp.bfloat16), extra.astype(jnp.bfloat16)], lax.axis_size("head")
+    )
     full_inner = inner_here * lax.axis_size("head")
-    width = partial.shape[1]
-    square_sum = reduced[:, width : width + 1] + reduced[:, width + 1 : width + 2]
+    square_sum = squares[:, 0:1] + squares[:, 1:2]
     scale = lax.rsqrt(square_sum / full_inner + EPS)
-    hidden_out = (rows_in + reduced[:, :width] * scale).astype(jnp.bfloat16)
+    hidden_out = (rows_in + reduced * scale).astype(jnp.bfloat16)
     return (hidden_out, states_out, edge_inner_out, edge_shared_out)
 
 

time: 135 us -> 136 us (level)
  no operation moved by 1% of the time
where the time goes in v15:
time: 136 us; the launch traced here: 135 us
  Pallas kernels  51.9 us (38%)
  blocking collectives  28.9 us (21%)
  local copies, waits for them, and re-layouts  17.9 us (13%)
  other arithmetic  14.9 us (11%)
  starting transfers between devices  6.79 us (5%)
  waiting for transfers between devices  6.27 us (5%)
  between operations  4.61 us (3%)
  matrix products  3.45 us (3%)
    all_gather x1, blocking collectives, local(): piece_rows = lax.all_gather(normed, 'head', axis=0, tiled=True)  28.9 us
    pallas_call x1, Pallas kernels, scatter_sum(): pl.pallas_call(functools.partial(scatter_sum_kernel, n=n, rows=rows, part...  19 us
    pallas_call x1, Pallas kernels, exchange_pack(): pl.pallas_call(functools.partial(exchange_pack_kernel, n=n), out_shape=[j...  13.9 us
    pallas_call x1, Pallas kernels, recurrence(): pl.pallas_call(functools.partial(recurrence_kernel, group=group, window=w...  9.93 us
    pallas_call x1, Pallas kernels, exchange(): pl.pallas_call(functools.partial(exchange_kernel, n=n), out_shape=jax.Sha...  9.06 us
    all_to_all x1, starting transfers between devices, local(): received = lax.all_to_all(send_buf, 'req', 0, 0, tiled=True)  6.79 us
    all_to_all x1, waiting for transfers between devices, local(): received = lax.all_to_all(send_buf, 'req', 0, 0, tiled=True)  6.27 us
    unnamed x35, local copies, waits for them, and re-layouts  5.29 us
  transfers between devices with their start and end apart: 1, of which 1 were waited for; matrix products, arithmetic and copies ran while one was open for 4% of the time, Pallas kernels for 0%

profile of v15, /device:TPU:2, one launch (start us, length us, event | category | flops | bytes accessed | tf_op | source)
XLA Modules:
  0.0 134.7 jit_solution(2350199635795984553)
XLA Ops:
  0.7 1.4 %fusion.51 = (s32[]{:T(128)}, s32[32]{0:T(128)S(1)}, s32[]{:T(128)}) fusion(s32[32]{0:T(128)} %param.38, s32[]{:T(128)S(6)} %axis_index.25, s32[32]{0:T(128)} %param.37), kind=kLoop, calls=%fused_computation.150 | loop fusion | flops 670 | bytes 396 | tf_op jit(solution)/shard_map/reduce_sum | solution.py:303
  2.7 0.9 select_reduce_fusion
  3.6 0.8 and_select_fusion.1
  4.4 0.2 convert_reduce_fusion
  4.6 0.6 fusion.52
  7.2 0.6 select_reduce_fusion.2.idx_ref
  7.8 0.9 copy.105
  8.8 0.8 copy.106
  9.7 0.7 pad_maximum_fusion.2.edges_ref
  10.4 0.9 constant_dynamic-slice_fusion
  11.3 0.7 reshape.370.x_ref
  12.1 13.9 %shard_map.219 = (bf16[32,13,128]{2,1,0:T(8,128)(2,1)}, bf16[32,399,128]{2,1,0:T(8,128)(2,1)}) custom-call(s32[32]{0:T(128)} %select_reduce_fusion.2.idx_ref, bf16[32,13,128]{2,1,0:T(8,128)(2,1)} %reshape.370.x_ref, bf16[32,384,128]{2,1,0:T(8,128)(2,1)} %bitcast.68, bf16[32,15,128]{2,1,0:T(8,128)(2,1)} %pad_maximum_fusion.2.edges_ref), custom_call_target="tpu_custom_call" | custom-call | tf_op jit(solution)/shard_map/pallas_call | solution.py:263
  26.0 1.1 convolution_convert_fusion.1
  27.1 0.8 reshape.373.x_ref
  27.9 9.1 %shard_map.220 = bf16[32,13,128]{2,1,0:T(8,128)(2,1)} custom-call(bf16[32,13,128]{2,1,0:T(8,128)(2,1)} %reshape.373.x_ref), custom_call_target="tpu_custom_call" | custom-call | tf_op jit(solution)/shard_map/pallas_call | solution.py:210
  37.0 1.0 reshape.374
  38.6 0.6 fusion.18
  39.2 6.8 %all-to-all-start = ((bf16[32,399,128]{2,1,0:T(8,128)(2,1)}), bf16[32,399,128]{2,1,0:T(8,128)(2,1)}, u32[]{:S(2)}, u32[]{:S(2)}) async-start(bf16[32,399,128]{2,1,0:T(8,128)(2,1)} %fusion.18), calls=%async_computation | async-start | bytes 6553600 | tf_op jit(solution)/shard_map/all_to_all | solution.py:388
  46.0 0.1 fusion.19
  46.3 28.9 %all_gather.3 = bf16[128,1536]{1,0:T(8,128)(2,1)S(1)} all-gather(bf16[16,1536]{1,0:T(8,128)(2,1)S(1)} %fusion.21), channel_id=1, replica_groups=mesh['req'=32,'head'=8] {'head'}, dimensions={0}, use_global_device_ids=true | all-gather | bytes 442368 | tf_op jit(solution)/shard_map/all_gather | solution.py:343
  75.2 0.4 convolution_convert_fusion.3
  75.6 0.1 copy.103
  76.0 2.1 %copy.127 = bf16[192,8,2,384]{3,1,2,0:T(8,128)(2,1)S(1)} copy(bf16[192,8,2,384]{3,2,1,0:T(2,128)(2,1)} %bitcast.69) | data formatting | bytes 4718592
  78.2 0.5 convolution_convert_fusion.2
  78.8 0.1 slice-done
  79.1 0.2 broadcast_in_dim.201
  79.3 0.1 reshape.377
  79.6 0.1 reshape.415
  79.8 0.1 reshape.412
  80.2 0.2 convert_reduce_fusion.1
  80.3 0.5 compare_select_fusion.1
  80.9 6.3 %all-to-all-done.refs_0_.refs_1_.refs_2_.refs_3_.refs_4_.refs_5_.refs_6_.refs_7_ = bf16[32,399,128]{2,1,0:T(8,128)(2,1)} async-done(((bf16[32,399,128]{2,1,0:T(8,128)(2,1)}), bf16[32,399,128]{2,1,0:T(8,128)(2,1)}, u32[]{:S(2)}, u32[]{:S(2)}) %all-to-all-start) | async-done | bytes 3268640 | tf_op jit(solution)/shard_map/all_to_all | solution.py:388
  87.2 0.9 slice.273
  88.1 0.6 gather_fusion
  88.9 0.2 divide_multiply_fusion.1
  89.1 0.3 fusion.54
  89.6 0.4 fusion.26
  90.0 0.3 fusion.32
  90.3 1.0 slice_reduce_fusion.9
  91.5 0.1 reshape.413
  91.7 0.1 reshape.414
  91.9 0.1 reshape.418
  92.2 0.1 reshape.419
  92.4 0.1 reshape.420
  92.7 0.1 reshape.423
  92.9 0.1 reshape.416
  93.1 0.1 reshape.417
  93.3 0.1 reshape.421
  93.9 0.3 copy_multiply_fusion
  94.2 0.2 fusion.62
  94.4 0.8 maximum_maximum_fusion.refs_8_
  95.2 1.1 concatenate.28.refs_9_
  96.4 9.9 %shard_map.221 = (f32[32,8,384]{2,1,0:T(8,128)}, bf16[32,384,128]{2,1,0:T(8,128)(2,1)}) custom-call(s32[32]{0:T(128)} %get-tuple-element.61.rows_ref, bf16[32,399,128]{2,1,0:T(8,128)(2,1)} %all-to-all-done.refs_0_.refs_1_.refs_2_.refs_3_.refs_4_.refs_5_.refs_6_.refs_7_, ...), custom_call_target="tpu_custom_call" | custom-call | tf_op jit(solution)/shard_map/pallas_call | solution.py:113
  106.3 1.4 %fusion.39 = (f32[32,1,384]{2,1,0:T(1,128)S(1)}, f32[32,1,384]{2,1,0:T(1,128)S(1)}) fusion(f32[32,4,384]{2,1,0:T(4,128)S(1)} %get-tuple-element.53, f32[32,1,384]{2,1,0:T(1,128)S(1)} %reshape.412, f32[32,8,384]{2,1,0:T(8,128)} %get-tuple-element.12, f32[32]{0:T(128)S(1)} %get-tuple-element.36, f32[384]{0:T(512)S(1)} %mul.376, ...), kind=kLoop, calls=%fused_computation.85 | loop fusion | flops 172032 | bytes 640768 | tf_op jit(solution)/shard_map/add | solution.py:446
  107.7 1.5 %fusion.38 = (f32[32,1,384]{2,1,0:T(1,128)S(1)}, f32[32,1,384]{2,1,0:T(1,128)S(1)}) fusion(f32[32,4,384]{2,1,0:T(4,128)S(1)} %get-tuple-element.53, f32[32,1,384]{2,1,0:T(1,128)S(1)} %reshape.417, f32[32,1,384]{2,1,0:T(1,128)S(1)} %reshape.416, f32[32,8,384]{2,1,0:T(8,128)} %get-tuple-element.12, f32[32]{0:T(128)S(1)} %get-tuple-element.44, ...), kind=kLoop, calls=%fused_computation.83 | loop fusion | flops 221184 | bytes 788224 | tf_op jit(solution)/shard_map/add | solution.py:446
  109.2 0.4 multiply_reduce_fusion
  109.8 0.1 copy.121
  110.0 0.6 pad.14.refs_1_
  110.7 1.1 convolution_convert_fusion.refs_0_
  111.8 19.0 %shard_map.222 = (f32[16,1536]{1,0:T(8,128)}, f32[16,128]{1,0:T(8,128)}) custom-call(bf16[128,1536]{1,0:T(8,128)(2,1)} %convolution_convert_fusion.refs_0_, bf16[128,128]{1,0:T(8,128)(2,1)} %pad.14.refs_1_), custom_call_target="tpu_custom_call" | custom-call | tf_op jit(solution)/shard_map/pallas_call | solution.py:165
  130.8 1.0 rsqrt_reduce_fusion
  131.8 0.7 copy.122
  132.4 0.6 copy.123
  133.1 1.6 %fusion.22 = bf16[16,1536]{1,0:T(8,128)(2,1)} fusion(bf16[16,1536]{1,0:T(8,128)(2,1)S(1)} %copy-done.4, f32[16,1536]{1,0:T(8,128)} %get-tuple-element.13, f32[16]{0:T(128)S(1)} %rsqrt_reduce_fusion), kind=kLoop, calls=%fused_computation.63 | loop fusion | flops 98304 | bytes 196672 | tf_op jit(solution)/shard_map/convert_element_type | solution.py:468
  (87 shorter events, 3.4 us)
Async XLA Ops:
  0.6 110.0 %copy-start = (bf16[384,1536]{1,0:T(8,128)(2,1)S(1)}, bf16[384,1536]{1,0:T(8,128)(2,1)}, u32[]{:S(2)}) copy-start(bf16[384,1536]{1,0:T(8,128)(2,1)} %param.32) | copy-start | bytes 3538948
  39.2 6.8 %copy-start.4 = (bf16[16,1536]{1,0:T(8,128)(2,1)S(1)}, bf16[16,1536]{1,0:T(8,128)(2,1)}, u32[]{:S(2)}) copy-start(bf16[16,1536]{1,0:T(8,128)(2,1)} %param.20) | copy-start | bytes 147460
  39.2 7.0 %copy-start.5 = (f32[1536]{0:T(1024)S(1)}, f32[1536]{0:T(1024)}, u32[]{:S(2)}) copy-start(f32[1536]{0:T(1024)} %param.21) | copy-start | bytes 18436
  39.2 35.9 %copy-start.3 = (bf16[1536,304]{0,1:T(8,128)(2,1)S(1)}, bf16[1536,304]{0,1:T(8,128)(2,1)}, u32[]{:S(2)}) copy-start(bf16[1536,304]{0,1:T(8,128)(2,1)} %param.23) | copy-start | bytes 2801668
  39.2 48.0 %all-to-all-start = ((bf16[32,399,128]{2,1,0:T(8,128)(2,1)}), bf16[32,399,128]{2,1,0:T(8,128)(2,1)}, u32[]{:S(2)}, u32[]{:S(2)}) async-start(bf16[32,399,128]{2,1,0:T(8,128)(2,1)} %fusion.18), calls=%async_computation | async-start | bytes 6553600 | tf_op jit(solution)/shard_map/all_to_all | solution.py:388
  46.0 29.8 %copy-start.10 = (s32[32]{0:T(128)S(1)}, s32[32]{0:T(128)}, u32[]{:S(2)}) copy-start(s32[32]{0:T(128)} %param.36) | copy-start | bytes 388
  75.7 2.4 %copy-start.1 = (bf16[32,4,304]{2,1,0:T(4,128)(2,1)}, bf16[32,4,304]{2,1,0:T(4,128)(2,1)S(1)}, u32[]{:S(2)}) copy-start(bf16[32,4,304]{2,1,0:T(4,128)(2,1)S(1)} %reshape.364) | copy-start | bytes 233476
  78.1 0.9 copy-start.14
  78.1 0.9 copy-start.12
  78.1 0.8 slice-start
  78.2 1.8 %copy-start.13 = (f32[6]{0:T(128)S(1)}, f32[6]{0:T(128)}, u32[]{:S(2)}) copy-start(f32[6]{0:T(128)} %param.30) | copy-start | bytes 76
  78.2 2.7 %copy-start.6 = (f32[4,384]{1,0:T(4,128)S(1)}, f32[4,384]{1,0:T(4,128)}, u32[]{:S(2)}) copy-start(f32[4,384]{1,0:T(4,128)} %param.24) | copy-start | bytes 18436
  78.2 2.7 %copy-start.7 = (f32[4,256]{1,0:T(4,128)S(1)}, f32[4,256]{1,0:T(4,128)}, u32[]{:S(2)}) copy-start(f32[4,256]{1,0:T(4,128)} %param.26) | copy-start | bytes 12292
  78.7 10.2 %copy-start.11 = (f32[256]{0:T(256)S(1)}, f32[256]{0:T(256)}, u32[]{:S(2)}) copy-start(f32[256]{0:T(256)} %param.27) | copy-start | bytes 3076
  79.5 10.5 %copy-start.2 = (bf16[32,4,304]{2,1,0:T(4,128)(2,1)S(1)}, bf16[32,4,304]{2,1,0:T(4,128)(2,1)}, u32[]{:S(2)}) copy-start(bf16[32,4,304]{2,1,0:T(4,128)(2,1)} %copy-done.1) | copy-start | bytes 233476
  89.6 4.3 %copy-start.8 = (f32[384]{0:T(512)S(1)}, f32[384]{0:T(512)}, u32[]{:S(2)}) copy-start(f32[384]{0:T(512)} %param.25) | copy-start | bytes 4612
  96.4 13.5 %copy-start.9 = (f32[384]{0:T(512)S(1)}, f32[384]{0:T(512)}, u32[]{:S(2)}) copy-start(f32[384]{0:T(512)} %param.31) | copy-start | bytes 4612
